TPU v7x, 128 devices: a whole 4x4x4 slice. The times are simulated.
128 devices in a mesh: seq: 32 (over z, y, core), slide: 4 (over x).
Axes of the slice: x: 4, y: 4, z: 4, core: 2. Of those that a mesh axis runs over, the one named last changes fastest.
Arguments:
- tile_embed: bfloat16 [16384, 1536], P(('seq', 'slide')), may hold values from -6 to 6
- destination: int32 [16384], P(('seq', 'slide')), may hold values from 0 to 16383, as said below
- slide_lengths: int32 [4], replicated, may hold values from 128 to 8192, as said below
- w_inner: bfloat16 [1536, 3072], replicated, may hold values from -0.15625 to 0.15625
- w_gate: bfloat16 [1536, 3072], replicated, may hold values from -0.15625 to 0.15625
- conv_weight: float32 [2, 4, 3072], replicated, may hold values from -2 to 2
- conv_bias: float32 [2, 3072], replicated, may hold values from -2 to 2
- x_project: bfloat16 [2, 3072, 128], replicated, may hold values from -0.109375 to 0.109375
- dt_project: bfloat16 [2, 96, 3072], replicated, may hold values from -0.625 to 0.625
- dt_bias: float32 [2, 3072], replicated, may hold values from -6 to -3.5
- decay: float32 [2, 16, 3072], replicated, may hold values from 0.0024414062 to 32
- skip_gain: float32 [2, 3072], replicated, may hold values from 0.5 to 1.5
Outputs:
- mixed: bfloat16 [16384, 3072], P(('seq', 'slide'))
Inputs may be any that keep to these rules, and one draw needn't show every extreme that they name: `destination`: a permutation; the tile in row b of the 128 rows of each encoder device has a packed position from b * 128 to (b + 1) * 128 - 1. `slide_lengths`: each a multiple of 128; they sum to 16384; the longest is exactly 8192.
All inputs are finite; a program needn't handle non-finite values.
Results may differ from a plain program's by a relative error of at most 0.0067.
Values may be sent and summed in bfloat16 or wider, within the bound.
No kernel may reach another device: no remote copies, remote signals or barrier semaphores. Data moves between devices by JAX's collectives and lax.ppermute only.
A program may use at most 320 MiB of HBM per device.

v0:
```python
import jax
import jax.numpy as jnp
from jax import lax
from jax.sharding import PartitionSpec as P


def with_halo(array, sides, width):
    for axis, dim in sides:
        size, length = (lax.axis_size(axis), array.shape[dim])
        up = [(i, (i + 1) % size) for i in range(size - 1)]
        down = [(j, i) for i, j in up]
        last = lax.slice_in_dim(array, length - width, length, axis=dim)
        first = lax.slice_in_dim(array, 0, width, axis=dim)
        before = lax.ppermute(last, axis, up)
        after = lax.ppermute(first, axis, down)
        array = jnp.concatenate([before, array, after], axis=dim)
    return array


def shifted(block, axis, distance):
    devices = range(lax.axis_size(axis))
    route = [(i - distance, i) for i in devices if i - distance in devices]
    return lax.ppermute(block, axis, route)


def state_sweep(start, step_size, mixed_in, b_rows, c_rows, keep, rates, reverse):
    row_count = step_size.shape[0]
    turns = 16
    per_turn = row_count // turns

    def blocked(array):
        return array.reshape((turns, per_turn) + array.shape[1:])

    def row_step(hidden, row_data):
        dt_row, u_row, b_row, c_row, keep_row = row_data
        hidden = (
            keep_row * jnp.exp(dt_row[None, :] * rates) * hidden
            + (dt_row * u_row)[None, :] * b_row[:, None]
        )
        return (hidden, jnp.sum(c_row[:, None] * hidden, axis=0))

    def block_step(hidden, block_data):
        return lax.scan(row_step, hidden, block_data, reverse=reverse, unroll=True)

    block_data = (
        blocked(step_size),
        blocked(mixed_in),
        blocked(b_rows),
        blocked(c_rows),
        blocked(keep),
    )
    last_state, outputs = lax.scan(block_step, start, block_data, reverse=reverse)
    return (last_state, outputs.reshape(row_count, -1))


def entering_rows(enter, step_size, c_rows, alive, rates, reverse):
    summed_dt = lax.cumsum(step_size, axis=0, reverse=reverse)
    added = jnp.zeros_like(step_size)
    for state in range(rates.shape[0]):
        added = (
            added
            + c_rows[:, state : state + 1]
            * jnp.exp(summed_dt * rates[state][None, :])
            * enter[state][None, :]
        )
    return added * alive[:, None]


def direction_terms(mixed_in, x_proj, dt_proj, bias, states):
    rank = dt_proj.shape[0]
    project = jnp.dot(mixed_in, x_proj, preferred_element_type=jnp.float32)
    low = project[:, :rank].astype(jnp.bfloat16)
    b_rows = project[:, rank : rank + states]
    c_rows = project[:, rank + states :]
    step_size = jax.nn.softplus(
        jnp.dot(low, dt_proj, preferred_element_type=jnp.float32) + bias[None, :]
    )
    return (step_size, b_rows, c_rows)


def slide_bounds(where_at, offsets, lengths, slide_ids):
    which = jnp.sum((where_at[:, None] >= offsets[None, 1:]).astype(jnp.int32), axis=1)
    pick = (which[:, None] == slide_ids[None, :]).astype(jnp.int32)
    begin = jnp.sum(pick * offsets[None, :], axis=1)
    return (begin, begin + jnp.sum(pick * lengths[None, :], axis=1))


def local(
    tile_embed,
    destination,
    slide_lengths,
    w_inner,
    w_gate,
    conv_weight,
    conv_bias,
    x_project,
    dt_project,
    dt_bias,
    decay,
    skip_gain,
):
    shards = lax.axis_size(("seq", "slide"))
    seq_count = lax.axis_size("seq")
    slide_count = lax.axis_size("slide")
    row_count = tile_embed.shape[0]
    model_width = tile_embed.shape[1]
    capacity = 2 * row_count
    width = w_inner.shape[1]
    states = decay.shape[1]
    taps = conv_weight.shape[1]
    slide_ids = jnp.arange(slide_lengths.shape[0], dtype=jnp.int32)
    offsets = jnp.cumsum(slide_lengths) - slide_lengths
    my_seq = lax.axis_index("seq")
    my_slide = lax.axis_index("slide")
    device_ids = jnp.arange(shards, dtype=jnp.int32)
    per_peer = capacity // shards
    slot_index = jnp.arange(per_peer, dtype=jnp.int32)
    device_slide = device_ids % slide_count
    device_seq = device_ids // slide_count
    device_pick = (device_slide[:, None] == slide_ids[None, :]).astype(jnp.int32)
    device_start = jnp.sum(device_pick * offsets[None, :], axis=1) + device_seq * capacity
    device_fill = jnp.clip(
        jnp.sum(device_pick * slide_lengths[None, :], axis=1) - device_seq * capacity, 0, capacity
    )
    first_block = device_start // shards
    live = slot_index[None, :] < (device_fill // shards)[:, None]
    safe_row = jnp.where(live, first_block[:, None] + slot_index[None, :], 0).reshape(-1)
    live_flat = live.reshape(-1)
    mine = slide_ids == my_slide
    my_start = jnp.sum(jnp.where(mine, offsets, 0)) + my_seq * capacity
    my_fill = jnp.clip(jnp.sum(jnp.where(mine, slide_lengths, 0)) - my_seq * capacity, 0, capacity)
    global_pos = my_start + jnp.arange(capacity, dtype=jnp.int32)
    row_begin = global_pos - taps
    row_end = global_pos + taps
    row_offset, _ = slide_bounds(destination, offsets, slide_lengths, slide_ids)
    row_slide = jnp.sum((destination[:, None] >= offsets[None, 1:]).astype(jnp.int32), axis=1)
    row_seq = (destination - row_offset) // capacity
    row_device = row_seq * slide_count + row_slide
    row_slot = destination // shards - (row_offset + row_seq * capacity) // shards
    send_dest = jnp.where(live_flat, jnp.take(destination, safe_row), -1).reshape(shards, per_peer)
    picked = jnp.take(tile_embed, safe_row, axis=0)
    send_rows = jnp.where(live_flat[:, None], picked, jnp.zeros_like(picked)).reshape(
        shards, per_peer, model_width
    )
    rows_in = lax.all_to_all(send_rows, ("seq", "slide"), split_axis=0, concat_axis=0, tiled=True)
    dest_in = lax.all_to_all(send_dest, ("seq", "slide"), split_axis=0, concat_axis=0, tiled=True)
    flat_rows = rows_in.reshape(-1, rows_in.shape[2])
    result = jnp.dot(flat_rows, w_inner, preferred_element_type=jnp.float32).astype(jnp.bfloat16)
    arrived = result.reshape(rows_in.shape[0], rows_in.shape[1], width)
    local_slot = dest_in - my_start
    slot_live = (dest_in >= 0) & (local_slot >= 0) & (local_slot < capacity)
    sort_key = jnp.where(slot_live, local_slot, capacity).reshape(-1)
    order = jnp.argsort(sort_key, stable=True)
    inner_rows = jnp.take(arrived.reshape(shards * per_peer, width), order, axis=0)
    padded = with_halo(inner_rows, (("seq", 0),), taps - 1)
    positions = jnp.arange(capacity, dtype=jnp.int32)
    valid = (positions < my_fill)[:, None]
    forward_sum = conv_bias[0][None, :]
    backward_sum = conv_bias[1][None, :]
    for tap in range(taps):
        ahead_ok = (global_pos - (taps - 1) + tap >= row_begin)[:, None]
        forward_sum = forward_sum + conv_weight[0, tap][None, :] * jnp.where(
            ahead_ok, padded[tap : tap + capacity], 0.0
        )
        lead = 2 * (taps - 1) - tap
        behind_ok = (global_pos + (taps - 1) - tap < row_end)[:, None]
        backward_sum = backward_sum + conv_weight[1, tap][None, :] * jnp.where(
            behind_ok, padded[lead : lead + capacity], 0.0
        )
    u_fwd = jnp.where(valid, jax.nn.silu(forward_sum), 0.0).astype(jnp.bfloat16)
    u_bwd = jnp.where(valid, jax.nn.silu(backward_sum), 0.0).astype(jnp.bfloat16)
    dt_fwd, b_fwd, c_fwd = direction_terms(u_fwd, x_project[0], dt_project[0], dt_bias[0], states)
    dt_bwd, b_bwd, c_bwd = direction_terms(u_bwd, x_project[1], dt_project[1], dt_bias[1], states)
    rates_fwd = -decay[0]
    rates_bwd = -decay[1]
    mixed_fwd = u_fwd.astype(jnp.float32)
    mixed_bwd = u_bwd.astype(jnp.float32)
    keep_fwd = (global_pos != row_begin).astype(jnp.float32)
    keep_bwd = (global_pos != row_end - 1).astype(jnp.float32)
    alive_fwd = lax.cumprod(keep_fwd, axis=0)
    alive_bwd = lax.cumprod(keep_bwd, axis=0, reverse=True)
    empty = jnp.zeros((states, width), jnp.float32)
    local_fwd, rows_fwd = state_sweep(
        empty, dt_fwd, mixed_fwd, b_fwd, c_fwd, keep_fwd, rates_fwd, False
    )
    local_bwd, rows_bwd = state_sweep(
        empty, dt_bwd, mixed_bwd, b_bwd, c_bwd, keep_bwd, rates_bwd, True
    )
    pass_fwd = jnp.exp(rates_fwd * jnp.sum(dt_fwd, axis=0)[None, :]) * alive_fwd[capacity - 1]
    pass_bwd = jnp.exp(rates_bwd * jnp.sum(dt_bwd, axis=0)[None, :]) * alive_bwd[0]

    def relay_step(turn, carried):
        from_below, from_above = carried
        from_below = shifted(pass_fwd * from_below + local_fwd, "seq", 1)
        from_above = shifted(pass_bwd * from_above + local_bwd, "seq", -1)
        return (from_below, from_above)

    enter_fwd, enter_bwd = lax.fori_loop(0, seq_count - 1, relay_step, (empty, empty))
    y_fwd = (
        rows_fwd
        + entering_rows(enter_fwd, dt_fwd, c_fwd, alive_fwd, rates_fwd, False)
        + skip_gain[0][None, :] * mixed_fwd
    )
    y_bwd = (
        rows_bwd
        + entering_rows(enter_bwd, dt_bwd, c_bwd, alive_bwd, rates_bwd, True)
        + skip_gain[1][None, :] * mixed_bwd
    )
    total = (y_fwd + y_bwd).astype(jnp.bfloat16)
    back_index = jnp.clip(local_slot, 0, capacity - 1).reshape(-1)
    send_back = jnp.take(total, back_index, axis=0).reshape(shards, per_peer, width)
    returned = lax.all_to_all(send_back, ("seq", "slide"), split_axis=0, concat_axis=0, tiled=True)
    gathered = jnp.take(
        returned.reshape(shards * per_peer, width), row_device * per_peer + row_slot, axis=0
    )
    gate = jnp.dot(tile_embed, w_gate, preferred_element_type=jnp.float32)
    return (gathered.astype(jnp.float32) * jax.nn.silu(gate)).astype(jnp.bfloat16)


def solution(mesh):
    placed = (
        P(("seq", "slide"), None),
        P(("seq", "slide")),
        P(),
        P(),
        P(),
        P(),
        P(),
        P(),
        P(),
        P(),
        P(),
        P(),
    )
    return jax.shard_map(
        local, mesh=mesh, in_specs=placed, out_specs=P(("seq", "slide"), None), check_vma=False
    )
```

profile of v0, /device:TPU:1, one launch (start us, length us, event | category | flops | bytes accessed | tf_op | source)
XLA Modules:
  0.0 1487.6 jit_solution(12748699543569437288)
XLA Ops:
  7.5 11.5 all-to-all-start.1
  35.8 10.4 all-to-all-start
  50.6 12.3 all-to-all-done
  100.3 28.2 %fusion.202 = f32[3072,2,128]{0,1,2:T(2,128)S(1)} fusion(f32[3072,2,128]{0,2,1:T(8,128)S(1)} %bitcast.1122), kind=kOutput, calls=%fused_computation.454 | output fusion | flops 99876864 | bytes 6291456 | tf_op jit(solution)/shard_map/reduce-window.7
  140.7 462.8 %while.44 = (s32[]{:T(128)}, f32[16,3072]{1,0:T(8,128)S(1)}, f32[16,16,3072]{2,1,0:T(8,128)}, f32[16,16]{1,0:T(8,128)}, f32[16,16,3072]{2,1,0:T(8,128)}, /*index...) while((s32[]{:T(128)}, f32[16,3072]{1,0:T(8,128)S(1)}, ...), condition=%wide.region_51.53_spmd.clone, body=%wide.region_34.52_spmd.clone.sunk | while | flops 8306707 | bytes 6177224 | solution.py:52
  628.8 441.3 %while.43 = (s32[]{:T(128)}, f32[16,3072]{1,0:T(8,128)S(1)}, f32[16,16,3072]{2,1,0:T(8,128)}, f32[16,16]{1,0:T(8,128)}, f32[16,16,3072]{2,1,0:T(8,128)}, /*index...) while((s32[]{:T(128)}, f32[16,3072]{1,0:T(8,128)S(1)}, ...), condition=%wide.region_25.27_spmd.clone, body=%wide.region_8.26_spmd.clone.sunk | while | flops 8306706 | bytes 6571840 | solution.py:52
  635.2 10.9 multiply_reduce_fusion.42
  662.7 10.9 multiply_reduce_fusion.42
  690.3 10.9 multiply_reduce_fusion.42
  717.8 10.9 multiply_reduce_fusion.42
  745.5 10.9 multiply_reduce_fusion.42
  773.2 10.9 multiply_reduce_fusion.42
  800.8 10.9 multiply_reduce_fusion.42
  828.5 10.9 multiply_reduce_fusion.42
  855.9 10.9 multiply_reduce_fusion.42
  883.5 10.9 multiply_reduce_fusion.42
  911.1 10.9 multiply_reduce_fusion.42
  938.5 10.9 multiply_reduce_fusion.42
  966.3 10.9 multiply_reduce_fusion.42
  993.6 10.9 multiply_reduce_fusion.42
  1021.0 10.9 multiply_reduce_fusion.42
  1048.8 10.9 multiply_reduce_fusion.42
  1072.2 337.5 %while.42 = (s32[]{:T(128)}, f32[16,3072]{1,0:T(8,128)S(1)}, f32[16,3072]{1,0:T(8,128)S(1)}, f32[16,3072]{1,0:T(8,128)S(1)}, f32[16,3072]{1,0:T(8,128)S(1)}, /*i...) while((s32[]{:T(128)}, f32[16,3072]{1,0:T(8,128)S(1)}, f32[16,3072]{1,0:T(8,128)S(1)}, ...), condition=%wide.region_53.55_spmd, body=%wide.region_52.54_spmd.sunk | while | flops 196610 | bytes 3145893 | solution.py:198
  1114.6 6.5 collective-permute-done.1
  1125.7 6.5 collective-permute-done.1
  1136.8 6.5 collective-permute-done.1
  1147.9 6.5 collective-permute-done.1
  1159.0 6.5 collective-permute-done.1
  1170.1 6.5 collective-permute-done.1
  1410.0 28.0 %fusion.70 = bf16[256,3072]{1,0:T(8,128)(2,1)S(1)} fusion(f32[3072,2,128]{0,2,1:T(8,128)} %copy.48, f32[16,16,3072]{2,1,0:T(8,128)} %get-tuple-element.278, f32[3072,2,128]{0,2,1:T(8,128)} %copy.44, f32[16,16,3072]{2,1,0:T(8,128)} %get-tuple-element.274, f32[3072]{0:T(1024)} %bitcast.1355, f32[256]{0:T(256)} %copy-done.30, f32[3072]{0:T(1024)S(1)} %bitcast.1323, ...), kind=kLoop, calls=%fused_computation.281 | loop fusion | flops 108527616 | bytes 18147328 | tf_op jit(solution)/shard_map/convert_element_type | solution.py:209
  1441.6 12.8 all-to-all-start.2
  1454.5 25.0 %all-to-all-done.2 = bf16[128,2,3072]{2,1,0:T(2,128)(2,1)S(1)} async-done(((bf16[128,2,3072]{2,1,0:T(2,128)(2,1)}), bf16[128,2,3072]{2,1,0:T(2,128)(2,1)S(1)}, u32[]{:S(2)}, u32[]{:S(2)}) %all-to-all-start.2) | async-done | bytes 1572896 | tf_op jit(solution)/shard_map/all_to_all | solution.py:212
  (1563 shorter events, 1134.9 us)
Async XLA Ops:
  7.5 28.4 %all-to-all-start.1 = ((s32[128,1,2]{2,1,0:T(1,128)}), s32[128,1,2]{2,1,0:T(1,128)S(1)}, u32[]{:S(2)}, u32[]{:S(2)}) async-start(s32[128,1,2]{2,1,0:T(1,128)} %bitcast.3), calls=%async_computation.1 | async-start | bytes 131072 | tf_op jit(solution)/shard_map/all_to_all | solution.py:146
  35.8 27.1 %all-to-all-start = ((bf16[128,2,1536]{2,1,0:T(2,128)(2,1)}), bf16[128,2,1536]{2,1,0:T(2,128)(2,1)S(1)}, u32[]{:S(2)}, u32[]{:S(2)}) async-start(bf16[128,2,1536]{2,1,0:T(2,128)(2,1)} %broadcast_select_fusion.3), calls=%async_computation | async-start | bytes 1572864 | tf_op jit(solution)/shard_map/all_to_all | solution.py:145
  78.1 10.0 collective-permute-start.2
  1101.2 8.8 collective-permute-start.1
  1112.0 9.1 collective-permute-start.1
  1123.1 9.1 collective-permute-start.1
  1134.2 9.1 collective-permute-start.1
  1145.3 9.1 collective-permute-start.1
  1156.4 9.1 collective-permute-start.1
  1167.5 9.1 collective-permute-start.1
  1178.6 9.1 collective-permute-start.1
  1189.7 9.1 collective-permute-start.1
  1200.8 9.1 collective-permute-start.1
  1211.9 9.1 collective-permute-start.1
  1223.0 9.1 collective-permute-start.1
  1234.1 9.1 collective-permute-start.1
  1245.2 9.1 collective-permute-start.1
  1256.3 9.1 collective-permute-start.1
  1267.4 9.1 collective-permute-start.1
  1278.5 9.1 collective-permute-start.1
  1289.6 9.1 collective-permute-start.1
  1300.7 9.1 collective-permute-start.1
  1311.8 9.1 collective-permute-start.1
  1322.9 9.1 collective-permute-start.1
  1334.0 9.1 collective-permute-start.1
  1345.1 9.1 collective-permute-start.1
  1356.2 9.1 collective-permute-start.1
  1367.3 9.1 collective-permute-start.1
  1378.4 9.1 collective-permute-start.1
  1389.5 9.1 collective-permute-start.1
  1400.6 9.1 collective-permute-start.1
  1441.6 37.9 %all-to-all-start.2 = ((bf16[128,2,3072]{2,1,0:T(2,128)(2,1)}), bf16[128,2,3072]{2,1,0:T(2,128)(2,1)S(1)}, u32[]{:S(2)}, u32[]{:S(2)}) async-start(bf16[128,2,3072]{2,1,0:T(2,128)(2,1)} %reshape.1402), calls=%async_computation.2 | async-start | bytes 3145728 | tf_op jit(solution)/shard_map/all_to_all | solution.py:212
  (238 other events, 4251.5 us)
where the time goes:
time: 1510 us; the launch traced here: 1490 us
  other arithmetic  778 us (52%)
  local copies, waits for them, and re-layouts  262 us (17%)
  waiting for transfers between devices  238 us (16%)
  starting transfers between devices  175 us (12%)
  matrix products  24 us (2%)
    reduce_sum x160, other arithmetic, row_step(): return (hidden, jnp.sum(c_row[:, None] * hidden, axis=0))  666 us
    ppermute x62, waiting for transfers between devices, shifted(): return lax.ppermute(block, axis, route)  200 us
    ppermute x62, starting transfers between devices, shifted(): return lax.ppermute(block, axis, route)  134 us
    slice x64, local copies, waits for them, and re-layouts, block_step(): return lax.scan(row_step, hidden, block_data, reverse=reverse, unroll=True)  117 us
    another operation x9, other arithmetic  39.1 us
  transfers between devices with their start and end apart: 67, of which 64 were waited for; matrix products, arithmetic and copies ran while one was open for 2% of the time, Pallas kernels for 0%

commit v1 on v0

v1 whole, which is shorter than its diff:
```python
import jax
import jax.numpy as jnp
from jax import lax
from jax.experimental import pallas as pl
from jax.experimental.pallas import tpu as pltpu
from jax.sharding import PartitionSpec as P

AXES = ("seq", "slide")
SUB = 8
LANES = 128
LOG2E = 1.4426950408889634


def row_positions(shape, per_sub):
    lane = lax.broadcasted_iota(jnp.int32, shape, 1)
    return (lane % SUB) * per_sub + lane // SUB


def one_hot(pos, half):
    place = row_positions(pos.shape, pos.shape[1] // SUB)
    odd = lax.broadcasted_iota(jnp.int32, pos.shape, 0) % 2
    hit = (pos.astype(jnp.int32) == place) & (odd == half)
    return hit.astype(jnp.float32).astype(jnp.bfloat16)


def over_rows(left, right):
    return lax.dot_general(
        left, right, (((0,), (0,)), ((), ())), preferred_element_type=jnp.float32
    )


def sort_kernel(arrived, sorted_rows, ahead, behind, places):
    width = sorted_rows.shape[1] // 2
    rows = sorted_rows.shape[0]
    data = arrived[:, :width]
    pos = arrived[:, width:].astype(jnp.float32)
    places[...] = pos
    lane = lax.broadcasted_iota(jnp.int32, pos.shape, 1)
    odd = lax.broadcasted_iota(jnp.int32, pos.shape, 0) % 2
    edge = jnp.where(lane < SUB, lane + rows - 3, lane - SUB)
    edge = jnp.where((lane % SUB < 3) & (lane < 2 * SUB), edge, -1)
    for half in range(2):
        cols = pl.ds(half * width, width)
        sorted_rows[:, cols] = over_rows(one_hot(pos, half), data).astype(jnp.bfloat16)
        hit = (pos.astype(jnp.int32) == edge) & (odd == half)
        ends = over_rows(hit.astype(jnp.float32).astype(jnp.bfloat16), data)
        ahead[:, cols] = ends[:SUB].astype(jnp.bfloat16)
        behind[:, cols] = ends[SUB : 2 * SUB].astype(jnp.bfloat16)


def sublane(shape):
    return lax.broadcasted_iota(jnp.int32, shape, 0)


def shift_sublanes(tile, count, reverse):
    return pltpu.roll(tile, SUB - count if reverse else count, 0)


def in_reach(count, reverse):
    row = sublane((SUB, LANES))
    return row < SUB - count if reverse else row >= count


def tiles_of(array):
    return [array[SUB * t : SUB * t + SUB] for t in range(array.shape[0] // SUB)]


def in_order(count, reverse):
    return list(range(count))[::-1] if reverse else list(range(count))


def spread_columns(target, d, columns, first, count):
    for n in range(count):
        target[d, n] = jnp.broadcast_to(
            columns[:, first + n : first + n + 1], (columns.shape[0], LANES)
        )


def silu(v):
    return v / (1.0 + jnp.exp(-v))


def softplus(v):
    return jnp.maximum(v, 0.0) + jnp.log1p(jnp.exp(-jnp.abs(v)))


def states_kernel(
    flags,
    rows_in,
    before,
    after,
    w_inner,
    conv_weight,
    conv_bias,
    x_project,
    dt_project,
    dt_bias,
    rates,
    u_out,
    proj_out,
    dt_out,
    inner_states,
    payload,
    all_rows,
    extended,
    b_wide,
):
    step = pl.program_id(0)
    tiles = pl.num_programs(0) // 2
    rows = rows_in.shape[0]
    taps = conv_weight.shape[1]
    reach = taps - 1
    width = w_inner.shape[1]
    states = rates.shape[1]
    rank = dt_project.shape[1]
    slots = rows // SUB

    @pl.when(step == 0)
    def _():
        all_rows[:rows] = rows_in[...]
        all_rows[rows : rows + SUB] = before[...]
        all_rows[rows + SUB :] = after[...]
        proj_out[...] = jnp.zeros_like(proj_out)

    @pl.when(step < tiles)
    def _():
        inner = jnp.dot(all_rows[...], w_inner[...], preferred_element_type=jnp.float32)
        inner = inner.astype(jnp.bfloat16).astype(jnp.float32)
        main = inner[:rows]
        prior = inner[rows : rows + SUB] * flags[0].astype(jnp.float32)
        later = inner[rows + SUB :] * flags[1].astype(jnp.float32)
        row = sublane((SUB, width))
        extended[SUB * reach : SUB * reach + rows] = main
        for k in range(reach):
            own = main[rows - SUB * (reach - k) : rows - SUB * (reach - k - 1)]
            extended[SUB * k : SUB * k + SUB] = jnp.where(
                row == 0, prior[k : k + 1], pltpu.roll(own, 1, 0)
            )
            own = main[SUB * k : SUB * k + SUB]
            base = SUB * (reach + slots + k)
            extended[base : base + SUB] = jnp.where(
                row == SUB - 1, later[k : k + 1], pltpu.roll(own, SUB - 1, 0)
            )
        cols = pl.ds(pl.multiple_of(step * width, LANES), width)
        for d in range(2):
            mixed = conv_bias[d : d + 1, :]
            for tap in range(taps):
                base = SUB * (2 * reach - tap if d else tap)
                mixed = mixed + conv_weight[d, tap : tap + 1, :] * extended[base : base + rows]
            u = silu(mixed).astype(jnp.bfloat16)
            u_out[d, :, cols] = u
            proj_out[d] += jnp.dot(u, x_project[d], preferred_element_type=jnp.float32)

    @pl.when(step == tiles)
    def _():
        for d in range(2):
            spread_columns(b_wide, d, proj_out[d], rank, states)

    @pl.when(step >= tiles)
    def _():
        for d in range(2):
            low = proj_out[d][:, :rank].astype(jnp.bfloat16)
            raw = jnp.dot(low, dt_project[d], preferred_element_type=jnp.float32)
            dt_out[d] = softplus(raw + dt_bias[d : d + 1, :])

        def lane_block(block, carry):
            start = pl.multiple_of(block * LANES, LANES)
            here = pl.ds(start, LANES)
            there = pl.ds(pl.multiple_of((step - tiles) * width + start, LANES), LANES)
            for d in range(2):
                reverse = d == 1
                dt = dt_out[d, :, here]
                fed = tiles_of(dt * u_out[d, :, there].astype(jnp.float32))
                dt = tiles_of(dt)
                total = dt[0]
                for t in range(1, slots):
                    total = total + dt[t]
                finals = []
                for n in range(states):
                    rate = rates[d, n : n + 1, here]
                    state = None
                    for t in in_order(slots, reverse):
                        new = fed[t] * b_wide[d, n, SUB * t : SUB * t + SUB]
                        if state is not None:
                            new = jnp.exp2(dt[t] * rate) * state + new
                        state = new
                    keep = jnp.exp2(total * rate)
                    for count in (1, 2, 4):
                        keep = jnp.where(in_reach(count, reverse), keep, 0.0)
                        state = state + keep * shift_sublanes(state, count, reverse)
                        if count < 4:
                            keep = keep * shift_sublanes(keep, count, reverse)
                    inner_states[d, n, :, here] = state
                    finals.append(state[0:1] if reverse else state[SUB - 1 : SUB])
                whole = jnp.sum(total, axis=0, keepdims=True)
                row = sublane((SUB, LANES))
                for n in range(0, states, 2):
                    out = jnp.where(row == 0, finals[n], finals[n + 1])
                    out = jnp.where(row >= 2, whole, out)
                    payload[d, n // 2, 0, :, here] = out[:4].astype(jnp.bfloat16)
            return carry

        lax.fori_loop(0, width // LANES, lane_block, 0)


def relay_kernel(keep, payload, rates, entering):
    blocks = payload.shape[0]
    backward = keep[blocks]

    def block_step(i, state):
        at = jnp.where(backward == 1, blocks - 1 - i, i)
        state = state * keep[at].astype(jnp.float32)
        entering[at] = state.astype(jnp.bfloat16)
        row = payload[at].astype(jnp.float32)
        return jnp.exp2(rates[...] * row[2:3]) * state + row[0:2]

    lax.fori_loop(0, blocks, block_step, jnp.zeros(rates.shape, jnp.float32), unroll=4)


def outputs_kernel(
    entering,
    inner_states,
    dt_in,
    u_in,
    proj,
    rates,
    skip_gain,
    places,
    out,
    b_wide,
    c_wide,
    mixed,
    partial,
):
    half = pl.program_id(1)
    states = rates.shape[1]
    rows = dt_in.shape[1]
    slots = rows // SUB
    rank = proj.shape[2] - 2 * states

    @pl.when((pl.program_id(0) == 0) & (half == 0))
    def _():
        for d in range(2):
            spread_columns(b_wide, d, proj[d], rank, states)
            spread_columns(c_wide, d, proj[d], rank + states, states)

    def lane_block(block, carry):
        here = pl.ds(pl.multiple_of(block * LANES, LANES), LANES)
        sums = None
        for d in range(2):
            reverse = d == 1
            dt = dt_in[d, :, here]
            u = u_in[d, :, here].astype(jnp.float32)
            fed = tiles_of(dt * u)
            dt = tiles_of(dt)
            u = tiles_of(u)
            ahead = dt[0]
            for t in range(1, slots):
                ahead = ahead + dt[t]
            for count in (1, 2, 4):
                moved = shift_sublanes(ahead, count, reverse)
                ahead = ahead + jnp.where(in_reach(count, reverse), moved, 0.0)
            near = in_reach(1, reverse)
            ahead = jnp.where(near, shift_sublanes(ahead, 1, reverse), 0.0)
            gain = skip_gain[d : d + 1, here]
            if sums is None:
                sums = [gain * tile for tile in u]
            else:
                sums = [total + gain * tile for total, tile in zip(sums, u)]
            for n in range(states):
                rate = rates[d, n : n + 1, here]
                pair = entering[d, n // 2, 0, :, here].astype(jnp.float32)
                state = inner_states[d, n, :, here]
                state = jnp.where(near, shift_sublanes(state, 1, reverse), 0.0)
                state = state + jnp.exp2(ahead * rate) * pair[n % 2 : n % 2 + 1]
                for t in in_order(slots, reverse):
                    at = slice(SUB * t, SUB * t + SUB)
                    state = jnp.exp2(dt[t] * rate) * state + fed[t] * b_wide[d, n, at]
                    sums[t] = sums[t] + c_wide[d, n, at] * state
        for t in range(slots):
            mixed[SUB * t : SUB * t + SUB, here] = sums[t]
        return carry

    lax.fori_loop(0, dt_in.shape[2] // LANES, lane_block, 0)
    pick = one_hot(places[...], half)
    placed = jnp.dot(pick, mixed[...].astype(jnp.bfloat16), preferred_element_type=jnp.float32)

    @pl.when(half == 0)
    def _():
        partial[...] = placed

    @pl.when(half == 1)
    def _():
        out[...] = (partial[...] + placed).astype(jnp.bfloat16)


def gate_kernel(returned, gate, out):
    rows = out.shape[0]
    width = returned.shape[1]
    row = lax.broadcasted_iota(jnp.int32, (rows, 2 * rows), 0)
    col = lax.broadcasted_iota(jnp.int32, (rows, 2 * rows), 1)
    for half in range(2):
        pick = (col == 2 * row + half).astype(jnp.float32).astype(jnp.bfloat16)
        total = jnp.dot(pick, returned[...], preferred_element_type=jnp.float32)
        cols = pl.ds(half * width, width)
        out[:, cols] = (total * gate[:, cols]).astype(jnp.bfloat16)


def full(shape):
    return pl.BlockSpec(shape, lambda *_: (0,) * len(shape))


def local(
    tile_embed,
    destination,
    slide_lengths,
    w_inner,
    w_gate,
    conv_weight,
    conv_bias,
    x_project,
    dt_project,
    dt_bias,
    decay,
    skip_gain,
):
    f32, bf16 = jnp.float32, jnp.bfloat16
    shards = lax.axis_size(AXES)
    me = lax.axis_index(AXES)
    rows, model = tile_embed.shape
    width = w_inner.shape[1]
    states = decay.shape[1]
    rank = dt_project.shape[1]
    taps = conv_weight.shape[1]
    tile = 3 * LANES
    groups = width // tile
    owner_states = 2 * groups * states // shards
    state_groups = states // owner_states
    slots = rows // SUB
    limits = pltpu.CompilerParams(vmem_limit_bytes=56 * 1024 * 1024)

    blocks = jnp.arange(shards, dtype=jnp.int32)
    slide = jnp.arange(slide_lengths.shape[0], dtype=jnp.int32)
    ends = jnp.sum(jnp.where(slide[:, None] <= slide[None, :], slide_lengths[:, None], 0), axis=0)
    starts = ends - slide_lengths
    opens = jnp.any(blocks[:, None] * rows == starts[None, :], axis=1)
    closes = jnp.any((blocks[:, None] + 1) * rows == ends[None, :], axis=1)
    mine = blocks == me
    flags = jnp.stack([~jnp.any(opens & mine), ~jnp.any(closes & mine)]).astype(jnp.int32)
    owner_dir = me // (state_groups * groups)
    owner_group = (me // groups) % state_groups
    owner_tile = me % groups
    keep = jnp.where(owner_dir == 1, ~closes, ~opens).astype(jnp.int32)
    keep = jnp.concatenate([keep, jnp.full((SUB,), owner_dir, jnp.int32)])
    rates = decay * (-LOG2E)
    owner_rates = lax.dynamic_slice(
        rates, (owner_dir, owner_group * owner_states, owner_tile * tile), (1, owner_states, tile)
    )[0]

    offset = (destination - blocks * rows).astype(bf16)
    offset = jnp.broadcast_to(offset[:, None, None], (rows, 2, LANES))
    sent = jnp.concatenate([tile_embed.reshape(rows, 2, model // 2), offset], axis=2)
    arrived = lax.all_to_all(sent, AXES, split_axis=0, concat_axis=0, tiled=True)
    arrived = arrived.reshape(2 * rows, model // 2 + LANES)

    gate = jax.nn.silu(jnp.dot(tile_embed, w_gate, preferred_element_type=f32))

    block_rows, ahead, behind, places = pl.pallas_call(
        sort_kernel,
        out_shape=(
            jax.ShapeDtypeStruct((rows, model), bf16),
            jax.ShapeDtypeStruct((SUB, model), bf16),
            jax.ShapeDtypeStruct((SUB, model), bf16),
            jax.ShapeDtypeStruct((2 * rows, LANES), f32),
        ),
        compiler_params=limits,
        name="sort_rows",
    )(arrived)
    before = lax.ppermute(ahead, AXES, [(i, i + 1) for i in range(shards - 1)])
    after = lax.ppermute(behind, AXES, [(i + 1, i) for i in range(shards - 1)])

    def early(*at):
        return lambda i, *_: tuple(jnp.minimum(i, groups - 1) if a else 0 for a in at)

    def late(*at):
        return lambda i, *_: tuple(jnp.maximum(i - groups, 0) if a else 0 for a in at)

    u, proj, dt, inner_states, payload = pl.pallas_call(
        states_kernel,
        out_shape=(
            jax.ShapeDtypeStruct((2, rows, width), bf16),
            jax.ShapeDtypeStruct((2, rows, LANES), f32),
            jax.ShapeDtypeStruct((2, rows, width), f32),
            jax.ShapeDtypeStruct((2, states, SUB, width), f32),
            jax.ShapeDtypeStruct((2, state_groups, groups, 4, tile), bf16),
        ),
        grid_spec=pltpu.PrefetchScalarGridSpec(
            num_scalar_prefetch=1,
            grid=(2 * groups,),
            in_specs=[
                full((rows, model)),
                full((SUB, model)),
                full((SUB, model)),
                pl.BlockSpec((model, tile), early(0, 1)),
                pl.BlockSpec((2, taps, tile), early(0, 0, 1)),
                pl.BlockSpec((2, tile), early(0, 1)),
                pl.BlockSpec((2, tile, LANES), early(0, 1, 0)),
                pl.BlockSpec((2, rank, tile), late(0, 0, 1)),
                pl.BlockSpec((2, tile), late(0, 1)),
                pl.BlockSpec((2, states, tile), late(0, 0, 1)),
            ],
            out_specs=[
                full((2, rows, width)),
                full((2, rows, LANES)),
                pl.BlockSpec((2, rows, tile), late(0, 0, 1)),
                pl.BlockSpec((2, states, SUB, tile), late(0, 0, 0, 1)),
                pl.BlockSpec((2, state_groups, 1, 4, tile), late(0, 0, 1, 0, 0)),
            ],
            scratch_shapes=[
                pltpu.VMEM((rows + 2 * SUB, model), bf16),
                pltpu.VMEM((rows + 2 * SUB * (taps - 1), tile), f32),
                pltpu.VMEM((2, states, rows, LANES), f32),
            ],
        ),
        compiler_params=limits,
        name="block_states",
    )(
        flags, block_rows, before, after, w_inner, conv_weight, conv_bias,
        x_project, dt_project, dt_bias, rates,
    )

    shared = lax.all_to_all(
        payload.reshape(shards, 4, tile), AXES, split_axis=0, concat_axis=0, tiled=True
    )
    entering = pl.pallas_call(
        relay_kernel,
        out_shape=jax.ShapeDtypeStruct((shards, owner_states, tile), bf16),
        grid_spec=pltpu.PrefetchScalarGridSpec(
            num_scalar_prefetch=1,
            grid=(1,),
            in_specs=[full((shards, 4, tile)), full((owner_states, tile))],
            out_specs=full((shards, owner_states, tile)),
        ),
        compiler_params=limits,
        name="relay",
    )(keep, shared, owner_rates)
    entering = lax.all_to_all(entering, AXES, split_axis=0, concat_axis=0, tiled=True)
    entering = entering.reshape(2, state_groups, groups, owner_states, tile)

    pairs = groups // 2
    totals = pl.pallas_call(
        outputs_kernel,
        out_shape=jax.ShapeDtypeStruct((2 * rows, width // 2), bf16),
        grid=(pairs, 2),
        in_specs=[
            pl.BlockSpec((2, state_groups, 1, owner_states, tile), lambda i, k: (0, 0, k * pairs + i, 0, 0)),
            pl.BlockSpec((2, states, SUB, tile), lambda i, k: (0, 0, 0, k * pairs + i)),
            pl.BlockSpec((2, rows, tile), lambda i, k: (0, 0, k * pairs + i)),
            pl.BlockSpec((2, rows, tile), lambda i, k: (0, 0, k * pairs + i)),
            full((2, rows, LANES)),
            pl.BlockSpec((2, states, tile), lambda i, k: (0, 0, k * pairs + i)),
            pl.BlockSpec((2, tile), lambda i, k: (0, k * pairs + i)),
            full((2 * rows, LANES)),
        ],
        out_specs=pl.BlockSpec((2 * rows, tile), lambda i, k: (0, i)),
        scratch_shapes=[
            pltpu.VMEM((2, states, rows, LANES), f32),
            pltpu.VMEM((2, states, rows, LANES), f32),
            pltpu.VMEM((rows, tile), f32),
            pltpu.VMEM((2 * rows, tile), f32),
        ],
        compiler_params=limits,
        name="block_outputs",
    )(entering, inner_states, dt, u, proj, rates, skip_gain, places)

    returned = lax.all_to_all(
        totals.reshape(rows, 2, width // 2), AXES, split_axis=0, concat_axis=0, tiled=True
    )
    return pl.pallas_call(
        gate_kernel,
        out_shape=jax.ShapeDtypeStruct((rows, width), bf16),
        compiler_params=limits,
        name="gated",
    )(returned.reshape(2 * rows, width // 2), gate)


def solution(mesh):
    placed = (P(AXES, None), P(AXES)) + (P(),) * 10
    return jax.shard_map(
        local, mesh=mesh, in_specs=placed, out_specs=P(AXES, None), check_vma=False
    )
```

time: 1510 us -> 159 us (0.11); the launches traced: 1490 us -> 158 us
  other arithmetic: 778 us -> 4.18 us
  local copies, waits for them, and re-layouts: 262 us -> 9.66 us
  waiting for transfers between devices: 238 us -> 31.9 us
  starting transfers between devices: 175 us -> 33.6 us
  Pallas kernels: 0 us -> 56 us
  matrix products: 24 us -> 6.34 us
  blocking collectives: 0 us -> 15.2 us
    reduce_sum x163 -> x1, other arithmetic: 669 us -> 0.08 us  [local(): jnp.sum(jnp.where(slide[:, None] <= slide[None, :], slide_lengths[:, None...]
    ppermute x64 -> x2, waiting for transfers between devices: 200 us -> 0.46 us  [the longest x1 0.46 us: local(): after = lax.ppermute(behind, AXES, [(i + 1, i) for i in range(shards - 1)])]
    ppermute x64 -> x2, starting transfers between devices: 140 us -> 6.76 us  [the longest x1 4.56 us: local(): after = lax.ppermute(behind, AXES, [(i + 1, i) for i in range(shards - 1)])]
    slice x80 -> x0, local copies, waits for them, and re-layouts: 124 us -> none  [the longest x64 117 us: block_step(): return lax.scan(row_step, hidden, block_data, reverse=reverse, unroll=True)]
    mul x32 -> x0, local copies, waits for them, and re-layouts: 56.1 us -> none  [the longest x16 29.9 us: row_step(): return (hidden, jnp.sum(c_row[:, None] * hidden, axis=0))]
    pallas_call x0 -> x5, Pallas kernels: none -> 56 us  [the longest x1 27.2 us: local(): pl.pallas_call(states_kernel, out_shape=(jax.ShapeDtypeStruct((2, rows, w...]
    another operation x11 -> x0, other arithmetic: 43.3 us -> none
    convert_element_type x5 -> x2, other arithmetic: 38.1 us -> 1.33 us  [the longest x1 0.67 us: local(): jnp.stack([~jnp.any(opens & mine), ~jnp.any(closes & mine)])]
  transfers between devices with their start and end apart: 67 -> 5, of which waited for: 64 -> 4; matrix products, arithmetic and copies ran while one was open for 2% -> 7% of each run, Pallas kernels for 0% -> 0%
where the time goes in v1:
time: 159 us; the launch traced here: 158 us
  Pallas kernels  56 us (35%)
  starting transfers between devices  33.6 us (21%)
  waiting for transfers between devices  31.9 us (20%)
  blocking collectives  15.2 us (10%)
  local copies, waits for them, and re-layouts  9.66 us (6%)
  matrix products  6.34 us (4%)
  other arithmetic  4.18 us (3%)
    pallas_call x1, Pallas kernels, local(): pl.pallas_call(states_kernel, out_shape=(jax.ShapeDtypeStruct((2, rows, w...  27.2 us
    pallas_call x1, Pallas kernels, local(): pl.pallas_call(outputs_kernel, out_shape=jax.ShapeDtypeStruct((2 * rows,...  20.2 us
    all_to_all x1, blocking collectives, local(): lax.all_to_all(entering, AXES, split_axis=0, concat_axis=0, tiled=True)  15.2 us
    all_to_all x1, starting transfers between devices, local(): lax.all_to_all(sent, AXES, split_axis=0, concat_axis=0, tiled=True)  11.5 us
    all_to_all x1, starting transfers between devices, local(): lax.all_to_all(payload.reshape(shards, 4, tile), AXES, split_axis=0, conc...  11.1 us
    all_to_all x1, waiting for transfers between devices, local(): lax.all_to_all(payload.reshape(shards, 4, tile), AXES, split_axis=0, conc...  10.7 us
    all_to_all x1, waiting for transfers between devices, local(): lax.all_to_all(totals.reshape(rows, 2, width // 2), AXES, split_axis=0, c...  10.4 us
    all_to_all x1, waiting for transfers between devices, local(): lax.all_to_all(sent, AXES, split_axis=0, concat_axis=0, tiled=True)  10.3 us
  transfers between devices with their start and end apart: 5, of which 4 were waited for; matrix products, arithmetic and copies ran while one was open for 7% of the time, Pallas kernels for 0%

profile of v1, /device:TPU:1, one launch (start us, length us, event | category | flops | bytes accessed | tf_op | source)
XLA Modules:
  0.0 158.3 jit_solution(11405233372070573196)
XLA Ops:
  0.0 1.1 reshape.34
  1.1 0.7 subtract_convert_fusion
  1.8 0.2 broadcast_in_dim.16
  2.0 1.2 pad_maximum_fusion
  3.2 11.5 %all-to-all-start = ((bf16[128,2,896]{2,1,0:T(2,128)(2,1)}), bf16[128,2,896]{2,1,0:T(2,128)(2,1)S(1)}, u32[]{:S(2)}, u32[]{:S(2)}) async-start(bf16[128,2,896]{2,1,0:T(2,128)(2,1)} %pad_maximum_fusion), calls=%async_computation | async-start | bytes 917504 | tf_op jit(solution)/shard_map/all_to_all | solution.py:363
  14.9 0.1 compare_reduce_fusion
  15.0 0.7 and_reduce_fusion.1
  16.9 0.8 broadcast_multiply_fusion.rates
  17.7 10.3 %all-to-all-done = bf16[128,2,896]{2,1,0:T(2,128)(2,1)S(1)} async-done(((bf16[128,2,896]{2,1,0:T(2,128)(2,1)}), bf16[128,2,896]{2,1,0:T(2,128)(2,1)S(1)}, u32[]{:S(2)}, u32[]{:S(2)}) %all-to-all-start) | async-done | bytes 458784 | tf_op jit(solution)/shard_map/all_to_all | solution.py:363
  28.0 0.9 reshape.35.arrived
  28.9 2.2 %sort_rows.1 = (bf16[128,1536]{1,0:T(8,128)(2,1)}, bf16[8,1536]{1,0:T(8,128)(2,1)}, bf16[8,1536]{1,0:T(8,128)(2,1)}, f32[256,128]{1,0:T(8,128)}) custom-call(bf16[256,896]{1,0:T(8,128)(2,1)} %reshape.35.arrived), custom_call_target="tpu_custom_call" | custom-call | tf_op jit(solution)/shard_map/sort_rows/pallas_call | solution.py:368
  31.2 2.2 %collective-permute-start = (bf16[8,1536]{1,0:T(8,128)(2,1)}, bf16[8,1536]{1,0:T(8,128)(2,1)S(1)}, u32[]{:S(2)}, u32[]{:S(2)}) collective-permute-start(bf16[8,1536]{1,0:T(8,128)(2,1)} %get-tuple-element.15), channel_id=1, source_target_pairs={{0,1},{1,2},{2,3},{3,4},{4,5},{5,6},{6,7},{7,8},{8,9},{9,10},{10,1... | collective-permute-start | bytes 73736 | tf_op jit(solution)/shard_map/ppermute | solution.py:379
  33.4 4.6 %collective-permute-start.1 = (bf16[8,1536]{1,0:T(8,128)(2,1)}, bf16[8,1536]{1,0:T(8,128)(2,1)S(1)}, u32[]{:S(2)}, u32[]{:S(2)}) collective-permute-start(bf16[8,1536]{1,0:T(8,128)(2,1)} %get-tuple-element.16), channel_id=1, source_target_pairs={{1,0},{2,1},{3,2},{4,3},{5,4},{6,5},{7,6},{8,7},{9,8},{10,9},{11,1... | collective-permute-start | bytes 73736 | tf_op jit(solution)/shard_map/ppermute | solution.py:380
  38.0 0.7 add_convert_fusion.flags
  38.6 0.5 collective-permute-done.1.after
  39.1 0.1 copy-done.3
  39.2 0.5 copy-done.4
  39.7 27.2 %block_states.1 = (bf16[2,128,3072]{2,1,0:T(8,128)(2,1)}, f32[2,128,128]{2,1,0:T(8,128)}, f32[2,128,3072]{2,1,0:T(8,128)}, f32[2,16,8,3072]{3,2,1,0:T(8,128)}, bf16[2,8,8,4,384]{4,3,2,1,0:T(4,128)(2,1)}) custom-call(s32[2]{0:T(128)} %add_convert_fusion.flags, bf16[128,1536]{1,0:T(8,128)(2,1)} %get-tuple-element.14.rows_in, bf16[8,1536]{1,0:T(8,128)(2,1)} %copy-done.3, ...), custom_call_target="tpu_custom_call" | custom-call | tf_op jit(solution)/shard_map/block_states/pallas_call | solution.py:388
  66.9 11.1 %all-to-all-start.1 = ((bf16[128,4,384]{2,1,0:T(4,128)(2,1)}), bf16[128,4,384]{2,1,0:T(4,128)(2,1)S(1)}, u32[]{:S(2)}, u32[]{:S(2)}) async-start(bf16[128,4,384]{2,1,0:T(4,128)(2,1)} %bitcast.9), calls=%async_computation.1 | async-start | bytes 786432 | tf_op jit(solution)/shard_map/all_to_all | solution.py:432
  78.1 0.5 concatenate.6.keep
  78.6 1.4 dynamic-slice_bitcast_fusion.rates
  80.0 10.7 %all-to-all-done.1.payload = bf16[128,4,384]{2,1,0:T(4,128)(2,1)S(1)} async-done(((bf16[128,4,384]{2,1,0:T(4,128)(2,1)}), bf16[128,4,384]{2,1,0:T(4,128)(2,1)S(1)}, u32[]{:S(2)}, u32[]{:S(2)}) %all-to-all-start.1) | async-done | bytes 393248 | tf_op jit(solution)/shard_map/all_to_all | solution.py:432
  90.7 0.7 copy-done
  91.4 3.4 %relay.1 = bf16[128,2,384]{2,1,0:T(2,128)(2,1)} custom-call(s32[136]{0:T(256)} %concatenate.6.keep, bf16[128,4,384]{2,1,0:T(4,128)(2,1)} %copy-done, f32[2,384]{1,0:T(2,128)} %dynamic-slice_bitcast_fusion.rates), custom_call_target="tpu_custom_call" | custom-call | tf_op jit(solution)/shard_map/relay/pallas_call | solution.py:435
  94.8 15.2 %all_to_all.20 = bf16[128,2,384]{2,1,0:T(2,128)(2,1)} all-to-all(bf16[128,2,384]{2,1,0:T(2,128)(2,1)} %relay.1), channel_id=1, replica_groups=mesh['seq'=32,'slide'=4] {'seq','slide'}, dimensions={0} | all-to-all | bytes 393216 | tf_op jit(solution)/shard_map/all_to_all | solution.py:447
  110.0 20.2 %block_outputs.1 = bf16[256,1536]{1,0:T(8,128)(2,1)} custom-call(bf16[2,8,8,2,384]{4,3,2,1,0:T(2,128)(2,1)} %bitcast.8, f32[2,16,8,3072]{3,2,1,0:T(8,128)} %get-tuple-element.18.inner_states, f32[2,128,3072]{2,1,0:T(8,128)} %get-tuple-element.19.dt_in, bf16[2,128,3072]{2,1,0:T(8,128)(2,1)} %get-tuple-element.20.u_in, f32[2,128,128]{2,1,0:T(8,128)} %get-tuple-element.21.proj, ...), custom_call_target="tpu_custom_call" | custom-call | tf_op jit(solution)/shard_map/block_outputs/pallas_call | solution.py:451
  130.3 2.9 %reshape.38 = bf16[128,2,1536]{2,1,0:T(2,128)(2,1)} reshape(bf16[256,1536]{1,0:T(8,128)(2,1)} %block_outputs.1) | data formatting | bytes 1572864 | tf_op jit(solution)/shard_map/reshape | solution.py:477
  133.2 4.2 %all-to-all-start.3 = ((bf16[128,2,1536]{2,1,0:T(2,128)(2,1)}), bf16[128,2,1536]{2,1,0:T(2,128)(2,1)S(1)}, u32[]{:S(2)}, u32[]{:S(2)}) async-start(bf16[128,2,1536]{2,1,0:T(2,128)(2,1)} %reshape.38), calls=%async_computation.3 | async-start | bytes 1572864 | tf_op jit(solution)/shard_map/all_to_all | solution.py:476
  137.4 6.3 %divide_multiply_fusion.gate = f32[128,3072]{1,0:T(8,128)} fusion(bf16[128,1536]{1,0:T(8,128)(2,1)S(1)} %copy-done.2, bf16[1536,3072]{1,0:T(8,128)(2,1)} %param.16), kind=kOutput, calls=%fused_computation | convolution fusion | flops 1209532416 | bytes 11403264 | tf_op jit(solution)/shard_map/dot_general | solution.py:366
  143.8 10.4 %all-to-all-done.3 = bf16[128,2,1536]{2,1,0:T(2,128)(2,1)S(1)} async-done(((bf16[128,2,1536]{2,1,0:T(2,128)(2,1)}), bf16[128,2,1536]{2,1,0:T(2,128)(2,1)S(1)}, u32[]{:S(2)}, u32[]{:S(2)}) %all-to-all-start.3) | async-done | bytes 786464 | tf_op jit(solution)/shard_map/all_to_all | solution.py:476
  154.2 1.2 reshape.39.returned
  155.4 2.9 %gated.1 = bf16[128,3072]{1,0:T(8,128)(2,1)} custom-call(bf16[256,1536]{1,0:T(8,128)(2,1)} %reshape.39.returned, f32[128,3072]{1,0:T(8,128)} %divide_multiply_fusion.gate), custom_call_target="tpu_custom_call" | custom-call | tf_op jit(solution)/shard_map/gated/pallas_call | solution.py:479
  (14 shorter events, 0.1 us)
Async XLA Ops:
  0.0 14.8 %copy-start.5 = (s32[4]{0:T(128)S(1)}, s32[4]{0:T(128)}, u32[]{:S(2)}) copy-start(s32[4]{0:T(128)} %param.14) | copy-start | bytes 52
  0.0 16.9 %copy-start.1 = (f32[2,16,3072]{2,1,0:T(8,128)S(1)}, f32[2,16,3072]{2,1,0:T(8,128)}, u32[]{:S(2)}) copy-start(f32[2,16,3072]{2,1,0:T(8,128)} %param.22) | copy-start | bytes 1179652
  3.2 24.8 %all-to-all-start = ((bf16[128,2,896]{2,1,0:T(2,128)(2,1)}), bf16[128,2,896]{2,1,0:T(2,128)(2,1)S(1)}, u32[]{:S(2)}, u32[]{:S(2)}) async-start(bf16[128,2,896]{2,1,0:T(2,128)(2,1)} %pad_maximum_fusion), calls=%async_computation | async-start | bytes 917504 | tf_op jit(solution)/shard_map/all_to_all | solution.py:363
  31.2 7.4 %collective-permute-start = (bf16[8,1536]{1,0:T(8,128)(2,1)}, bf16[8,1536]{1,0:T(8,128)(2,1)S(1)}, u32[]{:S(2)}, u32[]{:S(2)}) collective-permute-start(bf16[8,1536]{1,0:T(8,128)(2,1)} %get-tuple-element.15), channel_id=1, source_target_pairs={{0,1},{1,2},{2,3},{3,4},{4,5},{5,6},{6,7},{7,8},{8,9},{9,10},{10,1... | collective-permute-start | bytes 73736 | tf_op jit(solution)/shard_map/ppermute | solution.py:379
  33.4 5.7 %collective-permute-start.1 = (bf16[8,1536]{1,0:T(8,128)(2,1)}, bf16[8,1536]{1,0:T(8,128)(2,1)S(1)}, u32[]{:S(2)}, u32[]{:S(2)}) collective-permute-start(bf16[8,1536]{1,0:T(8,128)(2,1)} %get-tuple-element.16), channel_id=1, source_target_pairs={{1,0},{2,1},{3,2},{4,3},{5,4},{6,5},{7,6},{8,7},{9,8},{10,9},{11,1... | collective-permute-start | bytes 73736 | tf_op jit(solution)/shard_map/ppermute | solution.py:380
  38.6 0.6 copy-start.3
  39.1 0.6 copy-start.4
  66.9 23.8 %all-to-all-start.1 = ((bf16[128,4,384]{2,1,0:T(4,128)(2,1)}), bf16[128,4,384]{2,1,0:T(4,128)(2,1)S(1)}, u32[]{:S(2)}, u32[]{:S(2)}) async-start(bf16[128,4,384]{2,1,0:T(4,128)(2,1)} %bitcast.9), calls=%async_computation.1 | async-start | bytes 786432 | tf_op jit(solution)/shard_map/all_to_all | solution.py:432
  90.7 0.7 copy-start
  130.3 7.2 %copy-start.2 = (bf16[128,1536]{1,0:T(8,128)(2,1)S(1)}, bf16[128,1536]{1,0:T(8,128)(2,1)}, u32[]{:S(2)}) copy-start(bf16[128,1536]{1,0:T(8,128)(2,1)} %param.12) | copy-start | bytes 1179652
  133.2 21.0 %all-to-all-start.3 = ((bf16[128,2,1536]{2,1,0:T(2,128)(2,1)}), bf16[128,2,1536]{2,1,0:T(2,128)(2,1)S(1)}, u32[]{:S(2)}, u32[]{:S(2)}) async-start(bf16[128,2,1536]{2,1,0:T(2,128)(2,1)} %reshape.38), calls=%async_computation.3 | async-start | bytes 1572864 | tf_op jit(solution)/shard_map/all_to_all | solution.py:476

commit v2 on v1

v2 whole, which is shorter than its diff:
```python
import functools

import jax
import jax.numpy as jnp
from jax import lax
from jax.experimental import pallas as pl
from jax.experimental.pallas import tpu as pltpu
from jax.sharding import PartitionSpec as P

AXES = ("seq", "slide")
SUB = 8
LANES = 128
LOG2E = 1.4426950408889634


def spread_index(rows, turned=False):
    shape = (rows, rows)
    row = lax.broadcasted_iota(jnp.int32, shape, 1 if turned else 0)
    col = lax.broadcasted_iota(jnp.int32, shape, 0 if turned else 1)
    group = rows // SUB
    hit = (row // SUB == col % group) & (row % SUB == col // group)
    return hit.astype(jnp.float32).astype(jnp.bfloat16)


def as_bf16(product):
    return product.astype(jnp.bfloat16)


def matmul(left, right):
    return jnp.dot(left, right, preferred_element_type=jnp.float32)


def over_rows(left, right):
    return lax.dot_general(
        left, right, (((0,), (0,)), ((), ())), preferred_element_type=jnp.float32
    )


def chunked(pieces, out):
    rows = pieces[0].shape[0]
    group = rows // SUB
    spread = spread_index(rows)
    blank = [jnp.zeros_like(pieces[0])] * (SUB - len(pieces))
    for q in range(SUB):
        part = [piece[group * q : group * q + group] for piece in list(pieces) + blank]
        out[rows * q : rows * q + rows] = as_bf16(matmul(spread, jnp.concatenate(part, axis=0)))


def pack_kernel(embed, destination, out):
    rows = embed.shape[0]
    width = out.shape[1]
    pieces = [embed[:, at : at + width] for at in range(0, embed.shape[1], width)]
    row = lax.broadcasted_iota(jnp.int32, (rows, rows), 0)
    col = lax.broadcasted_iota(jnp.int32, (rows, rows), 1)
    offset = jnp.where(row == col, destination[...] - rows * col, 0)
    offset = as_bf16(offset.astype(jnp.float32))
    pieces.append(as_bf16(matmul(offset, jnp.ones((rows, width), jnp.bfloat16))))
    chunked(pieces, out)


def row_positions(shape, per_sub):
    lane = lax.broadcasted_iota(jnp.int32, shape, 1)
    return (lane % SUB) * per_sub + lane // SUB


def one_hot(pos):
    place = row_positions(pos.shape, pos.shape[1] // SUB)
    hit = pos.astype(jnp.int32) == place
    return hit.astype(jnp.float32).astype(jnp.bfloat16)


def sort_kernel(arrived, sorted_rows, ahead, behind, places, plain):
    rows = sorted_rows.shape[0]
    group = rows // SUB
    width = arrived.shape[1]
    pieces = sorted_rows.shape[1] // width
    gather = spread_index(rows, turned=True)
    for q in range(SUB):
        part = as_bf16(matmul(gather, arrived[rows * q : rows * q + rows]))
        for k in range(pieces + 1):
            plain[group * q : group * q + group, width * k : width * k + width] = part[
                group * k : group * k + group
            ]
    pos = plain[:, width * pieces : width * pieces + LANES].astype(jnp.float32)
    places[...] = pos
    lane = lax.broadcasted_iota(jnp.int32, pos.shape, 1)
    edge = jnp.where(lane < SUB, lane + rows - 3, lane - SUB)
    edge = jnp.where((lane % SUB < 3) & (lane < 2 * SUB), edge, -1)
    hit = (pos.astype(jnp.int32) == edge).astype(jnp.float32).astype(jnp.bfloat16)
    data = plain[:, : width * pieces]
    ends = as_bf16(over_rows(hit, data))
    ahead[...] = ends[:SUB]
    behind[...] = ends[SUB : 2 * SUB]
    sorted_rows[...] = as_bf16(over_rows(one_hot(pos), data))


def inner_kernel(rows_in, weight, x_project, dt_project, out, weight_here, x_here, dt_here, sems):
    parts = sems.shape[0] - 2
    width = weight.shape[1] // parts
    copies = []
    for k in range(parts):
        cols = pl.ds(k * width, width)
        copies.append((weight.at[:, cols], weight_here.at[:, cols]))
    copies += [(x_project, x_here), (dt_project, dt_here)]
    copies = [
        pltpu.make_async_copy(here, there, sems.at[k]) for k, (here, there) in enumerate(copies)
    ]
    for copy in copies:
        copy.start()
    for k in range(parts):
        cols = pl.ds(k * width, width)
        copies[k].wait()
        out[:, cols] = as_bf16(matmul(rows_in[...], weight_here[:, cols]))
    copies[parts].wait()
    copies[parts + 1].wait()


def sublane(shape):
    return lax.broadcasted_iota(jnp.int32, shape, 0)


def shift_sublanes(tile, count, reverse):
    return pltpu.roll(tile, SUB - count if reverse else count, 0)


def in_reach(count, reverse):
    row = sublane((SUB, LANES))
    return row < SUB - count if reverse else row >= count


def outside(total, reverse):
    for count in (1, 2, 4):
        moved = shift_sublanes(total, count, reverse)
        total = total + jnp.where(in_reach(count, reverse), moved, 0.0)
    return jnp.where(in_reach(1, reverse), shift_sublanes(total, 1, reverse), 0.0)


def tiles_of(array):
    return [array[SUB * t : SUB * t + SUB] for t in range(array.shape[0] // SUB)]


def in_order(count, reverse):
    return list(range(count))[::-1] if reverse else list(range(count))


def spread_columns(target, columns, first, count):
    for n in range(count):
        target[n] = jnp.broadcast_to(
            columns[:, first + n : first + n + 1], (columns.shape[0], LANES)
        )


def silu(v):
    return v / (1.0 + jnp.exp(-v))


def softplus(v):
    return jnp.maximum(v, 0.0) + jnp.log(1.0 + jnp.exp(-jnp.abs(v)))


def states_kernel(
    flags,
    inner_in,
    before,
    after,
    w_inner,
    conv_weight,
    conv_bias,
    x_project,
    dt_project,
    dt_bias,
    rates,
    u_result,
    proj_result,
    dt_result,
    payload_result,
    u_out,
    proj_out,
    dt_out,
    b_wide,
    payload,
    edge_rows,
    extended,
    sems,
):
    copies = [
        pltpu.make_async_copy(here, there, sems.at[k])
        for k, (here, there) in enumerate(
            (
                (u_out, u_result),
                (proj_out, proj_result),
                (dt_out, dt_result),
                (payload.at[0], payload_result.at[0]),
                (payload.at[1], payload_result.at[1]),
            )
        )
    ]
    rows, channels = inner_in.shape
    taps = conv_weight.shape[1]
    reach = taps - 1
    width = extended.shape[1]
    states = rates.shape[1]
    rank = dt_project.shape[1]
    slots = rows // SUB
    tile = payload.shape[4]
    edge_rows[:SUB] = before[...]
    edge_rows[SUB:] = after[...]
    proj_out[...] = jnp.zeros_like(proj_out)

    def conv_block(step, carry):
        cols = pl.ds(pl.multiple_of(step * width, LANES), width)
        edges = as_bf16(matmul(edge_rows[...], w_inner[:, cols])).astype(jnp.float32)
        main = inner_in[:, cols].astype(jnp.float32)
        prior = edges[:SUB] * flags[0].astype(jnp.float32)
        later = edges[SUB:] * flags[1].astype(jnp.float32)
        row = sublane((SUB, width))
        extended[SUB * reach : SUB * reach + rows] = main
        for k in range(reach):
            own = main[rows - SUB * (reach - k) : rows - SUB * (reach - k - 1)]
            extended[SUB * k : SUB * k + SUB] = jnp.where(
                row == 0, prior[k : k + 1], pltpu.roll(own, 1, 0)
            )
            own = main[SUB * k : SUB * k + SUB]
            base = SUB * (reach + slots + k)
            extended[base : base + SUB] = jnp.where(
                row == SUB - 1, later[k : k + 1], pltpu.roll(own, SUB - 1, 0)
            )
        for d in range(2):
            mixed = conv_bias[d : d + 1, cols]
            for tap in range(taps):
                base = SUB * (2 * reach - tap if d else tap)
                gain = conv_weight[d, tap : tap + 1, cols]
                mixed = mixed + gain * extended[base : base + rows]
            u = as_bf16(silu(mixed))
            u_out[d, :, cols] = u
            proj_out[d] += matmul(u, x_project[d, cols, :])
        return carry

    lax.fori_loop(0, channels // width, conv_block, 0)
    copies[0].start()
    copies[1].start()
    for d in range(2):
        spread_columns(b_wide.at[d], proj_out[d], rank, states)

    def step_block(step, carry):
        cols = pl.ds(pl.multiple_of(step * width, LANES), width)
        for d in range(2):
            low = as_bf16(proj_out[d][:, :rank])
            raw = matmul(low, dt_project[d, :, cols])
            dt_out[d, :, cols] = softplus(raw + dt_bias[d : d + 1, cols])
        return carry

    lax.fori_loop(0, channels // width, step_block, 0)
    copies[2].start()
    row = sublane((SUB, LANES))

    def state_block(block, carry, d):
        here = pl.ds(pl.multiple_of(block * LANES, LANES), LANES)
        group = block // (tile // LANES)
        within = pl.multiple_of((block - group * (tile // LANES)) * LANES, LANES)
        reverse = d == 1
        dt = dt_out[d, :, here]
        fed = tiles_of(dt * u_out[d, :, here].astype(jnp.float32))
        dt = tiles_of(dt)
        order = in_order(slots, not reverse)
        rest = {order[0]: None}
        total = dt[order[0]]
        for t in order[1:]:
            rest[t] = total
            total = total + dt[t]
        outer = outside(total, not reverse)
        whole = total + outer
        whole = whole[SUB - 1 : SUB] if reverse else whole[0:1]
        rest = {t: outer if part is None else part + outer for t, part in rest.items()}
        finals = []
        for n in range(states):
            rate = rates[d, n : n + 1, here]
            state = None
            for t in order:
                new = fed[t] * b_wide[d, n, SUB * t : SUB * t + SUB]
                new = jnp.exp2(rest[t] * rate) * new
                state = new if state is None else state + new
            finals.append(jnp.sum(state, axis=0, keepdims=True))
        for n in range(0, states, 2):
            out = jnp.where(row == 0, finals[n], finals[n + 1])
            out = jnp.where(row >= 2, whole, out)
            payload[d, n // 2, group, :, pl.ds(within, LANES)] = as_bf16(out[:4])
        return carry

    for d in range(2):
        lax.fori_loop(0, channels // LANES, functools.partial(state_block, d=d), 0)
        copies[3 + d].start()
    for copy in copies:
        copy.wait()


def local_kernel(dt_in, u_in, proj, rates, skip_gain, y_out, entry_out, b_wide, c_wide, *, reverse):
    d = int(reverse)
    states = rates.shape[1]
    rows, channels = y_out.shape
    slots = rows // SUB
    rank = proj.shape[2] - 2 * states

    @pl.when(pl.program_id(0) == 0)
    def _():
        spread_columns(b_wide, proj[0], rank, states)
        spread_columns(c_wide, proj[0], rank + states, states)

    def lane_block(block, carry):
        here = pl.ds(pl.multiple_of(block * LANES, LANES), LANES)
        dt = dt_in[0, :, here]
        u = u_in[0, :, here].astype(jnp.float32)
        fed = tiles_of(dt * u)
        dt = tiles_of(dt)
        gain = skip_gain[d : d + 1, here]
        sums = [gain * tile for tile in tiles_of(u)]
        total = dt[0]
        for t in range(1, slots):
            total = total + dt[t]
        for n in range(states):
            rate = rates[0, n : n + 1, here]
            state = None
            for t in in_order(slots, reverse):
                at = slice(SUB * t, SUB * t + SUB)
                new = fed[t] * b_wide[n, at]
                if state is not None:
                    new = jnp.exp2(dt[t] * rate) * state + new
                state = new
                sums[t] = sums[t] + c_wide[n, at] * state
            keep = jnp.exp2(total * rate)
            for count in (1, 2, 4):
                keep = jnp.where(in_reach(count, reverse), keep, 0.0)
                state = state + keep * shift_sublanes(state, count, reverse)
                if count < 4:
                    keep = keep * shift_sublanes(keep, count, reverse)
            near = in_reach(1, reverse)
            entry_out[n, :, here] = jnp.where(near, shift_sublanes(state, 1, reverse), 0.0)
        for t in range(slots):
            y_out[SUB * t : SUB * t + SUB, here] = sums[t]
        return carry

    lax.fori_loop(0, channels // LANES, lane_block, 0)


def relay_kernel(keep, payload, rates, entering):
    blocks = payload.shape[0]
    backward = keep[blocks]

    def block_step(i, state):
        at = jnp.where(backward == 1, blocks - 1 - i, i)
        state = state * keep[at].astype(jnp.float32)
        entering[at] = state.astype(jnp.bfloat16)
        row = payload[at].astype(jnp.float32)
        return jnp.exp2(rates[...] * row[2:3]) * state + row[0:2]

    lax.fori_loop(0, blocks, block_step, jnp.zeros(rates.shape, jnp.float32), unroll=16)


def outputs_kernel(
    entering,
    entry_fwd,
    entry_bwd,
    y_fwd,
    y_bwd,
    dt_in,
    proj,
    rates,
    places,
    out,
    c_wide,
    mixed,
    placed,
):
    step = pl.program_id(0)
    states = rates.shape[1]
    rows, channels = y_fwd.shape
    slots = rows // SUB
    rank = proj.shape[2] - 2 * states

    @pl.when(step == 0)
    def _():
        for d in range(2):
            spread_columns(c_wide.at[d], proj[d], rank + states, states)

    def lane_block(block, carry, d, entry):
        here = pl.ds(pl.multiple_of(block * LANES, LANES), LANES)
        reverse = d == 1
        sums = tiles_of(mixed[:, here] if reverse else y_fwd[:, here] + y_bwd[:, here])
        dt = tiles_of(dt_in[d, :, here])
        order = in_order(slots, reverse)
        past = {}
        total = None
        for t in order:
            total = dt[t] if total is None else total + dt[t]
            past[t] = total
        ahead = outside(total, reverse)
        for n in range(states):
            rate = rates[d, n : n + 1, here]
            pair = entering[d, n // 2, 0, :, here].astype(jnp.float32)
            state = jnp.exp2(ahead * rate) * pair[n % 2 : n % 2 + 1] + entry[n, :, here]
            for t in order:
                at = slice(SUB * t, SUB * t + SUB)
                decayed = jnp.exp2(past[t] * rate)
                sums[t] = sums[t] + decayed * (c_wide[d, n, at] * state)
        for t in range(slots):
            mixed[SUB * t : SUB * t + SUB, here] = sums[t]
        return carry

    for d, entry in ((0, entry_fwd), (1, entry_bwd)):
        lax.fori_loop(0, channels // LANES, functools.partial(lane_block, d=d, entry=entry), 0)
    placed[step] = as_bf16(matmul(one_hot(places[...]), as_bf16(mixed[...])))

    @pl.when(step == pl.num_programs(0) - 1)
    def _():
        chunked([placed[k] for k in range(SUB)], out)


def gate_kernel(returned, gate, out):
    rows = out.shape[0]
    group = rows // SUB
    width = returned.shape[1]
    gather = spread_index(rows, turned=True)
    for q in range(SUB):
        part = matmul(gather, returned[rows * q : rows * q + rows])
        here = slice(group * q, group * q + group)
        for k in range(SUB):
            cols = slice(width * k, width * k + width)
            out[here, cols] = as_bf16(part[group * k : group * k + group] * gate[here, cols])


def limits(mebibytes):
    return pltpu.CompilerParams(vmem_limit_bytes=mebibytes * 1024 * 1024)


def in_vmem(array):
    return pltpu.with_memory_space_constraint(array, pltpu.VMEM)


def in_hbm(array):
    return pltpu.with_memory_space_constraint(array, pltpu.HBM)


def on_chip(kernel, name, mebibytes, results, *operands, scalars=0, scratch=()):
    places = [pltpu.SMEM] * scalars + [pltpu.VMEM] * (len(operands) - scalars)
    one = pl.BlockSpec(memory_space=pltpu.VMEM)
    return pl.pallas_call(
        kernel,
        out_shape=results,
        in_specs=[pl.BlockSpec(memory_space=place) for place in places],
        out_specs=tuple(one for _ in results) if isinstance(results, tuple) else one,
        scratch_shapes=list(scratch),
        compiler_params=limits(mebibytes),
        name=name,
    )(
        *(
            in_vmem(operand) if place is pltpu.VMEM else operand
            for operand, place in zip(operands, places)
        )
    )


def local(
    tile_embed,
    destination,
    slide_lengths,
    w_inner,
    w_gate,
    conv_weight,
    conv_bias,
    x_project,
    dt_project,
    dt_bias,
    decay,
    skip_gain,
):
    f32, bf16 = jnp.float32, jnp.bfloat16
    shards = lax.axis_size(AXES)
    me = lax.axis_index(AXES)
    rows, model = tile_embed.shape
    width = w_inner.shape[1]
    states = decay.shape[1]
    rank = dt_project.shape[1]
    taps = conv_weight.shape[1]
    tile = 3 * LANES
    groups = width // tile
    owner_states = 2 * groups * states // shards
    state_groups = states // owner_states
    slots = rows // SUB

    blocks = jnp.arange(shards, dtype=jnp.int32)
    slide = jnp.arange(slide_lengths.shape[0], dtype=jnp.int32)
    ends = jnp.sum(jnp.where(slide[:, None] <= slide[None, :], slide_lengths[:, None], 0), axis=0)
    starts = ends - slide_lengths
    opens = jnp.any(blocks[:, None] * rows == starts[None, :], axis=1)
    closes = jnp.any((blocks[:, None] + 1) * rows == ends[None, :], axis=1)
    mine = blocks == me
    flags = jnp.stack([~jnp.any(opens & mine), ~jnp.any(closes & mine)]).astype(jnp.int32)
    owner_dir = me // (state_groups * groups)
    owner_group = (me // groups) % state_groups
    owner_tile = me % groups
    keep = jnp.where(owner_dir == 1, ~closes, ~opens).astype(jnp.int32)
    keep = jnp.concatenate([keep, jnp.full((SUB,), owner_dir, jnp.int32)])
    rates = decay * (-LOG2E)
    owner_rates = lax.dynamic_slice(
        rates, (owner_dir, owner_group * owner_states, owner_tile * tile), (1, owner_states, tile)
    )[0]

    piece = 2 * LANES
    sent = on_chip(
        pack_kernel, "pack", 3, pltpu.VMEM((SUB * rows, piece), bf16), tile_embed, destination[None, :]
    )
    arrived = lax.all_to_all(
        sent.reshape(rows, SUB, piece), AXES, split_axis=0, concat_axis=0, tiled=True
    ).reshape(SUB * rows, piece)
    gate = jax.nn.silu(jnp.dot(tile_embed, w_gate, preferred_element_type=f32))

    block_rows, ahead, behind, places = on_chip(
        sort_kernel,
        "sort_rows",
        4,
        (
            pltpu.VMEM((rows, model), bf16),
            pltpu.VMEM((SUB, model), bf16),
            pltpu.VMEM((SUB, model), bf16),
            pltpu.HBM((rows, LANES), f32),
        ),
        arrived,
        scratch=[pltpu.VMEM((rows, model + piece), bf16)],
    )
    before = lax.ppermute(ahead, AXES, [(i, i + 1) for i in range(shards - 1)])
    after = lax.ppermute(behind, AXES, [(i + 1, i) for i in range(shards - 1)])
    hbm_spec = pl.BlockSpec(memory_space=pltpu.HBM)
    vmem_spec = pl.BlockSpec(memory_space=pltpu.VMEM)
    weights = (w_inner, x_project, dt_project)
    inner, w_inner, x_project, dt_project = pl.pallas_call(
        inner_kernel,
        out_shape=(
            pltpu.VMEM((rows, width), bf16),
            *(pltpu.VMEM(w.shape, w.dtype) for w in weights),
        ),
        in_specs=[vmem_spec] + [hbm_spec] * 3,
        out_specs=(vmem_spec,) * 4,
        scratch_shapes=[pltpu.SemaphoreType.DMA((6,))],
        compiler_params=limits(2),
        name="inner",
    )(in_vmem(block_rows), *(in_hbm(w) for w in weights))

    operands = (
        inner, before, after, w_inner, conv_weight, conv_bias, x_project, dt_project, dt_bias, rates,
    )
    on_chip_results = [
        pltpu.VMEM((2, rows, width), bf16),
        pltpu.VMEM((2, rows, LANES), f32),
        pltpu.VMEM((2, rows, width), f32),
        pltpu.VMEM((2, states, rows, LANES), f32),
        pltpu.VMEM((2, state_groups, groups, 4, tile), bf16),
    ]
    u, proj, dt, payload = pl.pallas_call(
        states_kernel,
        out_shape=(
            pltpu.HBM((2, rows, width), bf16),
            pltpu.HBM((2, rows, LANES), f32),
            pltpu.HBM((2, rows, width), f32),
            pltpu.HBM((2, state_groups, groups, 4, tile), bf16),
        ),
        in_specs=[pl.BlockSpec(memory_space=pltpu.SMEM)] + [vmem_spec] * len(operands),
        out_specs=(hbm_spec,) * 4,
        scratch_shapes=on_chip_results
        + [
            pltpu.VMEM((2 * SUB, model), bf16),
            pltpu.VMEM((rows + 2 * SUB * (taps - 1), 2 * tile), f32),
            pltpu.SemaphoreType.DMA((5,)),
        ],
        compiler_params=limits(14),
        name="block_states",
    )(flags, *(in_vmem(operand) for operand in operands))

    def local_outputs(d):
        return pl.pallas_call(
            functools.partial(local_kernel, reverse=d == 1),
            out_shape=(
                pltpu.HBM((rows, width), f32),
                pltpu.HBM((states, SUB, width), f32),
            ),
            grid=(groups,),
            in_specs=[
                pl.BlockSpec((1, rows, tile), lambda i: (d, 0, i)),
                pl.BlockSpec((1, rows, tile), lambda i: (d, 0, i)),
                pl.BlockSpec((1, rows, LANES), lambda i: (d, 0, 0)),
                pl.BlockSpec((1, states, tile), lambda i: (d, 0, i)),
                pl.BlockSpec((2, tile), lambda i: (0, i)),
            ],
            out_specs=[
                pl.BlockSpec((rows, tile), lambda i: (0, i)),
                pl.BlockSpec((states, SUB, tile), lambda i: (0, 0, i)),
            ],
            scratch_shapes=[pltpu.VMEM((states, rows, LANES), f32)] * 2,
            compiler_params=limits(6),
            name="local_bwd_outputs" if d else "local_fwd_outputs",
        )(in_hbm(dt), in_hbm(u), in_hbm(proj), rates, skip_gain)

    local_fwd = local_outputs(0)
    local_bwd = local_outputs(1)

    shared = lax.all_to_all(
        payload.reshape(shards, 4, tile), AXES, split_axis=0, concat_axis=0, tiled=True
    )
    shared, *local_fwd = lax.optimization_barrier((shared, *local_fwd))
    entering = on_chip(
        relay_kernel,
        "relay",
        2,
        pltpu.VMEM((shards, owner_states, tile), bf16),
        keep, shared, owner_rates,
        scalars=1,
    )
    entering = lax.all_to_all(entering, AXES, split_axis=0, concat_axis=0, tiled=True)
    entering, *local_bwd = lax.optimization_barrier((entering, *local_bwd))
    entering = entering.reshape(2, state_groups, groups, owner_states, tile)
    y_fwd, entry_fwd = local_fwd
    y_bwd, entry_bwd = local_bwd

    totals = pl.pallas_call(
        outputs_kernel,
        out_shape=pltpu.HBM((SUB * rows, tile), bf16),
        grid=(groups,),
        in_specs=[
            pl.BlockSpec((2, state_groups, 1, owner_states, tile), lambda i: (0, 0, i, 0, 0)),
            pl.BlockSpec((states, SUB, tile), lambda i: (0, 0, i)),
            pl.BlockSpec((states, SUB, tile), lambda i: (0, 0, i)),
            pl.BlockSpec((rows, tile), lambda i: (0, i)),
            pl.BlockSpec((rows, tile), lambda i: (0, i)),
            pl.BlockSpec((2, rows, tile), lambda i: (0, 0, i)),
            pl.BlockSpec((2, rows, LANES), lambda i: (0, 0, 0)),
            pl.BlockSpec((2, states, tile), lambda i: (0, 0, i)),
            pl.BlockSpec((rows, LANES), lambda i: (0, 0)),
        ],
        out_specs=pl.BlockSpec((SUB * rows, tile), lambda i: (0, 0)),
        scratch_shapes=[
            pltpu.VMEM((2, states, rows, LANES), f32),
            pltpu.VMEM((rows, tile), f32),
            pltpu.VMEM((groups, rows, tile), bf16),
        ],
        compiler_params=limits(12),
        name="block_outputs",
    )(
        in_vmem(entering),
        *(in_hbm(array) for array in (entry_fwd, entry_bwd, y_fwd, y_bwd, dt, proj)),
        rates,
        in_hbm(places),
    )

    returned = lax.all_to_all(
        totals.reshape(rows, SUB, tile), AXES, split_axis=0, concat_axis=0, tiled=True
    ).reshape(SUB * rows, tile)
    return pl.pallas_call(
        gate_kernel,
        out_shape=jax.ShapeDtypeStruct((rows, width), bf16),
        compiler_params=limits(5),
        name="gated",
    )(in_vmem(returned), gate)


def solution(mesh):
    placed = (P(AXES, None), P(AXES)) + (P(),) * 10
    return jax.shard_map(
        local, mesh=mesh, in_specs=placed, out_specs=P(AXES, None), check_vma=False
    )
```

time: 159 us -> 143 us (0.90)
  blocking collectives: 15.2 us -> 0 us
  starting transfers between devices: 33.6 us -> 43.2 us
  Pallas kernels: 56 us -> 64.7 us
  local copies, waits for them, and re-layouts: 9.66 us -> 1.78 us
  waiting for transfers between devices: 31.9 us -> 25.3 us
  other arithmetic: 4.18 us -> 0.97 us
    all_to_all x1 -> x0, blocking collectives: 15.2 us -> none  [local(): lax.all_to_all(entering, AXES, split_axis=0, concat_axis=0, tiled=True)]
    all_to_all x2 -> x3, starting transfers between devices: 15.7 us -> 29.1 us  [the longest x1 11.5 us: local(): lax.all_to_all(sent.reshape(rows, SUB, piece), AXES, split_axis=0, concat...]
    pallas_call x4 -> x8, Pallas kernels: 53.1 us -> 63.5 us  [the longest x2 21.3 us: local_outputs(): pl.pallas_call(functools.partial(local_kernel, reverse=d == 1), out_shape...]
    all_to_all x1, waiting for transfers between devices: 10.7 us -> 1.83 us  [local(): lax.all_to_all(payload.reshape(shards, 4, tile), AXES, split_axis=0, conc...]
    reshape x4 -> x0, local copies, waits for them, and re-layouts: 6.19 us -> none  [the longest x1 2.91 us: local(): totals.reshape(rows, 2, width // 2)]
    all_to_all x1, starting transfers between devices: 11.1 us -> 7.3 us  [local(): lax.all_to_all(payload.reshape(shards, 4, tile), AXES, split_axis=0, conc...]
    all_to_all x2 -> x3, waiting for transfers between devices: 20.8 us -> 23.5 us  [the longest x1 11.8 us: local(): lax.all_to_all(sent.reshape(rows, SUB, piece), AXES, split_axis=0, concat...]
    pallas_call x1, Pallas kernels: 2.92 us -> 1.25 us  [local(): pl.pallas_call(gate_kernel, out_shape=jax.ShapeDtypeStruct((rows, width),...]
  transfers between devices with their start and end apart: 5 -> 6, of which waited for: 4 -> 4; matrix products, arithmetic and copies ran while one was open for 7% -> 4% of each run, Pallas kernels for 0% -> 18%
where the time goes in v2:
time: 143 us
  Pallas kernels  64.7 us (45%)
  starting transfers between devices  43.2 us (30%)
  waiting for transfers between devices  25.3 us (18%)
  matrix products  5.17 us (4%)
  local copies, waits for them, and re-layouts  1.78 us (1%)
  between operations  1.48 us (1%)
    pallas_call x2, Pallas kernels, local_outputs(): pl.pallas_call(functools.partial(local_kernel, reverse=d == 1), out_shape...  21.3 us
    pallas_call x1, Pallas kernels, local(): pl.pallas_call(states_kernel, out_shape=(pltpu.HBM((2, rows, width), bf16...  18.3 us
    pallas_call x1, Pallas kernels, local(): pl.pallas_call(outputs_kernel, out_shape=pltpu.HBM((SUB * rows, tile), bf...  15.3 us
    all_to_all x1, waiting for transfers between devices, local(): lax.all_to_all(sent.reshape(rows, SUB, piece), AXES, split_axis=0, concat...  11.8 us
    all_to_all x1, waiting for transfers between devices, local(): lax.all_to_all(totals.reshape(rows, SUB, tile), AXES, split_axis=0, conca...  11.6 us
    all_to_all x1, starting transfers between devices, local(): lax.all_to_all(sent.reshape(rows, SUB, piece), AXES, split_axis=0, concat...  11.5 us
    all_to_all x1, starting transfers between devices, local(): lax.all_to_all(totals.reshape(rows, SUB, tile), AXES, split_axis=0, conca...  9.71 us
    all_to_all x1, starting transfers between devices, local(): lax.all_to_all(entering, AXES, split_axis=0, concat_axis=0, tiled=True)  7.93 us
  transfers between devices with their start and end apart: 6, of which 4 were waited for; matrix products, arithmetic and copies ran while one was open for 4% of the time, Pallas kernels for 18%

profile of v2, /device:TPU:1, one launch (start us, length us, event | category | flops | bytes accessed | tf_op | source)
XLA Modules:
  0.0 142.6 jit_solution(8512458314438523087)
XLA Ops:
  0.0 1.0 copy-done
  1.0 0.7 copy-done.6
  1.7 1.2 pack.1
  2.9 11.5 %all-to-all-start = ((bf16[128,8,256]{2,1,0:T(8,128)(2,1)}), bf16[128,8,256]{2,1,0:T(8,128)(2,1)S(1)}, u32[]{:S(2)}, u32[]{:S(2)}) async-start(bf16[128,8,256]{2,1,0:T(8,128)(2,1)} %bitcast.3), calls=%async_computation | async-start | bytes 1048576 | tf_op jit(solution)/shard_map/all_to_all | solution.py:512
  14.4 0.0 copy-done.8
  14.5 0.1 select_reduce_fusion
  14.5 0.1 compare_reduce_fusion
  14.6 0.7 and_reduce_fusion.1
  16.5 0.0 copy-done.7
  16.6 11.8 %all-to-all-done = bf16[128,8,256]{2,1,0:T(8,128)(2,1)S(1)} async-done(((bf16[128,8,256]{2,1,0:T(8,128)(2,1)}), bf16[128,8,256]{2,1,0:T(8,128)(2,1)S(1)}, u32[]{:S(2)}, u32[]{:S(2)}) %all-to-all-start) | async-done | bytes 524320 | tf_op jit(solution)/shard_map/all_to_all | solution.py:512
  28.4 0.9 sort_rows.1
  29.3 2.2 %collective-permute-start = (bf16[8,1536]{1,0:T(8,128)(2,1)S(1)}, bf16[8,1536]{1,0:T(8,128)(2,1)S(1)}, u32[]{:S(2)}, u32[]{:S(2)}) collective-permute-start(bf16[8,1536]{1,0:T(8,128)(2,1)S(1)} %get-tuple-element.29), channel_id=1, source_target_pairs={{0,1},{1,2},{2,3},{3,4},{4,5},{5,6},{6,7},{7,8},{8,9},{9,10},{10,1... | collective-permute-start | bytes 73736 | tf_op jit(solution)/shard_map/ppermute | solution.py:530
  31.5 4.6 %collective-permute-start.1 = (bf16[8,1536]{1,0:T(8,128)(2,1)S(1)}, bf16[8,1536]{1,0:T(8,128)(2,1)S(1)}, u32[]{:S(2)}, u32[]{:S(2)}) collective-permute-start(bf16[8,1536]{1,0:T(8,128)(2,1)S(1)} %get-tuple-element.30), channel_id=1, source_target_pairs={{1,0},{2,1},{3,2},{4,3},{5,4},{6,5},{7,6},{8,7},{9,8},{10,9},{11,1... | collective-permute-start | bytes 73736 | tf_op jit(solution)/shard_map/ppermute | solution.py:531
  36.1 0.1 add_convert_fusion.flags
  36.1 4.6 %inner.1 = (bf16[128,3072]{1,0:T(8,128)(2,1)S(1)}, bf16[1536,3072]{1,0:T(8,128)(2,1)S(1)}, bf16[2,3072,128]{2,1,0:T(8,128)(2,1)S(1)}, bf16[2,96,3072]{2,1,0:T(8,128)(2,1)S(1)}) custom-call(bf16[128,1536]{1,0:T(8,128)(2,1)S(1)} %get-tuple-element.27.rows_in, bf16[1536,3072]{1,0:T(8,128)(2,1)} %weight.1, bf16[2,3072,128]{2,1,0:T(8,128)(2,1)} %x_project.1, ...), custom_call_target="tpu_custom_call" | custom-call | tf_op jit(solution)/shard_map/inner/pallas_call | solution.py:535
  40.8 0.0 collective-permute-done.before
  40.8 0.0 collective-permute-done.1.after
  40.8 0.0 copy-start.3
  40.8 18.3 %block_states.1 = (bf16[2,128,3072]{2,1,0:T(8,128)(2,1)}, f32[2,128,128]{2,1,0:T(8,128)}, f32[2,128,3072]{2,1,0:T(8,128)}, bf16[2,8,8,4,384]{4,3,2,1,0:T(4,128)(2,1)}) custom-call(s32[2]{0:T(128)S(1)} %add_convert_fusion.flags, bf16[128,3072]{1,0:T(8,128)(2,1)S(1)} %get-tuple-element.28.inner_in, bf16[8,1536]{1,0:T(8,128)(2,1)S(1)} %collective-permute-done.before, ...), custom_call_target="tpu_custom_call" | custom-call | tf_op jit(solution)/shard_map/block_states/pallas_call | solution.py:558
  59.1 7.3 %all-to-all-start.1 = ((bf16[128,4,384]{2,1,0:T(4,128)(2,1)}), bf16[128,4,384]{2,1,0:T(4,128)(2,1)S(1)}, u32[]{:S(2)}, u32[]{:S(2)}) async-start(bf16[128,4,384]{2,1,0:T(4,128)(2,1)} %bitcast.18), calls=%async_computation.1 | async-start | bytes 786432 | tf_op jit(solution)/shard_map/all_to_all | solution.py:605
  66.5 0.1 dynamic-slice_bitcast_fusion.rates
  66.6 10.6 %local_fwd_outputs.1 = (f32[128,3072]{1,0:T(8,128)}, f32[16,8,3072]{2,1,0:T(8,128)}) custom-call(f32[2,128,3072]{2,1,0:T(8,128)} %get-tuple-element.35.dt_in, bf16[2,128,3072]{2,1,0:T(8,128)(2,1)} %get-tuple-element.36.u_in, f32[2,128,128]{2,1,0:T(8,128)} %get-tuple-element.37.proj, f32[2,16,3072]{2,1,0:T(8,128)S(1)} %broadcast_multiply_fusion.rates, ...), custom_call_target="tpu_custom_call" | custom-call | tf_op jit(solution)/shard_map/local_fwd_outputs/pallas_call | solution.py:579
  77.2 1.8 %all-to-all-done.1.payload = bf16[128,4,384]{2,1,0:T(4,128)(2,1)S(1)} async-done(((bf16[128,4,384]{2,1,0:T(4,128)(2,1)}), bf16[128,4,384]{2,1,0:T(4,128)(2,1)S(1)}, u32[]{:S(2)}, u32[]{:S(2)}) %all-to-all-start.1) | async-done | bytes 393248 | tf_op jit(solution)/shard_map/all_to_all | solution.py:605
  79.0 1.8 %relay.1 = bf16[128,2,384]{2,1,0:T(2,128)(2,1)} custom-call(s32[136]{0:T(256)S(1)} %concatenate.3.keep, bf16[128,4,384]{2,1,0:T(4,128)(2,1)S(1)} %all-to-all-done.1.payload, f32[2,384]{1,0:T(2,128)S(1)} %dynamic-slice_bitcast_fusion.rates), custom_call_target="tpu_custom_call" | custom-call | tf_op jit(solution)/shard_map/relay/pallas_call | solution.py:446
  80.9 7.9 %all-to-all-start.2 = ((bf16[128,2,384]{2,1,0:T(2,128)(2,1)}), bf16[128,2,384]{2,1,0:T(2,128)(2,1)S(1)}, u32[]{:S(2)}, u32[]{:S(2)}) async-start(bf16[128,2,384]{2,1,0:T(2,128)(2,1)} %relay.1), calls=%async_computation.2 | async-start | bytes 393216 | tf_op jit(solution)/shard_map/all_to_all | solution.py:617
  88.8 10.6 %local_bwd_outputs.1 = (f32[128,3072]{1,0:T(8,128)}, f32[16,8,3072]{2,1,0:T(8,128)}) custom-call(f32[2,128,3072]{2,1,0:T(8,128)} %get-tuple-element.35.dt_in, bf16[2,128,3072]{2,1,0:T(8,128)(2,1)} %get-tuple-element.36.u_in, f32[2,128,128]{2,1,0:T(8,128)} %get-tuple-element.37.proj, f32[2,16,3072]{2,1,0:T(8,128)S(1)} %broadcast_multiply_fusion.rates, ...), custom_call_target="tpu_custom_call" | custom-call | tf_op jit(solution)/shard_map/local_bwd_outputs/pallas_call | solution.py:579
  99.5 0.1 all-to-all-done.2
  99.5 15.3 %block_outputs.1 = bf16[1024,384]{1,0:T(8,128)(2,1)} custom-call(bf16[2,8,8,2,384]{4,3,2,1,0:T(2,128)(2,1)S(1)} %bitcast.15, f32[16,8,3072]{2,1,0:T(8,128)} %get-tuple-element.44.entry_fwd, f32[16,8,3072]{2,1,0:T(8,128)} %get-tuple-element.45.entry_bwd, f32[128,3072]{1,0:T(8,128)} %get-tuple-element.46.y_fwd, f32[128,3072]{1,0:T(8,128)} %get-tuple-element.47.y_bwd, ...), custom_call_target="tpu_custom_call" | custom-call | tf_op jit(solution)/shard_map/block_outputs/pallas_call | solution.py:623
  114.9 9.7 %all-to-all-start.3 = ((bf16[128,8,384]{2,1,0:T(8,128)(2,1)}), bf16[128,8,384]{2,1,0:T(8,128)(2,1)S(1)}, u32[]{:S(2)}, u32[]{:S(2)}) async-start(bf16[128,8,384]{2,1,0:T(8,128)(2,1)} %bitcast.17), calls=%async_computation.3 | async-start | bytes 1572864 | tf_op jit(solution)/shard_map/all_to_all | solution.py:653
  124.6 5.2 %divide_multiply_fusion.gate = f32[128,3072]{1,0:T(8,128)S(1)} fusion(bf16[128,1536]{1,0:T(8,128)(2,1)S(1)} %copy-done.1, bf16[1536,3072]{1,0:T(8,128)(2,1)} %param.16), kind=kOutput, calls=%fused_computation | convolution fusion | flops 1209532416 | bytes 11403264 | tf_op jit(solution)/shard_map/dot_general | solution.py:515
  129.8 11.6 %all-to-all-done.3 = bf16[128,8,384]{2,1,0:T(8,128)(2,1)S(1)} async-done(((bf16[128,8,384]{2,1,0:T(8,128)(2,1)}), bf16[128,8,384]{2,1,0:T(8,128)(2,1)S(1)}, u32[]{:S(2)}, u32[]{:S(2)}) %all-to-all-start.3) | async-done | bytes 786464 | tf_op jit(solution)/shard_map/all_to_all | solution.py:653
  141.4 1.2 gated.1
  (18 shorter events, 0.1 us)
Async XLA Ops:
  0.0 14.4 %copy-start.8 = (s32[4]{0:T(128)S(1)}, s32[4]{0:T(128)}, u32[]{:S(2)}) copy-start(s32[4]{0:T(128)} %param.14) | copy-start | bytes 52
  0.0 1.0 copy-start
  1.0 0.7 copy-start.6
  1.7 14.8 %copy-start.7 = (f32[2,16,3072]{2,1,0:T(8,128)S(1)}, f32[2,16,3072]{2,1,0:T(8,128)}, u32[]{:S(2)}) copy-start(f32[2,16,3072]{2,1,0:T(8,128)} %param.22) | copy-start | bytes 1179652
  2.9 25.5 %all-to-all-start = ((bf16[128,8,256]{2,1,0:T(8,128)(2,1)}), bf16[128,8,256]{2,1,0:T(8,128)(2,1)S(1)}, u32[]{:S(2)}, u32[]{:S(2)}) async-start(bf16[128,8,256]{2,1,0:T(8,128)(2,1)} %bitcast.3), calls=%async_computation | async-start | bytes 1048576 | tf_op jit(solution)/shard_map/all_to_all | solution.py:512
  29.3 11.5 %collective-permute-start = (bf16[8,1536]{1,0:T(8,128)(2,1)S(1)}, bf16[8,1536]{1,0:T(8,128)(2,1)S(1)}, u32[]{:S(2)}, u32[]{:S(2)}) collective-permute-start(bf16[8,1536]{1,0:T(8,128)(2,1)S(1)} %get-tuple-element.29), channel_id=1, source_target_pairs={{0,1},{1,2},{2,3},{3,4},{4,5},{5,6},{6,7},{7,8},{8,9},{9,10},{10,1... | collective-permute-start | bytes 73736 | tf_op jit(solution)/shard_map/ppermute | solution.py:530
  31.5 9.3 %collective-permute-start.1 = (bf16[8,1536]{1,0:T(8,128)(2,1)S(1)}, bf16[8,1536]{1,0:T(8,128)(2,1)S(1)}, u32[]{:S(2)}, u32[]{:S(2)}) collective-permute-start(bf16[8,1536]{1,0:T(8,128)(2,1)S(1)} %get-tuple-element.30), channel_id=1, source_target_pairs={{1,0},{2,1},{3,2},{4,3},{5,4},{6,5},{7,6},{8,7},{9,8},{10,9},{11,1... | collective-permute-start | bytes 73736 | tf_op jit(solution)/shard_map/ppermute | solution.py:531
  36.1 4.7 %copy-start.2 = (f32[2,4,3072]{2,1,0:T(4,128)S(1)}, f32[2,4,3072]{2,1,0:T(4,128)}, u32[]{:S(2)}) copy-start(f32[2,4,3072]{2,1,0:T(4,128)} %conv_weight.1) | copy-start | bytes 294916
  36.1 4.7 %copy-start.4 = (f32[2,3072]{1,0:T(2,128)S(1)}, f32[2,3072]{1,0:T(2,128)}, u32[]{:S(2)}) copy-start(f32[2,3072]{1,0:T(2,128)} %conv_bias.1) | copy-start | bytes 73732
  36.1 4.7 %copy-start.5 = (f32[2,3072]{1,0:T(2,128)S(1)}, f32[2,3072]{1,0:T(2,128)}, u32[]{:S(2)}) copy-start(f32[2,3072]{1,0:T(2,128)} %dt_bias.1) | copy-start | bytes 73732
  40.8 25.7 %copy-start.3 = (f32[2,3072]{1,0:T(2,128)S(1)}, f32[2,3072]{1,0:T(2,128)}, u32[]{:S(2)}) copy-start(f32[2,3072]{1,0:T(2,128)} %skip_gain.3) | copy-start | bytes 73732
  59.1 19.9 %all-to-all-start.1 = ((bf16[128,4,384]{2,1,0:T(4,128)(2,1)}), bf16[128,4,384]{2,1,0:T(4,128)(2,1)S(1)}, u32[]{:S(2)}, u32[]{:S(2)}) async-start(bf16[128,4,384]{2,1,0:T(4,128)(2,1)} %bitcast.18), calls=%async_computation.1 | async-start | bytes 786432 | tf_op jit(solution)/shard_map/all_to_all | solution.py:605
  80.9 18.7 %all-to-all-start.2 = ((bf16[128,2,384]{2,1,0:T(2,128)(2,1)}), bf16[128,2,384]{2,1,0:T(2,128)(2,1)S(1)}, u32[]{:S(2)}, u32[]{:S(2)}) async-start(bf16[128,2,384]{2,1,0:T(2,128)(2,1)} %relay.1), calls=%async_computation.2 | async-start | bytes 393216 | tf_op jit(solution)/shard_map/all_to_all | solution.py:617
  114.9 9.7 %copy-start.1 = (bf16[128,1536]{1,0:T(8,128)(2,1)S(1)}, bf16[128,1536]{1,0:T(8,128)(2,1)}, u32[]{:S(2)}) copy-start(bf16[128,1536]{1,0:T(8,128)(2,1)} %embed.1) | copy-start | bytes 1179652
  114.9 26.5 %all-to-all-start.3 = ((bf16[128,8,384]{2,1,0:T(8,128)(2,1)}), bf16[128,8,384]{2,1,0:T(8,128)(2,1)S(1)}, u32[]{:S(2)}, u32[]{:S(2)}) async-start(bf16[128,8,384]{2,1,0:T(8,128)(2,1)} %bitcast.17), calls=%async_computation.3 | async-start | bytes 1572864 | tf_op jit(solution)/shard_map/all_to_all | solution.py:653

commit v3 on v2

--- a/solution.py
+++ b/solution.py
@@ -10,6 +10,7 @@
 AXES = ("seq", "slide")
 SUB = 8
 LANES = 128
+PACK = 16
 LOG2E = 1.4426950408889634
 
 
@@ -151,7 +152,55 @@
 
 
 def silu(v):
-    return v / (1.0 + jnp.exp(-v))
+    half = 0.5 * v
+    return half + half * jnp.tanh(half)
+
+
+def halves(array):
+    high = as_bf16(array)
+    return high, as_bf16(array - high.astype(jnp.float32))
+
+
+def sum_over_positions(columns, first, states):
+    rows = columns.shape[0]
+    size = (rows, rows * states)
+    row = lax.broadcasted_iota(jnp.int32, size, 0)
+    at = lax.broadcasted_iota(jnp.int32, size, 1)
+    repeat = row == at // (PACK * states) * PACK + at % PACK
+    repeat = repeat.astype(jnp.float32).astype(jnp.bfloat16)
+    size = (states, rows * states)
+    own = lax.broadcasted_iota(jnp.int32, size, 1) // PACK % states == sublane(size)
+    parts = [
+        as_bf16(jnp.where(own, matmul(part, repeat), 0.0))
+        for part in halves(columns.T[first : first + states])
+    ]
+    return jnp.concatenate(parts, axis=0)
+
+
+def in_fours(rows):
+    count = rows.shape[0]
+    size = (2 * count, count)
+    out_row = sublane(size)
+    wanted = out_row // 4 * 2 + out_row % 4
+    pick = (wanted == lax.broadcasted_iota(jnp.int32, size, 1)) & (out_row % 4 < 2)
+    return matmul(pick.astype(jnp.float32).astype(jnp.bfloat16), as_bf16(rows))
+
+
+def paired(first, second):
+    return as_bf16(jnp.concatenate([first, second], axis=0))
+
+
+def sum_over_states(columns, first, states):
+    rows = columns.shape[0]
+    size = (columns.shape[1], PACK * states)
+    col = lax.broadcasted_iota(jnp.int32, size, 0)
+    at = lax.broadcasted_iota(jnp.int32, size, 1)
+    repeat = (col == first + at // PACK).astype(jnp.float32).astype(jnp.bfloat16)
+    size = (rows, PACK * states)
+    row = lax.broadcasted_iota(jnp.int32, size, 0)
+    at = lax.broadcasted_iota(jnp.int32, size, 1)
+    own = row % PACK == at % PACK
+    return [as_bf16(jnp.where(own, matmul(part, repeat), 0.0)) for part in halves(columns)]
 
 
 def softplus(v):
@@ -177,8 +226,8 @@
     u_out,
     proj_out,
     dt_out,
-    b_wide,
     payload,
+    left,
     edge_rows,
     extended,
     sems,
@@ -240,7 +289,7 @@
     copies[0].start()
     copies[1].start()
     for d in range(2):
-        spread_columns(b_wide.at[d], proj_out[d], rank, states)
+        left[d] = sum_over_positions(proj_out[d], rank, states)
 
     def step_block(step, carry):
         cols = pl.ds(pl.multiple_of(step * width, LANES), width)
@@ -252,12 +301,42 @@
 
     lax.fori_loop(0, channels // width, step_block, 0)
     copies[2].start()
-    row = sublane((SUB, LANES))
-
-    def state_block(block, carry, d):
-        here = pl.ds(pl.multiple_of(block * LANES, LANES), LANES)
-        group = block // (tile // LANES)
-        within = pl.multiple_of((block - group * (tile // LANES)) * LANES, LANES)
+    def state_block(turn, carry):
+        for pair in range(2):
+            for d in range(2):
+                first = turn * 4 + pair * 2
+                sides = [
+                    spans(pl.ds(pl.multiple_of((first + side) * LANES, LANES), LANES), d)
+                    for side in range(2)
+                ]
+                out = None
+                for k in range(slots // 2):
+                    right = []
+                    for n in range(states):
+                        piece = []
+                        for here, fed, rest, _ in sides:
+                            rate = rates[d, n : n + 1, here]
+                            piece.append(
+                                paired(*(jnp.exp2(rest[t] * rate) * fed[t] for t in (2 * k, 2 * k + 1)))
+                            )
+                        right.append(jnp.concatenate(piece, axis=1))
+                    size = PACK * states
+                    part = matmul(
+                        left[d, :, size * k : size * k + size], jnp.concatenate(right, axis=0)
+                    )
+                    out = part if out is None else out + part
+                out = in_fours(out[:states] + out[states:])
+                for side in range(2):
+                    block = first + side
+                    group = block // (tile // LANES)
+                    within = pl.multiple_of((block - group * (tile // LANES)) * LANES, LANES)
+                    for k in range(states // 2):
+                        rows4 = out[4 * k : 4 * k + 4, side * LANES : side * LANES + LANES]
+                        rows4 = jnp.where(sublane((4, LANES)) < 2, rows4, sides[side][3])
+                        payload[d, k, group, :, pl.ds(within, LANES)] = as_bf16(rows4)
+        return carry
+
+    def spans(here, d):
         reverse = d == 1
         dt = dt_out[d, :, here]
         fed = tiles_of(dt * u_out[d, :, here].astype(jnp.float32))
@@ -272,24 +351,11 @@
         whole = total + outer
         whole = whole[SUB - 1 : SUB] if reverse else whole[0:1]
         rest = {t: outer if part is None else part + outer for t, part in rest.items()}
-        finals = []
-        for n in range(states):
-            rate = rates[d, n : n + 1, here]
-            state = None
-            for t in order:
-                new = fed[t] * b_wide[d, n, SUB * t : SUB * t + SUB]
-                new = jnp.exp2(rest[t] * rate) * new
-                state = new if state is None else state + new
-            finals.append(jnp.sum(state, axis=0, keepdims=True))
-        for n in range(0, states, 2):
-            out = jnp.where(row == 0, finals[n], finals[n + 1])
-            out = jnp.where(row >= 2, whole, out)
-            payload[d, n // 2, group, :, pl.ds(within, LANES)] = as_bf16(out[:4])
-        return carry
-
-    for d in range(2):
-        lax.fori_loop(0, channels // LANES, functools.partial(state_block, d=d), 0)
-        copies[3 + d].start()
+        return here, fed, rest, whole
+
+    lax.fori_loop(0, channels // (4 * LANES), state_block, 0)
+    copies[3].start()
+    copies[4].start()
     for copy in copies:
         copy.wait()
 
@@ -367,8 +433,7 @@
     rates,
     places,
     out,
-    c_wide,
-    mixed,
+    left,
     placed,
 ):
     step = pl.program_id(0)
@@ -376,43 +441,62 @@
     rows, channels = y_fwd.shape
     slots = rows // SUB
     rank = proj.shape[2] - 2 * states
+    tile = entering.shape[4]
 
     @pl.when(step == 0)
     def _():
         for d in range(2):
-            spread_columns(c_wide.at[d], proj[d], rank + states, states)
-
-    def lane_block(block, carry, d, entry):
-        here = pl.ds(pl.multiple_of(block * LANES, LANES), LANES)
+            parts = sum_over_states(proj[d], rank + states, states)
+            for k in range(slots // 2):
+                for i, part in enumerate(parts):
+                    left[d, k, PACK * i : PACK * i + PACK] = part[PACK * k : PACK * k + PACK]
+
+    def spans(at, d, entry):
+        here = slice(at * LANES, at * LANES + LANES)
+        block = step * (channels // LANES) + at
+        group = block // (tile // LANES)
+        within = pl.multiple_of((block - group * (tile // LANES)) * LANES, LANES)
         reverse = d == 1
-        sums = tiles_of(mixed[:, here] if reverse else y_fwd[:, here] + y_bwd[:, here])
         dt = tiles_of(dt_in[d, :, here])
-        order = in_order(slots, reverse)
         past = {}
         total = None
-        for t in order:
+        for t in in_order(slots, reverse):
             total = dt[t] if total is None else total + dt[t]
             past[t] = total
         ahead = outside(total, reverse)
+        entered = []
         for n in range(states):
             rate = rates[d, n : n + 1, here]
-            pair = entering[d, n // 2, 0, :, here].astype(jnp.float32)
-            state = jnp.exp2(ahead * rate) * pair[n % 2 : n % 2 + 1] + entry[n, :, here]
-            for t in order:
-                at = slice(SUB * t, SUB * t + SUB)
-                decayed = jnp.exp2(past[t] * rate)
-                sums[t] = sums[t] + decayed * (c_wide[d, n, at] * state)
-        for t in range(slots):
-            mixed[SUB * t : SUB * t + SUB, here] = sums[t]
-        return carry
-
-    for d, entry in ((0, entry_fwd), (1, entry_bwd)):
-        lax.fori_loop(0, channels // LANES, functools.partial(lane_block, d=d, entry=entry), 0)
-    placed[step] = as_bf16(matmul(one_hot(places[...]), as_bf16(mixed[...])))
+            pair = entering[d, n // 2, group, :, pl.ds(within, LANES)].astype(jnp.float32)
+            entered.append(jnp.exp2(ahead * rate) * pair[n % 2 : n % 2 + 1] + entry[n, :, here])
+        return here, past, entered
+
+    pick = one_hot(places[...])
+    for pair in range(channels // LANES // 2):
+        cols = slice(pair * 2 * LANES, (pair + 1) * 2 * LANES)
+        sums = y_fwd[:, cols] + y_bwd[:, cols]
+        for d, entry in ((0, entry_fwd), (1, entry_bwd)):
+            sides = [spans(2 * pair + side, d, entry) for side in range(2)]
+            parts = []
+            for k in range(slots // 2):
+                right = []
+                for n in range(states):
+                    piece = []
+                    for here, past, entered in sides:
+                        rate = rates[d, n : n + 1, here]
+                        piece.append(
+                            paired(*(jnp.exp2(past[t] * rate) * entered[n] for t in (2 * k, 2 * k + 1)))
+                        )
+                    right.append(jnp.concatenate(piece, axis=1))
+                part = matmul(left[d, k], jnp.concatenate(right, axis=0))
+                parts.append(part[:PACK] + part[PACK:])
+            sums = sums + jnp.concatenate(parts, axis=0)
+        start = pl.multiple_of(step * channels + pair * 2 * LANES, 2 * LANES)
+        placed[:, pl.ds(start, 2 * LANES)] = as_bf16(matmul(pick, as_bf16(sums)))
 
     @pl.when(step == pl.num_programs(0) - 1)
     def _():
-        chunked([placed[k] for k in range(SUB)], out)
+        chunked([placed[:, tile * k : tile * k + tile] for k in range(SUB)], out)
 
 
 def gate_kernel(returned, gate, out):
@@ -552,8 +636,8 @@
         pltpu.VMEM((2, rows, width), bf16),
         pltpu.VMEM((2, rows, LANES), f32),
         pltpu.VMEM((2, rows, width), f32),
-        pltpu.VMEM((2, states, rows, LANES), f32),
         pltpu.VMEM((2, state_groups, groups, 4, tile), bf16),
+        pltpu.VMEM((2, 2 * states, rows * states), bf16),
     ]
     u, proj, dt, payload = pl.pallas_call(
         states_kernel,
@@ -620,26 +704,26 @@
     y_fwd, entry_fwd = local_fwd
     y_bwd, entry_bwd = local_bwd
 
+    part = 4 * LANES
     totals = pl.pallas_call(
         outputs_kernel,
         out_shape=pltpu.HBM((SUB * rows, tile), bf16),
-        grid=(groups,),
+        grid=(width // part,),
         in_specs=[
-            pl.BlockSpec((2, state_groups, 1, owner_states, tile), lambda i: (0, 0, i, 0, 0)),
-            pl.BlockSpec((states, SUB, tile), lambda i: (0, 0, i)),
-            pl.BlockSpec((states, SUB, tile), lambda i: (0, 0, i)),
-            pl.BlockSpec((rows, tile), lambda i: (0, i)),
-            pl.BlockSpec((rows, tile), lambda i: (0, i)),
-            pl.BlockSpec((2, rows, tile), lambda i: (0, 0, i)),
+            vmem_spec,
+            pl.BlockSpec((states, SUB, part), lambda i: (0, 0, i)),
+            pl.BlockSpec((states, SUB, part), lambda i: (0, 0, i)),
+            pl.BlockSpec((rows, part), lambda i: (0, i)),
+            pl.BlockSpec((rows, part), lambda i: (0, i)),
+            pl.BlockSpec((2, rows, part), lambda i: (0, 0, i)),
             pl.BlockSpec((2, rows, LANES), lambda i: (0, 0, 0)),
-            pl.BlockSpec((2, states, tile), lambda i: (0, 0, i)),
+            pl.BlockSpec((2, states, part), lambda i: (0, 0, i)),
             pl.BlockSpec((rows, LANES), lambda i: (0, 0)),
         ],
         out_specs=pl.BlockSpec((SUB * rows, tile), lambda i: (0, 0)),
         scratch_shapes=[
-            pltpu.VMEM((2, states, rows, LANES), f32),
-            pltpu.VMEM((rows, tile), f32),
-            pltpu.VMEM((groups, rows, tile), bf16),
+            pltpu.VMEM((2, slots // 2, 2 * PACK, PACK * states), bf16),
+            pltpu.VMEM((rows, width), bf16),
         ],
         compiler_params=limits(12),
         name="block_outputs",

time: 143 us -> 139 us (0.972)
  Pallas kernels: 64.7 us -> 60.5 us
    pallas_call x1, Pallas kernels: 15.3 us -> 12.4 us  [local(): pl.pallas_call(outputs_kernel, out_shape=pltpu.HBM((SUB * rows, tile), bf...]
  transfers between devices with their start and end apart: 6 -> 6, of which waited for: 4 -> 4; matrix products, arithmetic and copies ran while one was open for 4% -> 4% of each run, Pallas kernels for 18% -> 19%
where the time goes in v3:
time: 139 us; the launch traced here: 138 us
  Pallas kernels  60.5 us (44%)
  starting transfers between devices  43.2 us (31%)
  waiting for transfers between devices  25.3 us (18%)
  matrix products  5.16 us (4%)
  local copies, waits for them, and re-layouts  1.78 us (1%)
  between operations  1.48 us (1%)
    pallas_call x2, Pallas kernels, local_outputs(): pl.pallas_call(functools.partial(local_kernel, reverse=d == 1), out_shape...  21.3 us
    pallas_call x1, Pallas kernels, local(): pl.pallas_call(states_kernel, out_shape=(pltpu.HBM((2, rows, width), bf16...  17 us
    pallas_call x1, Pallas kernels, local(): pl.pallas_call(outputs_kernel, out_shape=pltpu.HBM((SUB * rows, tile), bf...  12.4 us
    all_to_all x1, waiting for transfers between devices, local(): lax.all_to_all(sent.reshape(rows, SUB, piece), AXES, split_axis=0, concat...  11.8 us
    all_to_all x1, waiting for transfers between devices, local(): lax.all_to_all(totals.reshape(rows, SUB, tile), AXES, split_axis=0, conca...  11.6 us
    all_to_all x1, starting transfers between devices, local(): lax.all_to_all(sent.reshape(rows, SUB, piece), AXES, split_axis=0, concat...  11.5 us
    all_to_all x1, starting transfers between devices, local(): lax.all_to_all(totals.reshape(rows, SUB, tile), AXES, split_axis=0, conca...  9.7 us
    all_to_all x1, starting transfers between devices, local(): lax.all_to_all(entering, AXES, split_axis=0, concat_axis=0, tiled=True)  7.93 us
  transfers between devices with their start and end apart: 6, of which 4 were waited for; matrix products, arithmetic and copies ran while one was open for 4% of the time, Pallas kernels for 19%

profile of v3, /device:TPU:1, one launch (start us, length us, event | category | flops | bytes accessed | tf_op | source)
XLA Modules:
  0.0 138.4 jit_solution(3831392282678125428)
XLA Ops:
  0.0 1.0 copy-done
  1.0 0.7 copy-done.6
  1.7 1.2 pack.1
  2.9 11.5 %all-to-all-start = ((bf16[128,8,256]{2,1,0:T(8,128)(2,1)}), bf16[128,8,256]{2,1,0:T(8,128)(2,1)S(1)}, u32[]{:S(2)}, u32[]{:S(2)}) async-start(bf16[128,8,256]{2,1,0:T(8,128)(2,1)} %bitcast.3), calls=%async_computation | async-start | bytes 1048576 | tf_op jit(solution)/shard_map/all_to_all | solution.py:596
  14.4 0.0 copy-done.8
  14.5 0.1 select_reduce_fusion
  14.5 0.1 compare_reduce_fusion
  14.6 0.7 and_reduce_fusion.1
  16.5 0.0 copy-done.7
  16.6 11.8 %all-to-all-done = bf16[128,8,256]{2,1,0:T(8,128)(2,1)S(1)} async-done(((bf16[128,8,256]{2,1,0:T(8,128)(2,1)}), bf16[128,8,256]{2,1,0:T(8,128)(2,1)S(1)}, u32[]{:S(2)}, u32[]{:S(2)}) %all-to-all-start) | async-done | bytes 524320 | tf_op jit(solution)/shard_map/all_to_all | solution.py:596
  28.4 0.9 sort_rows.1
  29.3 2.2 %collective-permute-start = (bf16[8,1536]{1,0:T(8,128)(2,1)S(1)}, bf16[8,1536]{1,0:T(8,128)(2,1)S(1)}, u32[]{:S(2)}, u32[]{:S(2)}) collective-permute-start(bf16[8,1536]{1,0:T(8,128)(2,1)S(1)} %get-tuple-element.29), channel_id=1, source_target_pairs={{0,1},{1,2},{2,3},{3,4},{4,5},{5,6},{6,7},{7,8},{8,9},{9,10},{10,1... | collective-permute-start | bytes 73736 | tf_op jit(solution)/shard_map/ppermute | solution.py:614
  31.5 4.6 %collective-permute-start.1 = (bf16[8,1536]{1,0:T(8,128)(2,1)S(1)}, bf16[8,1536]{1,0:T(8,128)(2,1)S(1)}, u32[]{:S(2)}, u32[]{:S(2)}) collective-permute-start(bf16[8,1536]{1,0:T(8,128)(2,1)S(1)} %get-tuple-element.30), channel_id=1, source_target_pairs={{1,0},{2,1},{3,2},{4,3},{5,4},{6,5},{7,6},{8,7},{9,8},{10,9},{11,1... | collective-permute-start | bytes 73736 | tf_op jit(solution)/shard_map/ppermute | solution.py:615
  36.1 0.1 add_convert_fusion.flags
  36.1 4.6 %inner.1 = (bf16[128,3072]{1,0:T(8,128)(2,1)S(1)}, bf16[1536,3072]{1,0:T(8,128)(2,1)S(1)}, bf16[2,3072,128]{2,1,0:T(8,128)(2,1)S(1)}, bf16[2,96,3072]{2,1,0:T(8,128)(2,1)S(1)}) custom-call(bf16[128,1536]{1,0:T(8,128)(2,1)S(1)} %get-tuple-element.27.rows_in, bf16[1536,3072]{1,0:T(8,128)(2,1)} %weight.1, bf16[2,3072,128]{2,1,0:T(8,128)(2,1)} %x_project.1, ...), custom_call_target="tpu_custom_call" | custom-call | tf_op jit(solution)/shard_map/inner/pallas_call | solution.py:619
  40.8 0.0 collective-permute-done.before
  40.8 0.0 collective-permute-done.1.after
  40.8 0.0 copy-start.3
  40.8 17.0 %block_states.1 = (bf16[2,128,3072]{2,1,0:T(8,128)(2,1)}, f32[2,128,128]{2,1,0:T(8,128)}, f32[2,128,3072]{2,1,0:T(8,128)}, bf16[2,8,8,4,384]{4,3,2,1,0:T(4,128)(2,1)}) custom-call(s32[2]{0:T(128)S(1)} %add_convert_fusion.flags, bf16[128,3072]{1,0:T(8,128)(2,1)S(1)} %get-tuple-element.28.inner_in, bf16[8,1536]{1,0:T(8,128)(2,1)S(1)} %collective-permute-done.before, ...), custom_call_target="tpu_custom_call" | custom-call | tf_op jit(solution)/shard_map/block_states/pallas_call | solution.py:642
  57.8 7.3 %all-to-all-start.1 = ((bf16[128,4,384]{2,1,0:T(4,128)(2,1)}), bf16[128,4,384]{2,1,0:T(4,128)(2,1)S(1)}, u32[]{:S(2)}, u32[]{:S(2)}) async-start(bf16[128,4,384]{2,1,0:T(4,128)(2,1)} %bitcast.18), calls=%async_computation.1 | async-start | bytes 786432 | tf_op jit(solution)/shard_map/all_to_all | solution.py:689
  65.2 0.1 dynamic-slice_bitcast_fusion.rates
  65.3 10.6 %local_fwd_outputs.1 = (f32[128,3072]{1,0:T(8,128)}, f32[16,8,3072]{2,1,0:T(8,128)}) custom-call(f32[2,128,3072]{2,1,0:T(8,128)} %get-tuple-element.35.dt_in, bf16[2,128,3072]{2,1,0:T(8,128)(2,1)} %get-tuple-element.36.u_in, f32[2,128,128]{2,1,0:T(8,128)} %get-tuple-element.37.proj, f32[2,16,3072]{2,1,0:T(8,128)S(1)} %broadcast_multiply_fusion.rates, ...), custom_call_target="tpu_custom_call" | custom-call | tf_op jit(solution)/shard_map/local_fwd_outputs/pallas_call | solution.py:663
  75.9 1.8 %all-to-all-done.1.payload = bf16[128,4,384]{2,1,0:T(4,128)(2,1)S(1)} async-done(((bf16[128,4,384]{2,1,0:T(4,128)(2,1)}), bf16[128,4,384]{2,1,0:T(4,128)(2,1)S(1)}, u32[]{:S(2)}, u32[]{:S(2)}) %all-to-all-start.1) | async-done | bytes 393248 | tf_op jit(solution)/shard_map/all_to_all | solution.py:689
  77.8 1.8 %relay.1 = bf16[128,2,384]{2,1,0:T(2,128)(2,1)} custom-call(s32[136]{0:T(256)S(1)} %concatenate.3.keep, bf16[128,4,384]{2,1,0:T(4,128)(2,1)S(1)} %all-to-all-done.1.payload, f32[2,384]{1,0:T(2,128)S(1)} %dynamic-slice_bitcast_fusion.rates), custom_call_target="tpu_custom_call" | custom-call | tf_op jit(solution)/shard_map/relay/pallas_call | solution.py:530
  79.6 7.9 %all-to-all-start.2 = ((bf16[128,2,384]{2,1,0:T(2,128)(2,1)}), bf16[128,2,384]{2,1,0:T(2,128)(2,1)S(1)}, u32[]{:S(2)}, u32[]{:S(2)}) async-start(bf16[128,2,384]{2,1,0:T(2,128)(2,1)} %relay.1), calls=%async_computation.2 | async-start | bytes 393216 | tf_op jit(solution)/shard_map/all_to_all | solution.py:701
  87.6 10.6 %local_bwd_outputs.1 = (f32[128,3072]{1,0:T(8,128)}, f32[16,8,3072]{2,1,0:T(8,128)}) custom-call(f32[2,128,3072]{2,1,0:T(8,128)} %get-tuple-element.35.dt_in, bf16[2,128,3072]{2,1,0:T(8,128)(2,1)} %get-tuple-element.36.u_in, f32[2,128,128]{2,1,0:T(8,128)} %get-tuple-element.37.proj, f32[2,16,3072]{2,1,0:T(8,128)S(1)} %broadcast_multiply_fusion.rates, ...), custom_call_target="tpu_custom_call" | custom-call | tf_op jit(solution)/shard_map/local_bwd_outputs/pallas_call | solution.py:663
  98.2 0.1 all-to-all-done.2
  98.3 12.4 %block_outputs.1 = bf16[1024,384]{1,0:T(8,128)(2,1)} custom-call(bf16[2,8,8,2,384]{4,3,2,1,0:T(2,128)(2,1)S(1)} %bitcast.15, f32[16,8,3072]{2,1,0:T(8,128)} %get-tuple-element.44.entry_fwd, f32[16,8,3072]{2,1,0:T(8,128)} %get-tuple-element.45.entry_bwd, f32[128,3072]{1,0:T(8,128)} %get-tuple-element.46.y_fwd, f32[128,3072]{1,0:T(8,128)} %get-tuple-element.47.y_bwd, ...), custom_call_target="tpu_custom_call" | custom-call | tf_op jit(solution)/shard_map/block_outputs/pallas_call | solution.py:708
  110.7 9.7 %all-to-all-start.3 = ((bf16[128,8,384]{2,1,0:T(8,128)(2,1)}), bf16[128,8,384]{2,1,0:T(8,128)(2,1)S(1)}, u32[]{:S(2)}, u32[]{:S(2)}) async-start(bf16[128,8,384]{2,1,0:T(8,128)(2,1)} %bitcast.17), calls=%async_computation.3 | async-start | bytes 1572864 | tf_op jit(solution)/shard_map/all_to_all | solution.py:737
  120.4 5.2 %divide_multiply_fusion.gate = f32[128,3072]{1,0:T(8,128)S(1)} fusion(bf16[128,1536]{1,0:T(8,128)(2,1)S(1)} %copy-done.1, bf16[1536,3072]{1,0:T(8,128)(2,1)} %param.16), kind=kOutput, calls=%fused_computation | convolution fusion | flops 1209532416 | bytes 11403264 | tf_op jit(solution)/shard_map/dot_general | solution.py:599
  125.5 11.6 %all-to-all-done.3 = bf16[128,8,384]{2,1,0:T(8,128)(2,1)S(1)} async-done(((bf16[128,8,384]{2,1,0:T(8,128)(2,1)}), bf16[128,8,384]{2,1,0:T(8,128)(2,1)S(1)}, u32[]{:S(2)}, u32[]{:S(2)}) %all-to-all-start.3) | async-done | bytes 786464 | tf_op jit(solution)/shard_map/all_to_all | solution.py:737
  137.1 1.2 gated.1
  (18 shorter events, 0.1 us)
Async XLA Ops:
  0.0 14.4 %copy-start.8 = (s32[4]{0:T(128)S(1)}, s32[4]{0:T(128)}, u32[]{:S(2)}) copy-start(s32[4]{0:T(128)} %param.14) | copy-start | bytes 52
  0.0 1.0 copy-start
  1.0 0.7 copy-start.6
  1.7 14.8 %copy-start.7 = (f32[2,16,3072]{2,1,0:T(8,128)S(1)}, f32[2,16,3072]{2,1,0:T(8,128)}, u32[]{:S(2)}) copy-start(f32[2,16,3072]{2,1,0:T(8,128)} %param.22) | copy-start | bytes 1179652
  2.9 25.5 %all-to-all-start = ((bf16[128,8,256]{2,1,0:T(8,128)(2,1)}), bf16[128,8,256]{2,1,0:T(8,128)(2,1)S(1)}, u32[]{:S(2)}, u32[]{:S(2)}) async-start(bf16[128,8,256]{2,1,0:T(8,128)(2,1)} %bitcast.3), calls=%async_computation | async-start | bytes 1048576 | tf_op jit(solution)/shard_map/all_to_all | solution.py:596
  29.3 11.5 %collective-permute-start = (bf16[8,1536]{1,0:T(8,128)(2,1)S(1)}, bf16[8,1536]{1,0:T(8,128)(2,1)S(1)}, u32[]{:S(2)}, u32[]{:S(2)}) collective-permute-start(bf16[8,1536]{1,0:T(8,128)(2,1)S(1)} %get-tuple-element.29), channel_id=1, source_target_pairs={{0,1},{1,2},{2,3},{3,4},{4,5},{5,6},{6,7},{7,8},{8,9},{9,10},{10,1... | collective-permute-start | bytes 73736 | tf_op jit(solution)/shard_map/ppermute | solution.py:614
  31.5 9.3 %collective-permute-start.1 = (bf16[8,1536]{1,0:T(8,128)(2,1)S(1)}, bf16[8,1536]{1,0:T(8,128)(2,1)S(1)}, u32[]{:S(2)}, u32[]{:S(2)}) collective-permute-start(bf16[8,1536]{1,0:T(8,128)(2,1)S(1)} %get-tuple-element.30), channel_id=1, source_target_pairs={{1,0},{2,1},{3,2},{4,3},{5,4},{6,5},{7,6},{8,7},{9,8},{10,9},{11,1... | collective-permute-start | bytes 73736 | tf_op jit(solution)/shard_map/ppermute | solution.py:615
  36.1 4.7 %copy-start.2 = (f32[2,4,3072]{2,1,0:T(4,128)S(1)}, f32[2,4,3072]{2,1,0:T(4,128)}, u32[]{:S(2)}) copy-start(f32[2,4,3072]{2,1,0:T(4,128)} %conv_weight.1) | copy-start | bytes 294916
  36.1 4.7 %copy-start.4 = (f32[2,3072]{1,0:T(2,128)S(1)}, f32[2,3072]{1,0:T(2,128)}, u32[]{:S(2)}) copy-start(f32[2,3072]{1,0:T(2,128)} %conv_bias.1) | copy-start | bytes 73732
  36.1 4.7 %copy-start.5 = (f32[2,3072]{1,0:T(2,128)S(1)}, f32[2,3072]{1,0:T(2,128)}, u32[]{:S(2)}) copy-start(f32[2,3072]{1,0:T(2,128)} %dt_bias.1) | copy-start | bytes 73732
  40.8 24.5 %copy-start.3 = (f32[2,3072]{1,0:T(2,128)S(1)}, f32[2,3072]{1,0:T(2,128)}, u32[]{:S(2)}) copy-start(f32[2,3072]{1,0:T(2,128)} %skip_gain.3) | copy-start | bytes 73732
  57.8 19.9 %all-to-all-start.1 = ((bf16[128,4,384]{2,1,0:T(4,128)(2,1)}), bf16[128,4,384]{2,1,0:T(4,128)(2,1)S(1)}, u32[]{:S(2)}, u32[]{:S(2)}) async-start(bf16[128,4,384]{2,1,0:T(4,128)(2,1)} %bitcast.18), calls=%async_computation.1 | async-start | bytes 786432 | tf_op jit(solution)/shard_map/all_to_all | solution.py:689
  79.6 18.7 %all-to-all-start.2 = ((bf16[128,2,384]{2,1,0:T(2,128)(2,1)}), bf16[128,2,384]{2,1,0:T(2,128)(2,1)S(1)}, u32[]{:S(2)}, u32[]{:S(2)}) async-start(bf16[128,2,384]{2,1,0:T(2,128)(2,1)} %relay.1), calls=%async_computation.2 | async-start | bytes 393216 | tf_op jit(solution)/shard_map/all_to_all | solution.py:701
  110.7 9.7 %copy-start.1 = (bf16[128,1536]{1,0:T(8,128)(2,1)S(1)}, bf16[128,1536]{1,0:T(8,128)(2,1)}, u32[]{:S(2)}) copy-start(bf16[128,1536]{1,0:T(8,128)(2,1)} %embed.1) | copy-start | bytes 1179652
  110.7 26.5 %all-to-all-start.3 = ((bf16[128,8,384]{2,1,0:T(8,128)(2,1)}), bf16[128,8,384]{2,1,0:T(8,128)(2,1)S(1)}, u32[]{:S(2)}, u32[]{:S(2)}) async-start(bf16[128,8,384]{2,1,0:T(8,128)(2,1)} %bitcast.17), calls=%async_computation.3 | async-start | bytes 1572864 | tf_op jit(solution)/shard_map/all_to_all | solution.py:737

commit v4 on v2

--- a/solution.py
+++ b/solution.py
@@ -10,6 +10,7 @@
 AXES = ("seq", "slide")
 SUB = 8
 LANES = 128
+PACK = 16
 LOG2E = 1.4426950408889634
 
 
@@ -94,24 +95,69 @@
     sorted_rows[...] = as_bf16(over_rows(one_hot(pos), data))
 
 
-def inner_kernel(rows_in, weight, x_project, dt_project, out, weight_here, x_here, dt_here, sems):
+def inner_kernel(
+    rows_in,
+    conv_weight,
+    conv_bias,
+    weight,
+    x_project,
+    dt_project,
+    u_out,
+    proj_out,
+    edge_sums,
+    weight_here,
+    x_here,
+    dt_here,
+    extended,
+    sems,
+):
     parts = sems.shape[0] - 2
     width = weight.shape[1] // parts
-    copies = []
+    rows = rows_in.shape[0]
+    taps = conv_weight.shape[1]
+    reach = taps - 1
+    slots = rows // SUB
+    moves = []
     for k in range(parts):
         cols = pl.ds(k * width, width)
-        copies.append((weight.at[:, cols], weight_here.at[:, cols]))
-    copies += [(x_project, x_here), (dt_project, dt_here)]
+        moves.append((weight.at[:, cols], weight_here.at[:, cols]))
+        if k == 0:
+            moves.append((x_project, x_here))
+    moves.append((dt_project, dt_here))
     copies = [
-        pltpu.make_async_copy(here, there, sems.at[k]) for k, (here, there) in enumerate(copies)
+        pltpu.make_async_copy(here, there, sems.at[k]) for k, (here, there) in enumerate(moves)
     ]
     for copy in copies:
         copy.start()
+    proj_out[...] = jnp.zeros_like(proj_out)
+    row = sublane((SUB, width))
     for k in range(parts):
-        cols = pl.ds(k * width, width)
-        copies[k].wait()
-        out[:, cols] = as_bf16(matmul(rows_in[...], weight_here[:, cols]))
-    copies[parts].wait()
+        cols = slice(k * width, k * width + width)
+        if k == 0:
+            copies[0].wait()
+            copies[1].wait()
+        else:
+            copies[k + 1].wait()
+        main = as_bf16(matmul(rows_in[...], weight_here[:, cols])).astype(jnp.float32)
+        extended[SUB * reach : SUB * reach + rows] = main
+        for i in range(reach):
+            own = main[rows - SUB * (reach - i) : rows - SUB * (reach - i - 1)]
+            extended[SUB * i : SUB * i + SUB] = jnp.where(row == 0, 0.0, pltpu.roll(own, 1, 0))
+            own = main[SUB * i : SUB * i + SUB]
+            base = SUB * (reach + slots + i)
+            extended[base : base + SUB] = jnp.where(
+                row == SUB - 1, 0.0, pltpu.roll(own, SUB - 1, 0)
+            )
+        for d in range(2):
+            mixed = conv_bias[d : d + 1, cols]
+            for tap in range(taps):
+                base = SUB * (2 * reach - tap if d else tap)
+                mixed = mixed + conv_weight[d, tap : tap + 1, cols] * extended[base : base + rows]
+            edge = SUB * reach
+            edge_sums[d, :, cols] = mixed[rows - edge :] if d else mixed[:edge]
+            u = as_bf16(silu(mixed))
+            u_out[d, :, cols] = u
+            proj_out[d] += matmul(u, x_here[d, cols, :])
     copies[parts + 1].wait()
 
 
@@ -151,7 +197,30 @@
 
 
 def silu(v):
-    return v / (1.0 + jnp.exp(-v))
+    half = 0.5 * v
+    return half + half * jnp.tanh(half)
+
+
+def halves(array):
+    high = as_bf16(array)
+    return high, as_bf16(array - high.astype(jnp.float32))
+
+
+def paired(first, second):
+    return as_bf16(jnp.concatenate([first, second], axis=0))
+
+
+def sum_over_states(columns, first, states):
+    rows = columns.shape[0]
+    size = (columns.shape[1], PACK * states)
+    col = lax.broadcasted_iota(jnp.int32, size, 0)
+    at = lax.broadcasted_iota(jnp.int32, size, 1)
+    repeat = (col == first + at // PACK).astype(jnp.float32).astype(jnp.bfloat16)
+    size = (rows, PACK * states)
+    row = lax.broadcasted_iota(jnp.int32, size, 0)
+    at = lax.broadcasted_iota(jnp.int32, size, 1)
+    own = row % PACK == at % PACK
+    return [as_bf16(jnp.where(own, matmul(part, repeat), 0.0)) for part in halves(columns)]
 
 
 def softplus(v):
@@ -160,27 +229,29 @@
 
 def states_kernel(
     flags,
-    inner_in,
+    proj_in,
+    edge_sums,
     before,
     after,
     w_inner,
     conv_weight,
-    conv_bias,
     x_project,
     dt_project,
     dt_bias,
     rates,
+    u_in,
     u_result,
     proj_result,
     dt_result,
     payload_result,
+    entry_result,
     u_out,
     proj_out,
     dt_out,
+    payload,
+    entry,
     b_wide,
-    payload,
     edge_rows,
-    extended,
     sems,
 ):
     copies = [
@@ -195,49 +266,43 @@
             )
         )
     ]
-    rows, channels = inner_in.shape
+    _, rows, channels = u_out.shape
     taps = conv_weight.shape[1]
     reach = taps - 1
-    width = extended.shape[1]
+    width = channels // 4
     states = rates.shape[1]
     rank = dt_project.shape[1]
     slots = rows // SUB
     tile = payload.shape[4]
+    edge = SUB * reach
     edge_rows[:SUB] = before[...]
     edge_rows[SUB:] = after[...]
-    proj_out[...] = jnp.zeros_like(proj_out)
-
-    def conv_block(step, carry):
-        cols = pl.ds(pl.multiple_of(step * width, LANES), width)
+    row = sublane((SUB, width))
+    projected = [jnp.zeros((edge, LANES), jnp.float32)] * 2
+    for step in range(channels // width):
+        cols = slice(step * width, step * width + width)
         edges = as_bf16(matmul(edge_rows[...], w_inner[:, cols])).astype(jnp.float32)
-        main = inner_in[:, cols].astype(jnp.float32)
         prior = edges[:SUB] * flags[0].astype(jnp.float32)
         later = edges[SUB:] * flags[1].astype(jnp.float32)
-        row = sublane((SUB, width))
-        extended[SUB * reach : SUB * reach + rows] = main
-        for k in range(reach):
-            own = main[rows - SUB * (reach - k) : rows - SUB * (reach - k - 1)]
-            extended[SUB * k : SUB * k + SUB] = jnp.where(
-                row == 0, prior[k : k + 1], pltpu.roll(own, 1, 0)
-            )
-            own = main[SUB * k : SUB * k + SUB]
-            base = SUB * (reach + slots + k)
-            extended[base : base + SUB] = jnp.where(
-                row == SUB - 1, later[k : k + 1], pltpu.roll(own, SUB - 1, 0)
-            )
         for d in range(2):
-            mixed = conv_bias[d : d + 1, cols]
-            for tap in range(taps):
-                base = SUB * (2 * reach - tap if d else tap)
-                gain = conv_weight[d, tap : tap + 1, cols]
-                mixed = mixed + gain * extended[base : base + rows]
-            u = as_bf16(silu(mixed))
-            u_out[d, :, cols] = u
-            proj_out[d] += matmul(u, x_project[d, cols, :])
-        return carry
-
-    lax.fori_loop(0, channels // width, conv_block, 0)
+            tiles = []
+            for m in range(reach):
+                if d:
+                    terms = [(tap, later[m - tap : m - tap + 1]) for tap in range(m + 1)]
+                else:
+                    terms = [(tap, prior[m + tap : m + tap + 1]) for tap in range(reach - m)]
+                extra = sum(conv_weight[d, tap : tap + 1, cols] * term for tap, term in terms)
+                mixed = edge_sums[d, SUB * m : SUB * m + SUB, cols]
+                tiles.append(mixed + jnp.where(row == (SUB - 1 if d else 0), extra, 0.0))
+            u = as_bf16(silu(jnp.concatenate(tiles, axis=0)))
+            first = rows - edge if d else 0
+            u_out[d, first : first + edge, cols] = u
+            projected[d] = projected[d] + matmul(u, x_project[d, cols, :])
     copies[0].start()
+    for d in range(2):
+        proj_out[d] = proj_in[d]
+        first = rows - edge if d else 0
+        proj_out[d, first : first + edge] = projected[d]
     copies[1].start()
     for d in range(2):
         spread_columns(b_wide.at[d], proj_out[d], rank, states)
@@ -262,84 +327,51 @@
         dt = dt_out[d, :, here]
         fed = tiles_of(dt * u_out[d, :, here].astype(jnp.float32))
         dt = tiles_of(dt)
-        order = in_order(slots, not reverse)
-        rest = {order[0]: None}
-        total = dt[order[0]]
-        for t in order[1:]:
-            rest[t] = total
+        total = dt[0]
+        for t in range(1, slots):
             total = total + dt[t]
-        outer = outside(total, not reverse)
-        whole = total + outer
-        whole = whole[SUB - 1 : SUB] if reverse else whole[0:1]
-        rest = {t: outer if part is None else part + outer for t, part in rest.items()}
+        near = in_reach(1, reverse)
         finals = []
         for n in range(states):
             rate = rates[d, n : n + 1, here]
             state = None
-            for t in order:
+            for t in in_order(slots, reverse):
                 new = fed[t] * b_wide[d, n, SUB * t : SUB * t + SUB]
-                new = jnp.exp2(rest[t] * rate) * new
-                state = new if state is None else state + new
-            finals.append(jnp.sum(state, axis=0, keepdims=True))
-        for n in range(0, states, 2):
-            out = jnp.where(row == 0, finals[n], finals[n + 1])
-            out = jnp.where(row >= 2, whole, out)
-            payload[d, n // 2, group, :, pl.ds(within, LANES)] = as_bf16(out[:4])
-        return carry
-
-    for d in range(2):
-        lax.fori_loop(0, channels // LANES, functools.partial(state_block, d=d), 0)
-        copies[3 + d].start()
-    for copy in copies:
-        copy.wait()
-
-
-def local_kernel(dt_in, u_in, proj, rates, skip_gain, y_out, entry_out, b_wide, c_wide, *, reverse):
-    d = int(reverse)
-    states = rates.shape[1]
-    rows, channels = y_out.shape
-    slots = rows // SUB
-    rank = proj.shape[2] - 2 * states
-
-    @pl.when(pl.program_id(0) == 0)
-    def _():
-        spread_columns(b_wide, proj[0], rank, states)
-        spread_columns(c_wide, proj[0], rank + states, states)
-
-    def lane_block(block, carry):
-        here = pl.ds(pl.multiple_of(block * LANES, LANES), LANES)
-        dt = dt_in[0, :, here]
-        u = u_in[0, :, here].astype(jnp.float32)
-        fed = tiles_of(dt * u)
-        dt = tiles_of(dt)
-        gain = skip_gain[d : d + 1, here]
-        sums = [gain * tile for tile in tiles_of(u)]
-        total = dt[0]
-        for t in range(1, slots):
-            total = total + dt[t]
-        for n in range(states):
-            rate = rates[0, n : n + 1, here]
-            state = None
-            for t in in_order(slots, reverse):
-                at = slice(SUB * t, SUB * t + SUB)
-                new = fed[t] * b_wide[n, at]
                 if state is not None:
                     new = jnp.exp2(dt[t] * rate) * state + new
                 state = new
-                sums[t] = sums[t] + c_wide[n, at] * state
             keep = jnp.exp2(total * rate)
             for count in (1, 2, 4):
                 keep = jnp.where(in_reach(count, reverse), keep, 0.0)
                 state = state + keep * shift_sublanes(state, count, reverse)
                 if count < 4:
                     keep = keep * shift_sublanes(keep, count, reverse)
-            near = in_reach(1, reverse)
-            entry_out[n, :, here] = jnp.where(near, shift_sublanes(state, 1, reverse), 0.0)
-        for t in range(slots):
-            y_out[SUB * t : SUB * t + SUB, here] = sums[t]
+            entry[d, n, :, here] = jnp.where(near, shift_sublanes(state, 1, reverse), 0.0)
+            finals.append(state[0:1] if reverse else state[SUB - 1 : SUB])
+        whole = jnp.sum(total, axis=0, keepdims=True)
+        for n in range(0, states, 2):
+            out = jnp.where(row == 0, finals[n], finals[n + 1])
+            out = jnp.where(row >= 2, whole, out)
+            payload[d, n // 2, group, :, pl.ds(within, LANES)] = as_bf16(out[:4])
         return carry
 
-    lax.fori_loop(0, channels // LANES, lane_block, 0)
+    thirds = channels // LANES // 3
+    for d in range(2):
+        for part in range(3):
+            body = functools.partial(state_block, d=d)
+            lax.fori_loop(part * thirds, part * thirds + thirds, body, 0)
+            cols = pl.ds(part * thirds * LANES, thirds * LANES)
+            copies.append(
+                pltpu.make_async_copy(
+                    entry.at[d, :, :, cols],
+                    entry_result.at[d, :, :, cols],
+                    sems.at[5 + 3 * d + part],
+                )
+            )
+            copies[-1].start()
+        copies[3 + d].start()
+    for copy in copies:
+        copy.wait()
 
 
 def relay_kernel(keep, payload, rates, entering):
@@ -358,61 +390,78 @@
 
 def outputs_kernel(
     entering,
-    entry_fwd,
-    entry_bwd,
-    y_fwd,
-    y_bwd,
+    entry,
     dt_in,
+    u_in,
     proj,
     rates,
+    skip_gain,
     places,
     out,
-    c_wide,
-    mixed,
+    left,
+    b_wide,
     placed,
 ):
     step = pl.program_id(0)
     states = rates.shape[1]
-    rows, channels = y_fwd.shape
+    _, rows, channels = dt_in.shape
     slots = rows // SUB
     rank = proj.shape[2] - 2 * states
+    tile = entering.shape[4]
 
     @pl.when(step == 0)
     def _():
         for d in range(2):
-            spread_columns(c_wide.at[d], proj[d], rank + states, states)
-
-    def lane_block(block, carry, d, entry):
-        here = pl.ds(pl.multiple_of(block * LANES, LANES), LANES)
+            spread_columns(b_wide.at[d], proj[d], rank, states)
+            parts = sum_over_states(proj[d], rank + states, states)
+            for k in range(slots // 2):
+                for i, part in enumerate(parts):
+                    left[d, k, PACK * i : PACK * i + PACK] = part[PACK * k : PACK * k + PACK]
+
+    def swept(at, d):
+        here = slice(at * LANES, at * LANES + LANES)
+        block = step * (channels // LANES) + at
+        group = block // (tile // LANES)
+        within = pl.multiple_of((block - group * (tile // LANES)) * LANES, LANES)
         reverse = d == 1
-        sums = tiles_of(mixed[:, here] if reverse else y_fwd[:, here] + y_bwd[:, here])
-        dt = tiles_of(dt_in[d, :, here])
-        order = in_order(slots, reverse)
-        past = {}
-        total = None
-        for t in order:
-            total = dt[t] if total is None else total + dt[t]
-            past[t] = total
+        dt = dt_in[d, :, here]
+        u = u_in[d, :, here].astype(jnp.float32)
+        fed = tiles_of(dt * u)
+        dt = tiles_of(dt)
+        total = dt[0]
+        for t in range(1, slots):
+            total = total + dt[t]
         ahead = outside(total, reverse)
+        state = []
         for n in range(states):
-            rate = rates[d, n : n + 1, here]
-            pair = entering[d, n // 2, 0, :, here].astype(jnp.float32)
-            state = jnp.exp2(ahead * rate) * pair[n % 2 : n % 2 + 1] + entry[n, :, here]
-            for t in order:
-                at = slice(SUB * t, SUB * t + SUB)
-                decayed = jnp.exp2(past[t] * rate)
-                sums[t] = sums[t] + decayed * (c_wide[d, n, at] * state)
-        for t in range(slots):
-            mixed[SUB * t : SUB * t + SUB, here] = sums[t]
-        return carry
-
-    for d, entry in ((0, entry_fwd), (1, entry_bwd)):
-        lax.fori_loop(0, channels // LANES, functools.partial(lane_block, d=d, entry=entry), 0)
-    placed[step] = as_bf16(matmul(one_hot(places[...]), as_bf16(mixed[...])))
+            pair = entering[d, n // 2, group, :, pl.ds(within, LANES)].astype(jnp.float32)
+            carried = jnp.exp2(ahead * rates[d, n : n + 1, here]) * pair[n % 2 : n % 2 + 1]
+            state.append(carried + entry[d, n, :, here])
+        sums = [None] * (slots // 2)
+        for k in in_order(slots // 2, reverse):
+            right = []
+            for n in range(states):
+                rate = rates[d, n : n + 1, here]
+                both = []
+                for t in in_order(2, reverse):
+                    t = 2 * k + t
+                    new = fed[t] * b_wide[d, n, SUB * t : SUB * t + SUB]
+                    state[n] = jnp.exp2(dt[t] * rate) * state[n] + new
+                    both.append(state[n])
+                right.append(paired(*(both[::-1] if reverse else both)))
+            part = matmul(left[d, k], jnp.concatenate(right, axis=0))
+            sums[k] = part[:PACK] + part[PACK:]
+        return jnp.concatenate(sums, axis=0) + skip_gain[d : d + 1, here] * u
+
+    pick = one_hot(places[...])
+    for at in range(channels // LANES):
+        total = swept(at, 0) + swept(at, 1)
+        start = pl.multiple_of(step * channels + at * LANES, LANES)
+        placed[:, pl.ds(start, LANES)] = as_bf16(matmul(pick, as_bf16(total)))
 
     @pl.when(step == pl.num_programs(0) - 1)
     def _():
-        chunked([placed[k] for k in range(SUB)], out)
+        chunked([placed[:, tile * k : tile * k + tile] for k in range(SUB)], out)
 
 
 def gate_kernel(returned, gate, out):
@@ -506,9 +555,12 @@
     )[0]
 
     piece = 2 * LANES
-    sent = on_chip(
-        pack_kernel, "pack", 3, pltpu.VMEM((SUB * rows, piece), bf16), tile_embed, destination[None, :]
-    )
+    sent = pl.pallas_call(
+        pack_kernel,
+        out_shape=pltpu.VMEM((SUB * rows, piece), bf16),
+        compiler_params=limits(3),
+        name="pack",
+    )(in_hbm(tile_embed), in_hbm(destination[None, :]))
     arrived = lax.all_to_all(
         sent.reshape(rows, SUB, piece), AXES, split_axis=0, concat_axis=0, tiled=True
     ).reshape(SUB * rows, piece)
@@ -532,80 +584,64 @@
     hbm_spec = pl.BlockSpec(memory_space=pltpu.HBM)
     vmem_spec = pl.BlockSpec(memory_space=pltpu.VMEM)
     weights = (w_inner, x_project, dt_project)
-    inner, w_inner, x_project, dt_project = pl.pallas_call(
-        inner_kernel,
-        out_shape=(
-            pltpu.VMEM((rows, width), bf16),
-            *(pltpu.VMEM(w.shape, w.dtype) for w in weights),
-        ),
-        in_specs=[vmem_spec] + [hbm_spec] * 3,
-        out_specs=(vmem_spec,) * 4,
-        scratch_shapes=[pltpu.SemaphoreType.DMA((6,))],
-        compiler_params=limits(2),
-        name="inner",
-    )(in_vmem(block_rows), *(in_hbm(w) for w in weights))
-
-    operands = (
-        inner, before, after, w_inner, conv_weight, conv_bias, x_project, dt_project, dt_bias, rates,
-    )
-    on_chip_results = [
+    edge = SUB * (taps - 1)
+    results = (
         pltpu.VMEM((2, rows, width), bf16),
         pltpu.VMEM((2, rows, LANES), f32),
+        pltpu.VMEM((2, edge, width), f32),
+        *(pltpu.VMEM(w.shape, w.dtype) for w in weights),
+    )
+    u, proj, edge_sums, w_inner, x_project, dt_project = pl.pallas_call(
+        inner_kernel,
+        out_shape=results,
+        in_specs=[vmem_spec] * 3 + [hbm_spec] * 3,
+        out_specs=(vmem_spec,) * len(results),
+        scratch_shapes=[
+            pltpu.VMEM((rows + 2 * edge, width // 4), f32),
+            pltpu.SemaphoreType.DMA((6,)),
+        ],
+        compiler_params=limits(4),
+        name="inner",
+    )(
+        *(in_vmem(operand) for operand in (block_rows, conv_weight, conv_bias)),
+        *(in_hbm(w) for w in weights),
+    )
+
+    operands = (
+        proj, edge_sums, before, after, w_inner, conv_weight, x_project, dt_project, dt_bias, rates, u,
+    )
+    on_chip_results = [
+        pltpu.VMEM((2, rows, LANES), f32),
         pltpu.VMEM((2, rows, width), f32),
+        pltpu.VMEM((2, state_groups, groups, 4, tile), bf16),
+        pltpu.VMEM((2, states, SUB, width), f32),
         pltpu.VMEM((2, states, rows, LANES), f32),
-        pltpu.VMEM((2, state_groups, groups, 4, tile), bf16),
     ]
-    u, proj, dt, payload = pl.pallas_call(
+    u, proj, dt, payload, entry, _ = pl.pallas_call(
         states_kernel,
         out_shape=(
             pltpu.HBM((2, rows, width), bf16),
             pltpu.HBM((2, rows, LANES), f32),
             pltpu.HBM((2, rows, width), f32),
             pltpu.HBM((2, state_groups, groups, 4, tile), bf16),
+            pltpu.HBM((2, states, SUB, width), f32),
+            pltpu.VMEM((2, rows, width), bf16),
         ),
         in_specs=[pl.BlockSpec(memory_space=pltpu.SMEM)] + [vmem_spec] * len(operands),
-        out_specs=(hbm_spec,) * 4,
+        out_specs=(hbm_spec,) * 5 + (vmem_spec,),
+        input_output_aliases={len(operands): 5},
         scratch_shapes=on_chip_results
         + [
             pltpu.VMEM((2 * SUB, model), bf16),
-            pltpu.VMEM((rows + 2 * SUB * (taps - 1), 2 * tile), f32),
-            pltpu.SemaphoreType.DMA((5,)),
+            pltpu.SemaphoreType.DMA((11,)),
         ],
         compiler_params=limits(14),
         name="block_states",
     )(flags, *(in_vmem(operand) for operand in operands))
 
-    def local_outputs(d):
-        return pl.pallas_call(
-            functools.partial(local_kernel, reverse=d == 1),
-            out_shape=(
-                pltpu.HBM((rows, width), f32),
-                pltpu.HBM((states, SUB, width), f32),
-            ),
-            grid=(groups,),
-            in_specs=[
-                pl.BlockSpec((1, rows, tile), lambda i: (d, 0, i)),
-                pl.BlockSpec((1, rows, tile), lambda i: (d, 0, i)),
-                pl.BlockSpec((1, rows, LANES), lambda i: (d, 0, 0)),
-                pl.BlockSpec((1, states, tile), lambda i: (d, 0, i)),
-                pl.BlockSpec((2, tile), lambda i: (0, i)),
-            ],
-            out_specs=[
-                pl.BlockSpec((rows, tile), lambda i: (0, i)),
-                pl.BlockSpec((states, SUB, tile), lambda i: (0, 0, i)),
-            ],
-            scratch_shapes=[pltpu.VMEM((states, rows, LANES), f32)] * 2,
-            compiler_params=limits(6),
-            name="local_bwd_outputs" if d else "local_fwd_outputs",
-        )(in_hbm(dt), in_hbm(u), in_hbm(proj), rates, skip_gain)
-
-    local_fwd = local_outputs(0)
-    local_bwd = local_outputs(1)
-
     shared = lax.all_to_all(
         payload.reshape(shards, 4, tile), AXES, split_axis=0, concat_axis=0, tiled=True
     )
-    shared, *local_fwd = lax.optimization_barrier((shared, *local_fwd))
     entering = on_chip(
         relay_kernel,
         "relay",
@@ -615,38 +651,36 @@
         scalars=1,
     )
     entering = lax.all_to_all(entering, AXES, split_axis=0, concat_axis=0, tiled=True)
-    entering, *local_bwd = lax.optimization_barrier((entering, *local_bwd))
     entering = entering.reshape(2, state_groups, groups, owner_states, tile)
-    y_fwd, entry_fwd = local_fwd
-    y_bwd, entry_bwd = local_bwd
-
+
+    part = 4 * LANES
     totals = pl.pallas_call(
         outputs_kernel,
         out_shape=pltpu.HBM((SUB * rows, tile), bf16),
-        grid=(groups,),
+        grid=(width // part,),
         in_specs=[
-            pl.BlockSpec((2, state_groups, 1, owner_states, tile), lambda i: (0, 0, i, 0, 0)),
-            pl.BlockSpec((states, SUB, tile), lambda i: (0, 0, i)),
-            pl.BlockSpec((states, SUB, tile), lambda i: (0, 0, i)),
-            pl.BlockSpec((rows, tile), lambda i: (0, i)),
-            pl.BlockSpec((rows, tile), lambda i: (0, i)),
-            pl.BlockSpec((2, rows, tile), lambda i: (0, 0, i)),
+            vmem_spec,
+            pl.BlockSpec((2, states, SUB, part), lambda i: (0, 0, 0, i)),
+            pl.BlockSpec((2, rows, part), lambda i: (0, 0, i)),
+            pl.BlockSpec((2, rows, part), lambda i: (0, 0, i)),
             pl.BlockSpec((2, rows, LANES), lambda i: (0, 0, 0)),
-            pl.BlockSpec((2, states, tile), lambda i: (0, 0, i)),
+            pl.BlockSpec((2, states, part), lambda i: (0, 0, i)),
+            pl.BlockSpec((2, part), lambda i: (0, i)),
             pl.BlockSpec((rows, LANES), lambda i: (0, 0)),
         ],
         out_specs=pl.BlockSpec((SUB * rows, tile), lambda i: (0, 0)),
         scratch_shapes=[
+            pltpu.VMEM((2, slots // 2, 2 * PACK, PACK * states), bf16),
             pltpu.VMEM((2, states, rows, LANES), f32),
-            pltpu.VMEM((rows, tile), f32),
-            pltpu.VMEM((groups, rows, tile), bf16),
+            pltpu.VMEM((rows, width), bf16),
         ],
         compiler_params=limits(12),
         name="block_outputs",
     )(
         in_vmem(entering),
-        *(in_hbm(array) for array in (entry_fwd, entry_bwd, y_fwd, y_bwd, dt, proj)),
+        *(in_hbm(array) for array in (entry, dt, u, proj)),
         rates,
+        skip_gain,
         in_hbm(places),
     )
 

time: 143 us -> 132 us (0.923)
  Pallas kernels: 64.7 us -> 45.3 us
  starting transfers between devices: 43.2 us -> 28.3 us
  blocking collectives: 0 us -> 14.4 us
  waiting for transfers between devices: 25.3 us -> 35.9 us
  local copies, waits for them, and re-layouts: 1.78 us -> 0.12 us
    pallas_call x3 -> x2, Pallas kernels: 25.9 us -> 8.14 us  [the longest x1 5.87 us: local(): pl.pallas_call(inner_kernel, out_shape=results, in_specs=[vmem_spec] * 3...]
    all_to_all x0 -> x1, blocking collectives: none -> 14.4 us  [local(): lax.all_to_all(entering, AXES, split_axis=0, concat_axis=0, tiled=True)]
    all_to_all x1, waiting for transfers between devices: 1.83 us -> 12.5 us  [local(): lax.all_to_all(payload.reshape(shards, 4, tile), AXES, split_axis=0, conc...]
    all_to_all x1 -> x0, starting transfers between devices: 7.93 us -> none  [local(): lax.all_to_all(entering, AXES, split_axis=0, concat_axis=0, tiled=True)]
    all_to_all x1, starting transfers between devices: 9.71 us -> 3.96 us  [local(): lax.all_to_all(totals.reshape(rows, SUB, tile), AXES, split_axis=0, conca...]
    pallas_call x3 -> x2, Pallas kernels: 3.97 us -> 2.09 us  [on_chip(): pl.pallas_call(kernel, out_shape=results, in_specs=[pl.BlockSpec(memory_s...]
    unnamed x18 -> x14, local copies, waits for them, and re-layouts: 1.69 us -> 0.03 us
  transfers between devices with their start and end apart: 6 -> 5, of which waited for: 4 -> 3; matrix products, arithmetic and copies ran while one was open for 4% -> 5% of each run, Pallas kernels for 18% -> 4%
where the time goes in v4:
time: 132 us
  Pallas kernels  45.3 us (34%)
  waiting for transfers between devices  35.9 us (27%)
  starting transfers between devices  28.3 us (21%)
  blocking collectives  14.4 us (11%)
  matrix products  5.16 us (4%)
  between operations  1.52 us (1%)
    pallas_call x1, Pallas kernels, local(): pl.pallas_call(states_kernel, out_shape=(pltpu.HBM((2, rows, width), bf16...  17.6 us
    pallas_call x1, Pallas kernels, local(): pl.pallas_call(outputs_kernel, out_shape=pltpu.HBM((SUB * rows, tile), bf...  16.3 us
    all_to_all x1, blocking collectives, local(): lax.all_to_all(entering, AXES, split_axis=0, concat_axis=0, tiled=True)  14.4 us
    all_to_all x1, waiting for transfers between devices, local(): lax.all_to_all(payload.reshape(shards, 4, tile), AXES, split_axis=0, conc...  12.5 us
    all_to_all x1, waiting for transfers between devices, local(): lax.all_to_all(totals.reshape(rows, SUB, tile), AXES, split_axis=0, conca...  11.7 us
    all_to_all x1, waiting for transfers between devices, local(): lax.all_to_all(sent.reshape(rows, SUB, piece), AXES, split_axis=0, concat...  11.7 us
    all_to_all x1, starting transfers between devices, local(): lax.all_to_all(sent.reshape(rows, SUB, piece), AXES, split_axis=0, concat...  11.5 us
    all_to_all x1, starting transfers between devices, local(): lax.all_to_all(payload.reshape(shards, 4, tile), AXES, split_axis=0, conc...  6.06 us
  transfers between devices with their start and end apart: 5, of which 3 were waited for; matrix products, arithmetic and copies ran while one was open for 5% of the time, Pallas kernels for 4%

profile of v4, /device:TPU:1, one launch (start us, length us, event | category | flops | bytes accessed | tf_op | source)
XLA Modules:
  0.0 131.8 jit_solution(14858923265665487589)
XLA Ops:
  0.0 0.0 copy-start.2
  0.0 2.3 %pack.1 = bf16[1024,256]{1,0:T(8,128)(2,1)} custom-call(bf16[128,1536]{1,0:T(8,128)(2,1)} %embed.1, s32[1,128]{1,0:T(1,128)} %bitcast.18), custom_call_target="tpu_custom_call" | custom-call | tf_op jit(solution)/shard_map/pack/pallas_call | solution.py:558
  2.3 11.5 %all-to-all-start = ((bf16[128,8,256]{2,1,0:T(8,128)(2,1)}), bf16[128,8,256]{2,1,0:T(8,128)(2,1)S(1)}, u32[]{:S(2)}, u32[]{:S(2)}) async-start(bf16[128,8,256]{2,1,0:T(8,128)(2,1)} %bitcast.3), calls=%async_computation | async-start | bytes 1048576 | tf_op jit(solution)/shard_map/all_to_all | solution.py:564
  13.8 0.0 copy-done.6
  13.9 0.1 select_reduce_fusion
  14.0 0.1 compare_reduce_fusion
  14.0 0.7 and_reduce_fusion.1
  16.0 0.0 copy-done.4
  16.1 11.7 %all-to-all-done = bf16[128,8,256]{2,1,0:T(8,128)(2,1)S(1)} async-done(((bf16[128,8,256]{2,1,0:T(8,128)(2,1)}), bf16[128,8,256]{2,1,0:T(8,128)(2,1)S(1)}, u32[]{:S(2)}, u32[]{:S(2)}) %all-to-all-start) | async-done | bytes 524320 | tf_op jit(solution)/shard_map/all_to_all | solution.py:564
  27.8 0.9 sort_rows.1
  28.7 2.2 %collective-permute-start = (bf16[8,1536]{1,0:T(8,128)(2,1)S(1)}, bf16[8,1536]{1,0:T(8,128)(2,1)S(1)}, u32[]{:S(2)}, u32[]{:S(2)}) collective-permute-start(bf16[8,1536]{1,0:T(8,128)(2,1)S(1)} %get-tuple-element.23), channel_id=1, source_target_pairs={{0,1},{1,2},{2,3},{3,4},{4,5},{5,6},{6,7},{7,8},{8,9},{9,10},{10,1... | collective-permute-start | bytes 73736 | tf_op jit(solution)/shard_map/ppermute | solution.py:582
  30.9 4.6 %collective-permute-start.1 = (bf16[8,1536]{1,0:T(8,128)(2,1)S(1)}, bf16[8,1536]{1,0:T(8,128)(2,1)S(1)}, u32[]{:S(2)}, u32[]{:S(2)}) collective-permute-start(bf16[8,1536]{1,0:T(8,128)(2,1)S(1)} %get-tuple-element.24), channel_id=1, source_target_pairs={{1,0},{2,1},{3,2},{4,3},{5,4},{6,5},{7,6},{8,7},{9,8},{10,9},{11,1... | collective-permute-start | bytes 73736 | tf_op jit(solution)/shard_map/ppermute | solution.py:583
  35.5 0.1 add_convert_fusion.flags
  35.5 0.0 copy-done
  35.6 0.0 copy-done.2
  35.6 5.9 %inner.1 = (bf16[2,128,3072]{2,1,0:T(8,128)(2,1)S(1)}, f32[2,128,128]{2,1,0:T(8,128)S(1)}, f32[2,24,3072]{2,1,0:T(8,128)S(1)}, bf16[1536,3072]{1,0:T(8,128)(2,1)...) custom-call(bf16[128,1536]{1,0:T(8,128)(2,1)S(1)} %get-tuple-element.20.rows_in, ...), custom_call_target="tpu_custom_call" | custom-call | tf_op jit(solution)/shard_map/inner/pallas_call | solution.py:594
  41.4 0.0 collective-permute-done.before
  41.4 0.0 collective-permute-done.1.after
  41.5 0.0 copy-done.1
  41.5 17.6 %block_states.1 = (bf16[2,128,3072]{2,1,0:T(8,128)(2,1)}, f32[2,128,128]{2,1,0:T(8,128)}, f32[2,128,3072]{2,1,0:T(8,128)}, bf16[2,8,8,4,384]{4,3,2,1,0:T(4,128)(...) custom-call(s32[2]{0:T(128)S(1)} %add_convert_fusion.flags, ...), custom_call_target="tpu_custom_call", output_to_operand_aliasing={{5}: (11, {})} | custom-call | tf_op jit(solution)/shard_map/block_states/pallas_call | solution.py:620
  59.0 0.0 copy-start.3
  59.0 6.1 %all-to-all-start.1 = ((bf16[128,4,384]{2,1,0:T(4,128)(2,1)}), bf16[128,4,384]{2,1,0:T(4,128)(2,1)S(1)}, u32[]{:S(2)}, u32[]{:S(2)}) async-start(bf16[128,4,384]{2,1,0:T(4,128)(2,1)} %bitcast.17), calls=%async_computation.1 | async-start | bytes 786432 | tf_op jit(solution)/shard_map/all_to_all | solution.py:642
  65.2 0.1 dynamic-slice_bitcast_fusion.rates
  65.3 12.5 %all-to-all-done.1.payload = bf16[128,4,384]{2,1,0:T(4,128)(2,1)S(1)} async-done(((bf16[128,4,384]{2,1,0:T(4,128)(2,1)}), bf16[128,4,384]{2,1,0:T(4,128)(2,1)S(1)}, u32[]{:S(2)}, u32[]{:S(2)}) %all-to-all-start.1) | async-done | bytes 393248 | tf_op jit(solution)/shard_map/all_to_all | solution.py:642
  77.7 1.2 relay.1
  78.9 14.4 %all_to_all.20 = bf16[128,2,384]{2,1,0:T(2,128)(2,1)S(1)} all-to-all(bf16[128,2,384]{2,1,0:T(2,128)(2,1)S(1)} %relay.1), channel_id=1, replica_groups=mesh['seq'=32,'slide'=4] {'seq','slide'}, dimensions={0} | all-to-all | bytes 393216 | tf_op jit(solution)/shard_map/all_to_all | solution.py:653
  93.4 0.0 copy-done.3
  93.4 16.3 %block_outputs.1 = bf16[1024,384]{1,0:T(8,128)(2,1)} custom-call(bf16[2,8,8,2,384]{4,3,2,1,0:T(2,128)(2,1)S(1)} %bitcast.15, f32[2,16,8,3072]{3,2,1,0:T(8,128)} %get-tuple-element.30.entry, f32[2,128,3072]{2,1,0:T(8,128)} %get-tuple-element.31.dt_in, bf16[2,128,3072]{2,1,0:T(8,128)(2,1)} %get-tuple-element.32.u_in, f32[2,128,128]{2,1,0:T(8,128)} %get-tuple-element.33.proj, ...), custom_call_target="tpu_custom_call" | custom-call | tf_op jit(solution)/shard_map/block_outputs/pallas_call | solution.py:657
  109.7 4.0 %all-to-all-start.3 = ((bf16[128,8,384]{2,1,0:T(8,128)(2,1)}), bf16[128,8,384]{2,1,0:T(8,128)(2,1)S(1)}, u32[]{:S(2)}, u32[]{:S(2)}) async-start(bf16[128,8,384]{2,1,0:T(8,128)(2,1)} %bitcast.16), calls=%async_computation.3 | async-start | bytes 1572864 | tf_op jit(solution)/shard_map/all_to_all | solution.py:687
  113.7 5.2 %divide_multiply_fusion.gate = f32[128,3072]{1,0:T(8,128)S(1)} fusion(bf16[128,1536]{1,0:T(8,128)(2,1)S(1)} %copy-done.5, bf16[1536,3072]{1,0:T(8,128)(2,1)} %param.16), kind=kOutput, calls=%fused_computation | convolution fusion | flops 1209532416 | bytes 11403264 | tf_op jit(solution)/shard_map/dot_general | solution.py:567
  118.8 11.7 %all-to-all-done.3 = bf16[128,8,384]{2,1,0:T(8,128)(2,1)S(1)} async-done(((bf16[128,8,384]{2,1,0:T(8,128)(2,1)}), bf16[128,8,384]{2,1,0:T(8,128)(2,1)S(1)}, u32[]{:S(2)}, u32[]{:S(2)}) %all-to-all-start.3) | async-done | bytes 786464 | tf_op jit(solution)/shard_map/all_to_all | solution.py:687
  130.6 1.2 gated.1
  (11 shorter events, 0.1 us)
Async XLA Ops:
  0.0 13.9 %copy-start.6 = (s32[4]{0:T(128)S(1)}, s32[4]{0:T(128)}, u32[]{:S(2)}) copy-start(s32[4]{0:T(128)} %param.14) | copy-start | bytes 52
  0.0 16.0 %copy-start.4 = (f32[2,16,3072]{2,1,0:T(8,128)S(1)}, f32[2,16,3072]{2,1,0:T(8,128)}, u32[]{:S(2)}) copy-start(f32[2,16,3072]{2,1,0:T(8,128)} %param.22) | copy-start | bytes 1179652
  0.0 35.5 %copy-start = (f32[2,4,3072]{2,1,0:T(4,128)S(1)}, f32[2,4,3072]{2,1,0:T(4,128)}, u32[]{:S(2)}) copy-start(f32[2,4,3072]{2,1,0:T(4,128)} %conv_weight.3) | copy-start | bytes 294916
  0.0 35.5 %copy-start.2 = (f32[2,3072]{1,0:T(2,128)S(1)}, f32[2,3072]{1,0:T(2,128)}, u32[]{:S(2)}) copy-start(f32[2,3072]{1,0:T(2,128)} %conv_bias.1) | copy-start | bytes 73732
  2.3 25.5 %all-to-all-start = ((bf16[128,8,256]{2,1,0:T(8,128)(2,1)}), bf16[128,8,256]{2,1,0:T(8,128)(2,1)S(1)}, u32[]{:S(2)}, u32[]{:S(2)}) async-start(bf16[128,8,256]{2,1,0:T(8,128)(2,1)} %bitcast.3), calls=%async_computation | async-start | bytes 1048576 | tf_op jit(solution)/shard_map/all_to_all | solution.py:564
  28.7 12.7 %collective-permute-start = (bf16[8,1536]{1,0:T(8,128)(2,1)S(1)}, bf16[8,1536]{1,0:T(8,128)(2,1)S(1)}, u32[]{:S(2)}, u32[]{:S(2)}) collective-permute-start(bf16[8,1536]{1,0:T(8,128)(2,1)S(1)} %get-tuple-element.23), channel_id=1, source_target_pairs={{0,1},{1,2},{2,3},{3,4},{4,5},{5,6},{6,7},{7,8},{8,9},{9,10},{10,1... | collective-permute-start | bytes 73736 | tf_op jit(solution)/shard_map/ppermute | solution.py:582
  30.9 10.5 %collective-permute-start.1 = (bf16[8,1536]{1,0:T(8,128)(2,1)S(1)}, bf16[8,1536]{1,0:T(8,128)(2,1)S(1)}, u32[]{:S(2)}, u32[]{:S(2)}) collective-permute-start(bf16[8,1536]{1,0:T(8,128)(2,1)S(1)} %get-tuple-element.24), channel_id=1, source_target_pairs={{1,0},{2,1},{3,2},{4,3},{5,4},{6,5},{7,6},{8,7},{9,8},{10,9},{11,1... | collective-permute-start | bytes 73736 | tf_op jit(solution)/shard_map/ppermute | solution.py:583
  35.6 5.9 %copy-start.1 = (f32[2,3072]{1,0:T(2,128)S(1)}, f32[2,3072]{1,0:T(2,128)}, u32[]{:S(2)}) copy-start(f32[2,3072]{1,0:T(2,128)} %dt_bias.1) | copy-start | bytes 73732
  59.0 34.3 %copy-start.3 = (f32[2,3072]{1,0:T(2,128)S(1)}, f32[2,3072]{1,0:T(2,128)}, u32[]{:S(2)}) copy-start(f32[2,3072]{1,0:T(2,128)} %skip_gain.1) | copy-start | bytes 73732
  59.0 18.7 %all-to-all-start.1 = ((bf16[128,4,384]{2,1,0:T(4,128)(2,1)}), bf16[128,4,384]{2,1,0:T(4,128)(2,1)S(1)}, u32[]{:S(2)}, u32[]{:S(2)}) async-start(bf16[128,4,384]{2,1,0:T(4,128)(2,1)} %bitcast.17), calls=%async_computation.1 | async-start | bytes 786432 | tf_op jit(solution)/shard_map/all_to_all | solution.py:642
  109.7 4.0 %copy-start.5 = (bf16[128,1536]{1,0:T(8,128)(2,1)S(1)}, bf16[128,1536]{1,0:T(8,128)(2,1)}, u32[]{:S(2)}) copy-start(bf16[128,1536]{1,0:T(8,128)(2,1)} %embed.1) | copy-start | bytes 1179652
  109.7 20.9 %all-to-all-start.3 = ((bf16[128,8,384]{2,1,0:T(8,128)(2,1)}), bf16[128,8,384]{2,1,0:T(8,128)(2,1)S(1)}, u32[]{:S(2)}, u32[]{:S(2)}) async-start(bf16[128,8,384]{2,1,0:T(8,128)(2,1)} %bitcast.16), calls=%async_computation.3 | async-start | bytes 1572864 | tf_op jit(solution)/shard_map/all_to_all | solution.py:687

commit v5 on v4

--- a/solution.py
+++ b/solution.py
@@ -190,10 +190,13 @@
 
 
 def spread_columns(target, columns, first, count):
+    row = lax.broadcasted_iota(jnp.int32, (2 * count, count * LANES), 0)
+    at = lax.broadcasted_iota(jnp.int32, (2 * count, count * LANES), 1)
+    repeat = (row % count == at // LANES).astype(jnp.float32).astype(jnp.bfloat16)
+    parts = [part[:, first : first + count] for part in halves(columns)]
+    wide = matmul(jnp.concatenate(parts, axis=1), repeat)
     for n in range(count):
-        target[n] = jnp.broadcast_to(
-            columns[:, first + n : first + n + 1], (columns.shape[0], LANES)
-        )
+        target[n] = wide[:, LANES * n : LANES * n + LANES]
 
 
 def silu(v):
@@ -244,12 +247,14 @@
     proj_result,
     dt_result,
     payload_result,
-    entry_result,
+    ends_result,
+    span_result,
     u_out,
     proj_out,
     dt_out,
     payload,
-    entry,
+    ends,
+    span,
     b_wide,
     edge_rows,
     sems,
@@ -279,8 +284,14 @@
     edge_rows[SUB:] = after[...]
     row = sublane((SUB, width))
     projected = [jnp.zeros((edge, LANES), jnp.float32)] * 2
+    inside = [slice(edge, rows), slice(0, rows - edge)]
+    outermost = [slice(0, edge), slice(rows - edge, rows)]
+    low = [as_bf16(proj_in[d, inside[d]][:, :rank]) for d in range(2)]
     for step in range(channels // width):
         cols = slice(step * width, step * width + width)
+        for d in range(2):
+            raw = matmul(low[d], dt_project[d, :, cols])
+            dt_out[d, inside[d], cols] = softplus(raw + dt_bias[d : d + 1, cols])
         edges = as_bf16(matmul(edge_rows[...], w_inner[:, cols])).astype(jnp.float32)
         prior = edges[:SUB] * flags[0].astype(jnp.float32)
         later = edges[SUB:] * flags[1].astype(jnp.float32)
@@ -307,15 +318,10 @@
     for d in range(2):
         spread_columns(b_wide.at[d], proj_out[d], rank, states)
 
-    def step_block(step, carry):
-        cols = pl.ds(pl.multiple_of(step * width, LANES), width)
-        for d in range(2):
-            low = as_bf16(proj_out[d][:, :rank])
-            raw = matmul(low, dt_project[d, :, cols])
-            dt_out[d, :, cols] = softplus(raw + dt_bias[d : d + 1, cols])
-        return carry
-
-    lax.fori_loop(0, channels // width, step_block, 0)
+    for d in range(2):
+        low = as_bf16(projected[d][:, :rank])
+        raw = matmul(low, dt_project[d])
+        dt_out[d, outermost[d]] = softplus(raw + dt_bias[d : d + 1])
     copies[2].start()
     row = sublane((SUB, LANES))
 
@@ -330,7 +336,8 @@
         total = dt[0]
         for t in range(1, slots):
             total = total + dt[t]
-        near = in_reach(1, reverse)
+        span[d, :, here] = total
+        after_it = outside(total, not reverse)
         finals = []
         for n in range(states):
             rate = rates[d, n : n + 1, here]
@@ -340,14 +347,9 @@
                 if state is not None:
                     new = jnp.exp2(dt[t] * rate) * state + new
                 state = new
-            keep = jnp.exp2(total * rate)
-            for count in (1, 2, 4):
-                keep = jnp.where(in_reach(count, reverse), keep, 0.0)
-                state = state + keep * shift_sublanes(state, count, reverse)
-                if count < 4:
-                    keep = keep * shift_sublanes(keep, count, reverse)
-            entry[d, n, :, here] = jnp.where(near, shift_sublanes(state, 1, reverse), 0.0)
-            finals.append(state[0:1] if reverse else state[SUB - 1 : SUB])
+            ends[d, n, :, here] = state
+            state = jnp.exp2(after_it * rate) * state
+            finals.append(jnp.sum(state, axis=0, keepdims=True))
         whole = jnp.sum(total, axis=0, keepdims=True)
         for n in range(0, states, 2):
             out = jnp.where(row == 0, finals[n], finals[n + 1])
@@ -363,15 +365,35 @@
             cols = pl.ds(part * thirds * LANES, thirds * LANES)
             copies.append(
                 pltpu.make_async_copy(
-                    entry.at[d, :, :, cols],
-                    entry_result.at[d, :, :, cols],
+                    ends.at[d, :, :, cols],
+                    ends_result.at[d, :, :, cols],
                     sems.at[5 + 3 * d + part],
                 )
             )
             copies[-1].start()
         copies[3 + d].start()
+    copies.append(pltpu.make_async_copy(span, span_result, sems.at[11]))
+    copies[-1].start()
     for copy in copies:
         copy.wait()
+
+
+def entry_kernel(ends, span, rates, entry):
+    states = rates.shape[1]
+    for at in range(0, span.shape[2], LANES):
+        here = slice(at, at + LANES)
+        for d in range(2):
+            reverse = d == 1
+            near = in_reach(1, reverse)
+            for n in range(states):
+                state = ends[d, n, :, here]
+                keep = jnp.exp2(span[d, :, here] * rates[d, n : n + 1, here])
+                for count in (1, 2, 4):
+                    keep = jnp.where(in_reach(count, reverse), keep, 0.0)
+                    state = state + keep * shift_sublanes(state, count, reverse)
+                    if count < 4:
+                        keep = keep * shift_sublanes(keep, count, reverse)
+                entry[d, n, :, here] = jnp.where(near, shift_sublanes(state, 1, reverse), 0.0)
 
 
 def relay_kernel(keep, payload, rates, entering):
@@ -424,13 +446,9 @@
         group = block // (tile // LANES)
         within = pl.multiple_of((block - group * (tile // LANES)) * LANES, LANES)
         reverse = d == 1
-        dt = dt_in[d, :, here]
-        u = u_in[d, :, here].astype(jnp.float32)
-        fed = tiles_of(dt * u)
-        dt = tiles_of(dt)
-        total = dt[0]
+        total = dt_in[d, :SUB, here]
         for t in range(1, slots):
-            total = total + dt[t]
+            total = total + dt_in[d, SUB * t : SUB * t + SUB, here]
         ahead = outside(total, reverse)
         state = []
         for n in range(states):
@@ -440,18 +458,23 @@
         sums = [None] * (slots // 2)
         for k in in_order(slots // 2, reverse):
             right = []
+            two = slice(PACK * k, PACK * k + PACK)
+            u = u_in[d, two, here].astype(jnp.float32)
+            dt = dt_in[d, two, here]
+            fed = tiles_of(dt * u)
+            dt = tiles_of(dt)
             for n in range(states):
                 rate = rates[d, n : n + 1, here]
                 both = []
                 for t in in_order(2, reverse):
-                    t = 2 * k + t
-                    new = fed[t] * b_wide[d, n, SUB * t : SUB * t + SUB]
+                    first = PACK * k + SUB * t
+                    new = fed[t] * b_wide[d, n, first : first + SUB]
                     state[n] = jnp.exp2(dt[t] * rate) * state[n] + new
                     both.append(state[n])
                 right.append(paired(*(both[::-1] if reverse else both)))
             part = matmul(left[d, k], jnp.concatenate(right, axis=0))
-            sums[k] = part[:PACK] + part[PACK:]
-        return jnp.concatenate(sums, axis=0) + skip_gain[d : d + 1, here] * u
+            sums[k] = part[:PACK] + part[PACK:] + skip_gain[d : d + 1, here] * u
+        return jnp.concatenate(sums, axis=0)
 
     pick = one_hot(places[...])
     for at in range(channels // LANES):
@@ -615,9 +638,10 @@
         pltpu.VMEM((2, rows, width), f32),
         pltpu.VMEM((2, state_groups, groups, 4, tile), bf16),
         pltpu.VMEM((2, states, SUB, width), f32),
+        pltpu.VMEM((2, SUB, width), f32),
         pltpu.VMEM((2, states, rows, LANES), f32),
     ]
-    u, proj, dt, payload, entry, _ = pl.pallas_call(
+    u, proj, dt, payload, ends, span, _ = pl.pallas_call(
         states_kernel,
         out_shape=(
             pltpu.HBM((2, rows, width), bf16),
@@ -625,23 +649,39 @@
             pltpu.HBM((2, rows, width), f32),
             pltpu.HBM((2, state_groups, groups, 4, tile), bf16),
             pltpu.HBM((2, states, SUB, width), f32),
+            pltpu.HBM((2, SUB, width), f32),
             pltpu.VMEM((2, rows, width), bf16),
         ),
         in_specs=[pl.BlockSpec(memory_space=pltpu.SMEM)] + [vmem_spec] * len(operands),
-        out_specs=(hbm_spec,) * 5 + (vmem_spec,),
-        input_output_aliases={len(operands): 5},
+        out_specs=(hbm_spec,) * 6 + (vmem_spec,),
+        input_output_aliases={len(operands): 6},
         scratch_shapes=on_chip_results
         + [
             pltpu.VMEM((2 * SUB, model), bf16),
-            pltpu.SemaphoreType.DMA((11,)),
+            pltpu.SemaphoreType.DMA((12,)),
         ],
         compiler_params=limits(14),
         name="block_states",
     )(flags, *(in_vmem(operand) for operand in operands))
 
+    part = 4 * LANES
     shared = lax.all_to_all(
         payload.reshape(shards, 4, tile), AXES, split_axis=0, concat_axis=0, tiled=True
     )
+    entry = pl.pallas_call(
+        entry_kernel,
+        out_shape=pltpu.HBM((2, states, SUB, width), f32),
+        grid=(width // part,),
+        in_specs=[
+            pl.BlockSpec((2, states, SUB, part), lambda i: (0, 0, 0, i)),
+            pl.BlockSpec((2, SUB, part), lambda i: (0, 0, i)),
+            pl.BlockSpec((2, states, part), lambda i: (0, 0, i)),
+        ],
+        out_specs=pl.BlockSpec((2, states, SUB, part), lambda i: (0, 0, 0, i)),
+        compiler_params=limits(3),
+        name="entries",
+    )(in_hbm(ends), in_hbm(span), rates)
+    shared, entry = lax.optimization_barrier((shared, entry))
     entering = on_chip(
         relay_kernel,
         "relay",
@@ -653,7 +693,6 @@
     entering = lax.all_to_all(entering, AXES, split_axis=0, concat_axis=0, tiled=True)
     entering = entering.reshape(2, state_groups, groups, owner_states, tile)
 
-    part = 4 * LANES
     totals = pl.pallas_call(
         outputs_kernel,
         out_shape=pltpu.HBM((SUB * rows, tile), bf16),

time: 132 us -> 130 us (0.985)
  waiting for transfers between devices: 35.9 us -> 29.8 us
  Pallas kernels: 45.3 us -> 49.5 us
    all_to_all x1, waiting for transfers between devices: 12.5 us -> 6.35 us  [local(): lax.all_to_all(payload.reshape(shards, 4, tile), AXES, split_axis=0, conc...]
    pallas_call x0 -> x1, Pallas kernels: none -> 6.12 us  [local(): pl.pallas_call(entry_kernel, out_shape=pltpu.HBM((2, states, SUB, width),...]
    pallas_call x1, Pallas kernels: 17.6 us -> 15.7 us  [local(): pl.pallas_call(states_kernel, out_shape=(pltpu.HBM((2, rows, width), bf16...]
  transfers between devices with their start and end apart: 5 -> 5, of which waited for: 3 -> 3; matrix products, arithmetic and copies ran while one was open for 5% -> 5% of each run, Pallas kernels for 4% -> 9%
where the time goes in v5:
time: 130 us
  Pallas kernels  49.5 us (38%)
  waiting for transfers between devices  29.8 us (23%)
  starting transfers between devices  28.3 us (22%)
  blocking collectives  14.4 us (11%)
  matrix products  5.16 us (4%)
  between operations  1.52 us (1%)
    pallas_call x1, Pallas kernels, local(): pl.pallas_call(outputs_kernel, out_shape=pltpu.HBM((SUB * rows, tile), bf...  16.2 us
    pallas_call x1, Pallas kernels, local(): pl.pallas_call(states_kernel, out_shape=(pltpu.HBM((2, rows, width), bf16...  15.7 us
    all_to_all x1, blocking collectives, local(): lax.all_to_all(entering, AXES, split_axis=0, concat_axis=0, tiled=True)  14.4 us
    all_to_all x1, waiting for transfers between devices, local(): lax.all_to_all(totals.reshape(rows, SUB, tile), AXES, split_axis=0, conca...  11.7 us
    all_to_all x1, waiting for transfers between devices, local(): lax.all_to_all(sent.reshape(rows, SUB, piece), AXES, split_axis=0, concat...  11.7 us
    all_to_all x1, starting transfers between devices, local(): lax.all_to_all(sent.reshape(rows, SUB, piece), AXES, split_axis=0, concat...  11.5 us
    all_to_all x1, waiting for transfers between devices, local(): lax.all_to_all(payload.reshape(shards, 4, tile), AXES, split_axis=0, conc...  6.35 us
    pallas_call x1, Pallas kernels, local(): pl.pallas_call(entry_kernel, out_shape=pltpu.HBM((2, states, SUB, width),...  6.12 us
  transfers between devices with their start and end apart: 5, of which 3 were waited for; matrix products, arithmetic and copies ran while one was open for 5% of the time, Pallas kernels for 9%

profile of v5, /device:TPU:1, one launch (start us, length us, event | category | flops | bytes accessed | tf_op | source)
XLA Modules:
  0.0 129.8 jit_solution(14226318857209019027)
XLA Ops:
  0.0 0.0 copy-start.2
  0.0 2.3 %pack.1 = bf16[1024,256]{1,0:T(8,128)(2,1)} custom-call(bf16[128,1536]{1,0:T(8,128)(2,1)} %embed.1, s32[1,128]{1,0:T(1,128)} %bitcast.18), custom_call_target="tpu_custom_call" | custom-call | tf_op jit(solution)/shard_map/pack/pallas_call | solution.py:581
  2.3 11.5 %all-to-all-start = ((bf16[128,8,256]{2,1,0:T(8,128)(2,1)}), bf16[128,8,256]{2,1,0:T(8,128)(2,1)S(1)}, u32[]{:S(2)}, u32[]{:S(2)}) async-start(bf16[128,8,256]{2,1,0:T(8,128)(2,1)} %bitcast.3), calls=%async_computation | async-start | bytes 1048576 | tf_op jit(solution)/shard_map/all_to_all | solution.py:587
  13.8 0.0 copy-done.6
  13.9 0.1 select_reduce_fusion
  14.0 0.1 compare_reduce_fusion
  14.0 0.7 and_reduce_fusion.1
  16.0 0.0 copy-done.4
  16.1 11.7 %all-to-all-done = bf16[128,8,256]{2,1,0:T(8,128)(2,1)S(1)} async-done(((bf16[128,8,256]{2,1,0:T(8,128)(2,1)}), bf16[128,8,256]{2,1,0:T(8,128)(2,1)S(1)}, u32[]{:S(2)}, u32[]{:S(2)}) %all-to-all-start) | async-done | bytes 524320 | tf_op jit(solution)/shard_map/all_to_all | solution.py:587
  27.8 0.9 sort_rows.1
  28.7 2.2 %collective-permute-start = (bf16[8,1536]{1,0:T(8,128)(2,1)S(1)}, bf16[8,1536]{1,0:T(8,128)(2,1)S(1)}, u32[]{:S(2)}, u32[]{:S(2)}) collective-permute-start(bf16[8,1536]{1,0:T(8,128)(2,1)S(1)} %get-tuple-element.26), channel_id=1, source_target_pairs={{0,1},{1,2},{2,3},{3,4},{4,5},{5,6},{6,7},{7,8},{8,9},{9,10},{10,1... | collective-permute-start | bytes 73736 | tf_op jit(solution)/shard_map/ppermute | solution.py:605
  30.9 4.6 %collective-permute-start.1 = (bf16[8,1536]{1,0:T(8,128)(2,1)S(1)}, bf16[8,1536]{1,0:T(8,128)(2,1)S(1)}, u32[]{:S(2)}, u32[]{:S(2)}) collective-permute-start(bf16[8,1536]{1,0:T(8,128)(2,1)S(1)} %get-tuple-element.27), channel_id=1, source_target_pairs={{1,0},{2,1},{3,2},{4,3},{5,4},{6,5},{7,6},{8,7},{9,8},{10,9},{11,1... | collective-permute-start | bytes 73736 | tf_op jit(solution)/shard_map/ppermute | solution.py:606
  35.5 0.1 add_convert_fusion.flags
  35.5 0.0 copy-done
  35.5 0.0 copy-done.2
  35.5 5.9 %inner.1 = (bf16[2,128,3072]{2,1,0:T(8,128)(2,1)S(1)}, f32[2,128,128]{2,1,0:T(8,128)S(1)}, f32[2,24,3072]{2,1,0:T(8,128)S(1)}, bf16[1536,3072]{1,0:T(8,128)(2,1)...) custom-call(bf16[128,1536]{1,0:T(8,128)(2,1)S(1)} %get-tuple-element.23.rows_in, ...), custom_call_target="tpu_custom_call" | custom-call | tf_op jit(solution)/shard_map/inner/pallas_call | solution.py:617
  41.4 0.0 collective-permute-done.before
  41.4 0.0 collective-permute-done.1.after
  41.4 0.0 copy-done.1
  41.5 15.7 %block_states.1 = (bf16[2,128,3072]{2,1,0:T(8,128)(2,1)}, f32[2,128,128]{2,1,0:T(8,128)}, f32[2,128,3072]{2,1,0:T(8,128)}, bf16[2,8,8,4,384]{4,3,2,1,0:T(4,128)(...) custom-call(s32[2]{0:T(128)S(1)} %add_convert_fusion.flags, ...), custom_call_target="tpu_custom_call", output_to_operand_aliasing={{6}: (11, {})} | custom-call | tf_op jit(solution)/shard_map/block_states/pallas_call | solution.py:644
  57.2 6.1 %all-to-all-start.1 = ((bf16[128,4,384]{2,1,0:T(4,128)(2,1)}), bf16[128,4,384]{2,1,0:T(4,128)(2,1)S(1)}, u32[]{:S(2)}, u32[]{:S(2)}) async-start(bf16[128,4,384]{2,1,0:T(4,128)(2,1)} %bitcast.17), calls=%async_computation.1 | async-start | bytes 786432 | tf_op jit(solution)/shard_map/all_to_all | solution.py:668
  63.3 0.1 dynamic-slice_bitcast_fusion.rates
  63.4 6.1 %entries.1.entry = f32[2,16,8,3072]{3,2,1,0:T(8,128)} custom-call(f32[2,16,8,3072]{3,2,1,0:T(8,128)} %get-tuple-element.33.ends, f32[2,8,3072]{2,1,0:T(8,128)} %get-tuple-element.34.span, f32[2,16,3072]{2,1,0:T(8,128)S(1)} %broadcast_multiply_fusion.rates), custom_call_target="tpu_custom_call" | custom-call | tf_op jit(solution)/shard_map/entries/pallas_call | solution.py:671
  69.5 6.4 %all-to-all-done.1.payload = bf16[128,4,384]{2,1,0:T(4,128)(2,1)S(1)} async-done(((bf16[128,4,384]{2,1,0:T(4,128)(2,1)}), bf16[128,4,384]{2,1,0:T(4,128)(2,1)S(1)}, u32[]{:S(2)}, u32[]{:S(2)}) %all-to-all-start.1) | async-done | bytes 393248 | tf_op jit(solution)/shard_map/all_to_all | solution.py:668
  75.9 1.2 relay.1
  77.1 14.4 %all_to_all.20 = bf16[128,2,384]{2,1,0:T(2,128)(2,1)S(1)} all-to-all(bf16[128,2,384]{2,1,0:T(2,128)(2,1)S(1)} %relay.1), channel_id=1, replica_groups=mesh['seq'=32,'slide'=4] {'seq','slide'}, dimensions={0} | all-to-all | bytes 393216 | tf_op jit(solution)/shard_map/all_to_all | solution.py:693
  91.5 0.0 copy-done.3
  91.5 16.2 %block_outputs.1 = bf16[1024,384]{1,0:T(8,128)(2,1)} custom-call(bf16[2,8,8,2,384]{4,3,2,1,0:T(2,128)(2,1)S(1)} %bitcast.15, f32[2,16,8,3072]{3,2,1,0:T(8,128)} %entries.1.entry, f32[2,128,3072]{2,1,0:T(8,128)} %get-tuple-element.37.dt_in, bf16[2,128,3072]{2,1,0:T(8,128)(2,1)} %get-tuple-element.38.u_in, f32[2,128,128]{2,1,0:T(8,128)} %get-tuple-element.39.proj, ...), custom_call_target="tpu_custom_call" | custom-call | tf_op jit(solution)/shard_map/block_outputs/pallas_call | solution.py:696
  107.7 4.0 %all-to-all-start.3 = ((bf16[128,8,384]{2,1,0:T(8,128)(2,1)}), bf16[128,8,384]{2,1,0:T(8,128)(2,1)S(1)}, u32[]{:S(2)}, u32[]{:S(2)}) async-start(bf16[128,8,384]{2,1,0:T(8,128)(2,1)} %bitcast.16), calls=%async_computation.3 | async-start | bytes 1572864 | tf_op jit(solution)/shard_map/all_to_all | solution.py:726
  111.7 5.2 %divide_multiply_fusion.gate = f32[128,3072]{1,0:T(8,128)S(1)} fusion(bf16[128,1536]{1,0:T(8,128)(2,1)S(1)} %copy-done.5, bf16[1536,3072]{1,0:T(8,128)(2,1)} %param.16), kind=kOutput, calls=%fused_computation | convolution fusion | flops 1209532416 | bytes 11403264 | tf_op jit(solution)/shard_map/dot_general | solution.py:590
  116.9 11.7 %all-to-all-done.3 = bf16[128,8,384]{2,1,0:T(8,128)(2,1)S(1)} async-done(((bf16[128,8,384]{2,1,0:T(8,128)(2,1)}), bf16[128,8,384]{2,1,0:T(8,128)(2,1)S(1)}, u32[]{:S(2)}, u32[]{:S(2)}) %all-to-all-start.3) | async-done | bytes 786464 | tf_op jit(solution)/shard_map/all_to_all | solution.py:726
  128.6 1.2 gated.1
  (12 shorter events, 0.1 us)
Async XLA Ops:
  0.0 13.9 %copy-start.6 = (s32[4]{0:T(128)S(1)}, s32[4]{0:T(128)}, u32[]{:S(2)}) copy-start(s32[4]{0:T(128)} %param.14) | copy-start | bytes 52
  0.0 16.0 %copy-start.4 = (f32[2,16,3072]{2,1,0:T(8,128)S(1)}, f32[2,16,3072]{2,1,0:T(8,128)}, u32[]{:S(2)}) copy-start(f32[2,16,3072]{2,1,0:T(8,128)} %param.22) | copy-start | bytes 1179652
  0.0 35.5 %copy-start = (f32[2,4,3072]{2,1,0:T(4,128)S(1)}, f32[2,4,3072]{2,1,0:T(4,128)}, u32[]{:S(2)}) copy-start(f32[2,4,3072]{2,1,0:T(4,128)} %conv_weight.3) | copy-start | bytes 294916
  0.0 35.5 %copy-start.2 = (f32[2,3072]{1,0:T(2,128)S(1)}, f32[2,3072]{1,0:T(2,128)}, u32[]{:S(2)}) copy-start(f32[2,3072]{1,0:T(2,128)} %conv_bias.1) | copy-start | bytes 73732
  2.3 25.5 %all-to-all-start = ((bf16[128,8,256]{2,1,0:T(8,128)(2,1)}), bf16[128,8,256]{2,1,0:T(8,128)(2,1)S(1)}, u32[]{:S(2)}, u32[]{:S(2)}) async-start(bf16[128,8,256]{2,1,0:T(8,128)(2,1)} %bitcast.3), calls=%async_computation | async-start | bytes 1048576 | tf_op jit(solution)/shard_map/all_to_all | solution.py:587
  28.7 12.7 %collective-permute-start = (bf16[8,1536]{1,0:T(8,128)(2,1)S(1)}, bf16[8,1536]{1,0:T(8,128)(2,1)S(1)}, u32[]{:S(2)}, u32[]{:S(2)}) collective-permute-start(bf16[8,1536]{1,0:T(8,128)(2,1)S(1)} %get-tuple-element.26), channel_id=1, source_target_pairs={{0,1},{1,2},{2,3},{3,4},{4,5},{5,6},{6,7},{7,8},{8,9},{9,10},{10,1... | collective-permute-start | bytes 73736 | tf_op jit(solution)/shard_map/ppermute | solution.py:605
  30.9 10.5 %collective-permute-start.1 = (bf16[8,1536]{1,0:T(8,128)(2,1)S(1)}, bf16[8,1536]{1,0:T(8,128)(2,1)S(1)}, u32[]{:S(2)}, u32[]{:S(2)}) collective-permute-start(bf16[8,1536]{1,0:T(8,128)(2,1)S(1)} %get-tuple-element.27), channel_id=1, source_target_pairs={{1,0},{2,1},{3,2},{4,3},{5,4},{6,5},{7,6},{8,7},{9,8},{10,9},{11,1... | collective-permute-start | bytes 73736 | tf_op jit(solution)/shard_map/ppermute | solution.py:606
  35.5 5.9 %copy-start.1 = (f32[2,3072]{1,0:T(2,128)S(1)}, f32[2,3072]{1,0:T(2,128)}, u32[]{:S(2)}) copy-start(f32[2,3072]{1,0:T(2,128)} %dt_bias.1) | copy-start | bytes 73732
  57.2 18.7 %all-to-all-start.1 = ((bf16[128,4,384]{2,1,0:T(4,128)(2,1)}), bf16[128,4,384]{2,1,0:T(4,128)(2,1)S(1)}, u32[]{:S(2)}, u32[]{:S(2)}) async-start(bf16[128,4,384]{2,1,0:T(4,128)(2,1)} %bitcast.17), calls=%async_computation.1 | async-start | bytes 786432 | tf_op jit(solution)/shard_map/all_to_all | solution.py:668
  63.4 28.1 %copy-start.3 = (f32[2,3072]{1,0:T(2,128)S(1)}, f32[2,3072]{1,0:T(2,128)}, u32[]{:S(2)}) copy-start(f32[2,3072]{1,0:T(2,128)} %skip_gain.1) | copy-start | bytes 73732
  107.7 4.0 %copy-start.5 = (bf16[128,1536]{1,0:T(8,128)(2,1)S(1)}, bf16[128,1536]{1,0:T(8,128)(2,1)}, u32[]{:S(2)}) copy-start(bf16[128,1536]{1,0:T(8,128)(2,1)} %embed.1) | copy-start | bytes 1179652
  107.7 20.9 %all-to-all-start.3 = ((bf16[128,8,384]{2,1,0:T(8,128)(2,1)}), bf16[128,8,384]{2,1,0:T(8,128)(2,1)S(1)}, u32[]{:S(2)}, u32[]{:S(2)}) async-start(bf16[128,8,384]{2,1,0:T(8,128)(2,1)} %bitcast.16), calls=%async_computation.3 | async-start | bytes 1572864 | tf_op jit(solution)/shard_map/all_to_all | solution.py:726

commit v6 on v5

--- a/solution.py
+++ b/solution.py
@@ -70,33 +70,35 @@
     return hit.astype(jnp.float32).astype(jnp.bfloat16)
 
 
-def sort_kernel(arrived, sorted_rows, ahead, behind, places, plain):
-    rows = sorted_rows.shape[0]
+def edges_kernel(arrived, plain, first_out, second_out):
+    rows = plain.shape[0]
     group = rows // SUB
     width = arrived.shape[1]
-    pieces = sorted_rows.shape[1] // width
+    pieces = plain.shape[1] // width
     gather = spread_index(rows, turned=True)
     for q in range(SUB):
         part = as_bf16(matmul(gather, arrived[rows * q : rows * q + rows]))
-        for k in range(pieces + 1):
+        for k in range(pieces):
             plain[group * q : group * q + group, width * k : width * k + width] = part[
                 group * k : group * k + group
             ]
-    pos = plain[:, width * pieces : width * pieces + LANES].astype(jnp.float32)
-    places[...] = pos
+    model = width * (pieces - 1)
+    pos = plain[:, model : model + LANES].astype(jnp.float32)
     lane = lax.broadcasted_iota(jnp.int32, pos.shape, 1)
-    edge = jnp.where(lane < SUB, lane + rows - 3, lane - SUB)
+    ahead = lane + rows - 3
+    behind = lane % SUB
+    odd = lax.axis_index(AXES[1]) % 2
+    early = lane < SUB
+    edge = jnp.where(early == (odd == 0), jnp.where(early, ahead, ahead - SUB), behind)
     edge = jnp.where((lane % SUB < 3) & (lane < 2 * SUB), edge, -1)
     hit = (pos.astype(jnp.int32) == edge).astype(jnp.float32).astype(jnp.bfloat16)
-    data = plain[:, : width * pieces]
-    ends = as_bf16(over_rows(hit, data))
-    ahead[...] = ends[:SUB]
-    behind[...] = ends[SUB : 2 * SUB]
-    sorted_rows[...] = as_bf16(over_rows(one_hot(pos), data))
+    ends = as_bf16(over_rows(hit, plain[:, :model]))
+    first_out[...] = ends[:SUB]
+    second_out[...] = ends[SUB : 2 * SUB]
 
 
 def inner_kernel(
-    rows_in,
+    plain,
     conv_weight,
     conv_bias,
     weight,
@@ -108,12 +110,15 @@
     weight_here,
     x_here,
     dt_here,
+    places_result,
+    rows_in,
+    places,
     extended,
     sems,
 ):
-    parts = sems.shape[0] - 2
+    parts = sems.shape[0] - 3
     width = weight.shape[1] // parts
-    rows = rows_in.shape[0]
+    rows, model = rows_in.shape
     taps = conv_weight.shape[1]
     reach = taps - 1
     slots = rows // SUB
@@ -129,6 +134,11 @@
     ]
     for copy in copies:
         copy.start()
+    pos = plain[:, model : model + LANES].astype(jnp.float32)
+    places[...] = pos
+    copies.append(pltpu.make_async_copy(places, places_result, sems.at[parts + 2]))
+    copies[-1].start()
+    rows_in[...] = as_bf16(over_rows(one_hot(pos), plain[:, :model]))
     proj_out[...] = jnp.zeros_like(proj_out)
     row = sublane((SUB, width))
     for k in range(parts):
@@ -159,6 +169,7 @@
             u_out[d, :, cols] = u
             proj_out[d] += matmul(u, x_here[d, cols, :])
     copies[parts + 1].wait()
+    copies[parts + 2].wait()
 
 
 def sublane(shape):
@@ -234,8 +245,8 @@
     flags,
     proj_in,
     edge_sums,
-    before,
-    after,
+    first_in,
+    second_in,
     w_inner,
     conv_weight,
     x_project,
@@ -280,8 +291,9 @@
     slots = rows // SUB
     tile = payload.shape[4]
     edge = SUB * reach
-    edge_rows[:SUB] = before[...]
-    edge_rows[SUB:] = after[...]
+    even = flags[2] == 0
+    edge_rows[:SUB] = jnp.where(even, second_in[...], first_in[...])
+    edge_rows[SUB:] = jnp.where(even, first_in[...], second_in[...])
     row = sublane((SUB, width))
     projected = [jnp.zeros((edge, LANES), jnp.float32)] * 2
     inside = [slice(edge, rows), slice(0, rows - edge)]
@@ -566,7 +578,7 @@
     opens = jnp.any(blocks[:, None] * rows == starts[None, :], axis=1)
     closes = jnp.any((blocks[:, None] + 1) * rows == ends[None, :], axis=1)
     mine = blocks == me
-    flags = jnp.stack([~jnp.any(opens & mine), ~jnp.any(closes & mine)]).astype(jnp.int32)
+    flags = jnp.stack([~jnp.any(opens & mine), ~jnp.any(closes & mine), me % 2 == 1]).astype(jnp.int32)
     owner_dir = me // (state_groups * groups)
     owner_group = (me // groups) % state_groups
     owner_tile = me % groups
@@ -589,21 +601,21 @@
     ).reshape(SUB * rows, piece)
     gate = jax.nn.silu(jnp.dot(tile_embed, w_gate, preferred_element_type=f32))
 
-    block_rows, ahead, behind, places = on_chip(
-        sort_kernel,
-        "sort_rows",
-        4,
+    plain, first_out, second_out = on_chip(
+        edges_kernel,
+        "edges",
+        3,
         (
-            pltpu.VMEM((rows, model), bf16),
+            pltpu.VMEM((rows, model + piece), bf16),
             pltpu.VMEM((SUB, model), bf16),
             pltpu.VMEM((SUB, model), bf16),
-            pltpu.HBM((rows, LANES), f32),
         ),
         arrived,
-        scratch=[pltpu.VMEM((rows, model + piece), bf16)],
-    )
-    before = lax.ppermute(ahead, AXES, [(i, i + 1) for i in range(shards - 1)])
-    after = lax.ppermute(behind, AXES, [(i + 1, i) for i in range(shards - 1)])
+    )
+    pairs = [(i, i + 1) for i in range(0, shards, 2)]
+    first_in = lax.ppermute(first_out, AXES, pairs + [(j, i) for i, j in pairs])
+    pairs = [(i, i + 1) for i in range(1, shards - 1, 2)]
+    second_in = lax.ppermute(second_out, AXES, pairs + [(j, i) for i, j in pairs])
     hbm_spec = pl.BlockSpec(memory_space=pltpu.HBM)
     vmem_spec = pl.BlockSpec(memory_space=pltpu.VMEM)
     weights = (w_inner, x_project, dt_project)
@@ -613,25 +625,28 @@
         pltpu.VMEM((2, rows, LANES), f32),
         pltpu.VMEM((2, edge, width), f32),
         *(pltpu.VMEM(w.shape, w.dtype) for w in weights),
-    )
-    u, proj, edge_sums, w_inner, x_project, dt_project = pl.pallas_call(
+        pltpu.HBM((rows, LANES), f32),
+    )
+    u, proj, edge_sums, w_inner, x_project, dt_project, places = pl.pallas_call(
         inner_kernel,
         out_shape=results,
         in_specs=[vmem_spec] * 3 + [hbm_spec] * 3,
-        out_specs=(vmem_spec,) * len(results),
+        out_specs=(vmem_spec,) * (len(results) - 1) + (hbm_spec,),
         scratch_shapes=[
+            pltpu.VMEM((rows, model), bf16),
+            pltpu.VMEM((rows, LANES), f32),
             pltpu.VMEM((rows + 2 * edge, width // 4), f32),
-            pltpu.SemaphoreType.DMA((6,)),
+            pltpu.SemaphoreType.DMA((7,)),
         ],
         compiler_params=limits(4),
         name="inner",
     )(
-        *(in_vmem(operand) for operand in (block_rows, conv_weight, conv_bias)),
+        *(in_vmem(operand) for operand in (plain, conv_weight, conv_bias)),
         *(in_hbm(w) for w in weights),
     )
 
     operands = (
-        proj, edge_sums, before, after, w_inner, conv_weight, x_project, dt_project, dt_bias, rates, u,
+        proj, edge_sums, first_in, second_in, w_inner, conv_weight, x_project, dt_project, dt_bias, rates, u,
     )
     on_chip_results = [
         pltpu.VMEM((2, rows, LANES), f32),

time: 130 us -> 127 us (0.977)
  starting transfers between devices: 28.3 us -> 25.6 us
    ppermute x2, starting transfers between devices: 6.76 us -> 3.87 us  [the longest x1 3.49 us: local(): lax.ppermute(second_out, AXES, pairs + [(j, i) for i, j in pairs])]
where the time goes in v6:
time: 127 us
  Pallas kernels  49.2 us (39%)
  waiting for transfers between devices  29.8 us (23%)
  starting transfers between devices  25.6 us (20%)
  blocking collectives  14.4 us (11%)
  matrix products  5.16 us (4%)
  between operations  1.53 us (1%)
    pallas_call x1, Pallas kernels, local(): pl.pallas_call(outputs_kernel, out_shape=pltpu.HBM((SUB * rows, tile), bf...  16.2 us
    pallas_call x1, Pallas kernels, local(): pl.pallas_call(states_kernel, out_shape=(pltpu.HBM((2, rows, width), bf16...  15.8 us
    all_to_all x1, blocking collectives, local(): lax.all_to_all(entering, AXES, split_axis=0, concat_axis=0, tiled=True)  14.4 us
    all_to_all x1, waiting for transfers between devices, local(): lax.all_to_all(totals.reshape(rows, SUB, tile), AXES, split_axis=0, conca...  11.7 us
    all_to_all x1, waiting for transfers between devices, local(): lax.all_to_all(sent.reshape(rows, SUB, piece), AXES, split_axis=0, concat...  11.7 us
    all_to_all x1, starting transfers between devices, local(): lax.all_to_all(sent.reshape(rows, SUB, piece), AXES, split_axis=0, concat...  11.5 us
    all_to_all x1, waiting for transfers between devices, local(): lax.all_to_all(payload.reshape(shards, 4, tile), AXES, split_axis=0, conc...  6.35 us
    all_to_all x1, starting transfers between devices, local(): lax.all_to_all(payload.reshape(shards, 4, tile), AXES, split_axis=0, conc...  6.25 us
  transfers between devices with their start and end apart: 5, of which 3 were waited for; matrix products, arithmetic and copies ran while one was open for 5% of the time, Pallas kernels for 9%

profile of v6, /device:TPU:1, one launch (start us, length us, event | category | flops | bytes accessed | tf_op | source)
XLA Modules:
  0.0 126.9 jit_solution(14678958133296772808)
XLA Ops:
  0.0 0.0 copy-start.2
  0.0 2.3 %pack.1 = bf16[1024,256]{1,0:T(8,128)(2,1)} custom-call(bf16[128,1536]{1,0:T(8,128)(2,1)} %embed.1, s32[1,128]{1,0:T(1,128)} %bitcast.19), custom_call_target="tpu_custom_call" | custom-call | tf_op jit(solution)/shard_map/pack/pallas_call | solution.py:593
  2.3 11.5 %all-to-all-start = ((bf16[128,8,256]{2,1,0:T(8,128)(2,1)}), bf16[128,8,256]{2,1,0:T(8,128)(2,1)S(1)}, u32[]{:S(2)}, u32[]{:S(2)}) async-start(bf16[128,8,256]{2,1,0:T(8,128)(2,1)} %bitcast.4), calls=%async_computation | async-start | bytes 1048576 | tf_op jit(solution)/shard_map/all_to_all | solution.py:599
  13.9 0.0 copy-done.6
  13.9 0.1 select_reduce_fusion
  14.0 0.1 compare_reduce_fusion
  14.1 0.7 and_reduce_fusion.1
  16.0 0.0 copy-done.4
  16.1 11.7 %all-to-all-done = bf16[128,8,256]{2,1,0:T(8,128)(2,1)S(1)} async-done(((bf16[128,8,256]{2,1,0:T(8,128)(2,1)}), bf16[128,8,256]{2,1,0:T(8,128)(2,1)S(1)}, u32[]{:S(2)}, u32[]{:S(2)}) %all-to-all-start) | async-done | bytes 524320 | tf_op jit(solution)/shard_map/all_to_all | solution.py:599
  27.8 0.6 edges.1
  28.3 0.4 collective-permute-start
  28.7 3.5 %collective-permute-start.1 = (bf16[8,1536]{1,0:T(8,128)(2,1)S(1)}, bf16[8,1536]{1,0:T(8,128)(2,1)S(1)}, u32[]{:S(2)}, u32[]{:S(2)}) collective-permute-start(bf16[8,1536]{1,0:T(8,128)(2,1)S(1)} %get-tuple-element.27), channel_id=1, source_target_pairs={{1,2},{3,4},{5,6},{7,8},{9,10},{11,12},{13,14},{15,16},{17,18},{19... | collective-permute-start | bytes 73736 | tf_op jit(solution)/shard_map/ppermute | solution.py:618
  32.2 0.1 add_convert_fusion.flags
  32.3 0.0 copy-done
  32.3 0.0 copy-done.2
  32.3 5.9 %inner.1 = (bf16[2,128,3072]{2,1,0:T(8,128)(2,1)S(1)}, f32[2,128,128]{2,1,0:T(8,128)S(1)}, f32[2,24,3072]{2,1,0:T(8,128)S(1)}, bf16[1536,3072]{1,0:T(8,128)(2,1)...) custom-call(bf16[128,1792]{1,0:T(8,128)(2,1)S(1)} %get-tuple-element.23.plain, ...), custom_call_target="tpu_custom_call" | custom-call | tf_op jit(solution)/shard_map/inner/pallas_call | solution.py:630
  38.2 0.0 collective-permute-done.first_in
  38.2 0.0 collective-permute-done.1.second_in
  38.3 0.0 copy-done.1
  38.3 15.8 %block_states.1 = (bf16[2,128,3072]{2,1,0:T(8,128)(2,1)}, f32[2,128,128]{2,1,0:T(8,128)}, f32[2,128,3072]{2,1,0:T(8,128)}, bf16[2,8,8,4,384]{4,3,2,1,0:T(4,128)(...) custom-call(s32[3]{0:T(128)S(1)} %add_convert_fusion.flags, ...), custom_call_target="tpu_custom_call", output_to_operand_aliasing={{6}: (11, {})} | custom-call | tf_op jit(solution)/shard_map/block_states/pallas_call | solution.py:659
  54.0 6.3 %all-to-all-start.1 = ((bf16[128,4,384]{2,1,0:T(4,128)(2,1)}), bf16[128,4,384]{2,1,0:T(4,128)(2,1)S(1)}, u32[]{:S(2)}, u32[]{:S(2)}) async-start(bf16[128,4,384]{2,1,0:T(4,128)(2,1)} %bitcast.18), calls=%async_computation.1 | async-start | bytes 786432 | tf_op jit(solution)/shard_map/all_to_all | solution.py:683
  60.4 0.1 dynamic-slice_bitcast_fusion.rates
  60.5 6.1 %entries.1.entry = f32[2,16,8,3072]{3,2,1,0:T(8,128)} custom-call(f32[2,16,8,3072]{3,2,1,0:T(8,128)} %get-tuple-element.33.ends, f32[2,8,3072]{2,1,0:T(8,128)} %get-tuple-element.34.span, f32[2,16,3072]{2,1,0:T(8,128)S(1)} %broadcast_multiply_fusion.rates), custom_call_target="tpu_custom_call" | custom-call | tf_op jit(solution)/shard_map/entries/pallas_call | solution.py:686
  66.6 6.4 %all-to-all-done.1.payload = bf16[128,4,384]{2,1,0:T(4,128)(2,1)S(1)} async-done(((bf16[128,4,384]{2,1,0:T(4,128)(2,1)}), bf16[128,4,384]{2,1,0:T(4,128)(2,1)S(1)}, u32[]{:S(2)}, u32[]{:S(2)}) %all-to-all-start.1) | async-done | bytes 393248 | tf_op jit(solution)/shard_map/all_to_all | solution.py:683
  72.9 1.2 relay.1
  74.1 14.4 %all_to_all.20 = bf16[128,2,384]{2,1,0:T(2,128)(2,1)S(1)} all-to-all(bf16[128,2,384]{2,1,0:T(2,128)(2,1)S(1)} %relay.1), channel_id=1, replica_groups=mesh['seq'=32,'slide'=4] {'seq','slide'}, dimensions={0} | all-to-all | bytes 393216 | tf_op jit(solution)/shard_map/all_to_all | solution.py:708
  88.6 0.0 copy-done.3
  88.6 16.2 %block_outputs.1 = bf16[1024,384]{1,0:T(8,128)(2,1)} custom-call(bf16[2,8,8,2,384]{4,3,2,1,0:T(2,128)(2,1)S(1)} %bitcast.16, f32[2,16,8,3072]{3,2,1,0:T(8,128)} %entries.1.entry, f32[2,128,3072]{2,1,0:T(8,128)} %get-tuple-element.37.dt_in, bf16[2,128,3072]{2,1,0:T(8,128)(2,1)} %get-tuple-element.38.u_in, f32[2,128,128]{2,1,0:T(8,128)} %get-tuple-element.39.proj, ...), custom_call_target="tpu_custom_call" | custom-call | tf_op jit(solution)/shard_map/block_outputs/pallas_call | solution.py:711
  104.8 4.0 %all-to-all-start.3 = ((bf16[128,8,384]{2,1,0:T(8,128)(2,1)}), bf16[128,8,384]{2,1,0:T(8,128)(2,1)S(1)}, u32[]{:S(2)}, u32[]{:S(2)}) async-start(bf16[128,8,384]{2,1,0:T(8,128)(2,1)} %bitcast.17), calls=%async_computation.3 | async-start | bytes 1572864 | tf_op jit(solution)/shard_map/all_to_all | solution.py:741
  108.7 5.2 %divide_multiply_fusion.gate = f32[128,3072]{1,0:T(8,128)S(1)} fusion(bf16[128,1536]{1,0:T(8,128)(2,1)S(1)} %copy-done.5, bf16[1536,3072]{1,0:T(8,128)(2,1)} %param.16), kind=kOutput, calls=%fused_computation | convolution fusion | flops 1209532416 | bytes 11403264 | tf_op jit(solution)/shard_map/dot_general | solution.py:602
  113.9 11.7 %all-to-all-done.3 = bf16[128,8,384]{2,1,0:T(8,128)(2,1)S(1)} async-done(((bf16[128,8,384]{2,1,0:T(8,128)(2,1)}), bf16[128,8,384]{2,1,0:T(8,128)(2,1)S(1)}, u32[]{:S(2)}, u32[]{:S(2)}) %all-to-all-start.3) | async-done | bytes 786464 | tf_op jit(solution)/shard_map/all_to_all | solution.py:741
  125.7 1.2 gated.1
  (12 shorter events, 0.1 us)
Async XLA Ops:
  0.0 13.9 %copy-start.6 = (s32[4]{0:T(128)S(1)}, s32[4]{0:T(128)}, u32[]{:S(2)}) copy-start(s32[4]{0:T(128)} %param.14) | copy-start | bytes 52
  0.0 16.0 %copy-start.4 = (f32[2,16,3072]{2,1,0:T(8,128)S(1)}, f32[2,16,3072]{2,1,0:T(8,128)}, u32[]{:S(2)}) copy-start(f32[2,16,3072]{2,1,0:T(8,128)} %param.22) | copy-start | bytes 1179652
  0.0 32.3 %copy-start = (f32[2,4,3072]{2,1,0:T(4,128)S(1)}, f32[2,4,3072]{2,1,0:T(4,128)}, u32[]{:S(2)}) copy-start(f32[2,4,3072]{2,1,0:T(4,128)} %conv_weight.3) | copy-start | bytes 294916
  0.0 32.3 %copy-start.2 = (f32[2,3072]{1,0:T(2,128)S(1)}, f32[2,3072]{1,0:T(2,128)}, u32[]{:S(2)}) copy-start(f32[2,3072]{1,0:T(2,128)} %conv_bias.1) | copy-start | bytes 73732
  2.3 25.5 %all-to-all-start = ((bf16[128,8,256]{2,1,0:T(8,128)(2,1)}), bf16[128,8,256]{2,1,0:T(8,128)(2,1)S(1)}, u32[]{:S(2)}, u32[]{:S(2)}) async-start(bf16[128,8,256]{2,1,0:T(8,128)(2,1)} %bitcast.4), calls=%async_computation | async-start | bytes 1048576 | tf_op jit(solution)/shard_map/all_to_all | solution.py:599
  28.3 9.9 %collective-permute-start = (bf16[8,1536]{1,0:T(8,128)(2,1)S(1)}, bf16[8,1536]{1,0:T(8,128)(2,1)S(1)}, u32[]{:S(2)}, u32[]{:S(2)}) collective-permute-start(bf16[8,1536]{1,0:T(8,128)(2,1)S(1)} %get-tuple-element.26), channel_id=1, source_target_pairs={{0,1},{2,3},{4,5},{6,7},{8,9},{10,11},{12,13},{14,15},{16,17},{18,... | collective-permute-start | bytes 73736 | tf_op jit(solution)/shard_map/ppermute | solution.py:616
  28.7 9.5 %collective-permute-start.1 = (bf16[8,1536]{1,0:T(8,128)(2,1)S(1)}, bf16[8,1536]{1,0:T(8,128)(2,1)S(1)}, u32[]{:S(2)}, u32[]{:S(2)}) collective-permute-start(bf16[8,1536]{1,0:T(8,128)(2,1)S(1)} %get-tuple-element.27), channel_id=1, source_target_pairs={{1,2},{3,4},{5,6},{7,8},{9,10},{11,12},{13,14},{15,16},{17,18},{19... | collective-permute-start | bytes 73736 | tf_op jit(solution)/shard_map/ppermute | solution.py:618
  32.3 6.0 %copy-start.1 = (f32[2,3072]{1,0:T(2,128)S(1)}, f32[2,3072]{1,0:T(2,128)}, u32[]{:S(2)}) copy-start(f32[2,3072]{1,0:T(2,128)} %dt_bias.1) | copy-start | bytes 73732
  54.0 18.9 %all-to-all-start.1 = ((bf16[128,4,384]{2,1,0:T(4,128)(2,1)}), bf16[128,4,384]{2,1,0:T(4,128)(2,1)S(1)}, u32[]{:S(2)}, u32[]{:S(2)}) async-start(bf16[128,4,384]{2,1,0:T(4,128)(2,1)} %bitcast.18), calls=%async_computation.1 | async-start | bytes 786432 | tf_op jit(solution)/shard_map/all_to_all | solution.py:683
  60.5 28.1 %copy-start.3 = (f32[2,3072]{1,0:T(2,128)S(1)}, f32[2,3072]{1,0:T(2,128)}, u32[]{:S(2)}) copy-start(f32[2,3072]{1,0:T(2,128)} %skip_gain.1) | copy-start | bytes 73732
  104.8 4.0 %copy-start.5 = (bf16[128,1536]{1,0:T(8,128)(2,1)S(1)}, bf16[128,1536]{1,0:T(8,128)(2,1)}, u32[]{:S(2)}) copy-start(bf16[128,1536]{1,0:T(8,128)(2,1)} %embed.1) | copy-start | bytes 1179652
  104.8 20.9 %all-to-all-start.3 = ((bf16[128,8,384]{2,1,0:T(8,128)(2,1)}), bf16[128,8,384]{2,1,0:T(8,128)(2,1)S(1)}, u32[]{:S(2)}, u32[]{:S(2)}) async-start(bf16[128,8,384]{2,1,0:T(8,128)(2,1)} %bitcast.17), calls=%async_computation.3 | async-start | bytes 1572864 | tf_op jit(solution)/shard_map/all_to_all | solution.py:741

commit v7 on v6

--- a/solution.py
+++ b/solution.py
@@ -679,7 +679,7 @@
         name="block_states",
     )(flags, *(in_vmem(operand) for operand in operands))
 
-    part = 4 * LANES
+    part = 6 * LANES
     shared = lax.all_to_all(
         payload.reshape(shards, 4, tile), AXES, split_axis=0, concat_axis=0, tiled=True
     )
@@ -693,7 +693,7 @@
             pl.BlockSpec((2, states, part), lambda i: (0, 0, i)),
         ],
         out_specs=pl.BlockSpec((2, states, SUB, part), lambda i: (0, 0, 0, i)),
-        compiler_params=limits(3),
+        compiler_params=limits(6),
         name="entries",
     )(in_hbm(ends), in_hbm(span), rates)
     shared, entry = lax.optimization_barrier((shared, entry))
@@ -728,7 +728,7 @@
             pltpu.VMEM((2, states, rows, LANES), f32),
             pltpu.VMEM((rows, width), bf16),
         ],
-        compiler_params=limits(12),
+        compiler_params=limits(14),
         name="block_outputs",
     )(
         in_vmem(entering),

time: 127 us -> 127 us (level)
  Pallas kernels: 49.2 us -> 47.8 us
where the time goes in v7:
time: 127 us; the launch traced here: 126 us
  Pallas kernels  47.8 us (38%)
  waiting for transfers between devices  30.7 us (24%)
  starting transfers between devices  25.6 us (20%)
  blocking collectives  14.4 us (11%)
  matrix products  5.16 us (4%)
  between operations  1.53 us (1%)
    pallas_call x1, Pallas kernels, local(): pl.pallas_call(states_kernel, out_shape=(pltpu.HBM((2, rows, width), bf16...  15.8 us
    pallas_call x1, Pallas kernels, local(): pl.pallas_call(outputs_kernel, out_shape=pltpu.HBM((SUB * rows, tile), bf...  15.7 us
    all_to_all x1, blocking collectives, local(): lax.all_to_all(entering, AXES, split_axis=0, concat_axis=0, tiled=True)  14.4 us
    all_to_all x1, waiting for transfers between devices, local(): lax.all_to_all(totals.reshape(rows, SUB, tile), AXES, split_axis=0, conca...  11.7 us
    all_to_all x1, waiting for transfers between devices, local(): lax.all_to_all(sent.reshape(rows, SUB, piece), AXES, split_axis=0, concat...  11.7 us
    all_to_all x1, starting transfers between devices, local(): lax.all_to_all(sent.reshape(rows, SUB, piece), AXES, split_axis=0, concat...  11.5 us
    all_to_all x1, waiting for transfers between devices, local(): lax.all_to_all(payload.reshape(shards, 4, tile), AXES, split_axis=0, conc...  7.28 us
    all_to_all x1, starting transfers between devices, local(): lax.all_to_all(payload.reshape(shards, 4, tile), AXES, split_axis=0, conc...  6.25 us
  transfers between devices with their start and end apart: 5, of which 3 were waited for; matrix products, arithmetic and copies ran while one was open for 5% of the time, Pallas kernels for 9%

profile of v7, /device:TPU:1, one launch (start us, length us, event | category | flops | bytes accessed | tf_op | source)
XLA Modules:
  0.0 126.4 jit_solution(12198654053344034740)
XLA Ops:
  0.0 0.0 copy-start.2
  0.0 2.3 %pack.1 = bf16[1024,256]{1,0:T(8,128)(2,1)} custom-call(bf16[128,1536]{1,0:T(8,128)(2,1)} %embed.1, s32[1,128]{1,0:T(1,128)} %bitcast.19), custom_call_target="tpu_custom_call" | custom-call | tf_op jit(solution)/shard_map/pack/pallas_call | solution.py:593
  2.3 11.5 %all-to-all-start = ((bf16[128,8,256]{2,1,0:T(8,128)(2,1)}), bf16[128,8,256]{2,1,0:T(8,128)(2,1)S(1)}, u32[]{:S(2)}, u32[]{:S(2)}) async-start(bf16[128,8,256]{2,1,0:T(8,128)(2,1)} %bitcast.4), calls=%async_computation | async-start | bytes 1048576 | tf_op jit(solution)/shard_map/all_to_all | solution.py:599
  13.9 0.0 copy-done.6
  13.9 0.1 select_reduce_fusion
  14.0 0.1 compare_reduce_fusion
  14.1 0.7 and_reduce_fusion.1
  16.0 0.0 copy-done.4
  16.1 11.7 %all-to-all-done = bf16[128,8,256]{2,1,0:T(8,128)(2,1)S(1)} async-done(((bf16[128,8,256]{2,1,0:T(8,128)(2,1)}), bf16[128,8,256]{2,1,0:T(8,128)(2,1)S(1)}, u32[]{:S(2)}, u32[]{:S(2)}) %all-to-all-start) | async-done | bytes 524320 | tf_op jit(solution)/shard_map/all_to_all | solution.py:599
  27.8 0.6 edges.1
  28.3 0.4 collective-permute-start
  28.7 3.5 %collective-permute-start.1 = (bf16[8,1536]{1,0:T(8,128)(2,1)S(1)}, bf16[8,1536]{1,0:T(8,128)(2,1)S(1)}, u32[]{:S(2)}, u32[]{:S(2)}) collective-permute-start(bf16[8,1536]{1,0:T(8,128)(2,1)S(1)} %get-tuple-element.27), channel_id=1, source_target_pairs={{1,2},{3,4},{5,6},{7,8},{9,10},{11,12},{13,14},{15,16},{17,18},{19... | collective-permute-start | bytes 73736 | tf_op jit(solution)/shard_map/ppermute | solution.py:618
  32.2 0.1 add_convert_fusion.flags
  32.3 0.0 copy-done
  32.3 0.0 copy-done.2
  32.3 5.9 %inner.1 = (bf16[2,128,3072]{2,1,0:T(8,128)(2,1)S(1)}, f32[2,128,128]{2,1,0:T(8,128)S(1)}, f32[2,24,3072]{2,1,0:T(8,128)S(1)}, bf16[1536,3072]{1,0:T(8,128)(2,1)...) custom-call(bf16[128,1792]{1,0:T(8,128)(2,1)S(1)} %get-tuple-element.23.plain, ...), custom_call_target="tpu_custom_call" | custom-call | tf_op jit(solution)/shard_map/inner/pallas_call | solution.py:630
  38.2 0.0 collective-permute-done.first_in
  38.2 0.0 collective-permute-done.1.second_in
  38.3 0.0 copy-done.1
  38.3 15.8 %block_states.1 = (bf16[2,128,3072]{2,1,0:T(8,128)(2,1)}, f32[2,128,128]{2,1,0:T(8,128)}, f32[2,128,3072]{2,1,0:T(8,128)}, bf16[2,8,8,4,384]{4,3,2,1,0:T(4,128)(...) custom-call(s32[3]{0:T(128)S(1)} %add_convert_fusion.flags, ...), custom_call_target="tpu_custom_call", output_to_operand_aliasing={{6}: (11, {})} | custom-call | tf_op jit(solution)/shard_map/block_states/pallas_call | solution.py:659
  54.0 6.3 %all-to-all-start.1 = ((bf16[128,4,384]{2,1,0:T(4,128)(2,1)}), bf16[128,4,384]{2,1,0:T(4,128)(2,1)S(1)}, u32[]{:S(2)}, u32[]{:S(2)}) async-start(bf16[128,4,384]{2,1,0:T(4,128)(2,1)} %bitcast.18), calls=%async_computation.1 | async-start | bytes 786432 | tf_op jit(solution)/shard_map/all_to_all | solution.py:683
  60.4 0.1 dynamic-slice_bitcast_fusion.rates
  60.5 5.2 %entries.1.entry = f32[2,16,8,3072]{3,2,1,0:T(8,128)} custom-call(f32[2,16,8,3072]{3,2,1,0:T(8,128)} %get-tuple-element.33.ends, f32[2,8,3072]{2,1,0:T(8,128)} %get-tuple-element.34.span, f32[2,16,3072]{2,1,0:T(8,128)S(1)} %broadcast_multiply_fusion.rates), custom_call_target="tpu_custom_call" | custom-call | tf_op jit(solution)/shard_map/entries/pallas_call | solution.py:686
  65.7 7.3 %all-to-all-done.1.payload = bf16[128,4,384]{2,1,0:T(4,128)(2,1)S(1)} async-done(((bf16[128,4,384]{2,1,0:T(4,128)(2,1)}), bf16[128,4,384]{2,1,0:T(4,128)(2,1)S(1)}, u32[]{:S(2)}, u32[]{:S(2)}) %all-to-all-start.1) | async-done | bytes 393248 | tf_op jit(solution)/shard_map/all_to_all | solution.py:683
  72.9 1.2 relay.1
  74.1 14.4 %all_to_all.20 = bf16[128,2,384]{2,1,0:T(2,128)(2,1)S(1)} all-to-all(bf16[128,2,384]{2,1,0:T(2,128)(2,1)S(1)} %relay.1), channel_id=1, replica_groups=mesh['seq'=32,'slide'=4] {'seq','slide'}, dimensions={0} | all-to-all | bytes 393216 | tf_op jit(solution)/shard_map/all_to_all | solution.py:708
  88.6 0.0 copy-done.3
  88.6 15.7 %block_outputs.1 = bf16[1024,384]{1,0:T(8,128)(2,1)} custom-call(bf16[2,8,8,2,384]{4,3,2,1,0:T(2,128)(2,1)S(1)} %bitcast.16, f32[2,16,8,3072]{3,2,1,0:T(8,128)} %entries.1.entry, f32[2,128,3072]{2,1,0:T(8,128)} %get-tuple-element.37.dt_in, bf16[2,128,3072]{2,1,0:T(8,128)(2,1)} %get-tuple-element.38.u_in, f32[2,128,128]{2,1,0:T(8,128)} %get-tuple-element.39.proj, ...), custom_call_target="tpu_custom_call" | custom-call | tf_op jit(solution)/shard_map/block_outputs/pallas_call | solution.py:711
  104.3 4.0 %all-to-all-start.3 = ((bf16[128,8,384]{2,1,0:T(8,128)(2,1)}), bf16[128,8,384]{2,1,0:T(8,128)(2,1)S(1)}, u32[]{:S(2)}, u32[]{:S(2)}) async-start(bf16[128,8,384]{2,1,0:T(8,128)(2,1)} %bitcast.17), calls=%async_computation.3 | async-start | bytes 1572864 | tf_op jit(solution)/shard_map/all_to_all | solution.py:741
  108.3 5.2 %divide_multiply_fusion.gate = f32[128,3072]{1,0:T(8,128)S(1)} fusion(bf16[128,1536]{1,0:T(8,128)(2,1)S(1)} %copy-done.5, bf16[1536,3072]{1,0:T(8,128)(2,1)} %param.16), kind=kOutput, calls=%fused_computation | convolution fusion | flops 1209532416 | bytes 11403264 | tf_op jit(solution)/shard_map/dot_general | solution.py:602
  113.4 11.7 %all-to-all-done.3 = bf16[128,8,384]{2,1,0:T(8,128)(2,1)S(1)} async-done(((bf16[128,8,384]{2,1,0:T(8,128)(2,1)}), bf16[128,8,384]{2,1,0:T(8,128)(2,1)S(1)}, u32[]{:S(2)}, u32[]{:S(2)}) %all-to-all-start.3) | async-done | bytes 786464 | tf_op jit(solution)/shard_map/all_to_all | solution.py:741
  125.2 1.2 gated.1
  (12 shorter events, 0.1 us)
Async XLA Ops:
  0.0 13.9 %copy-start.6 = (s32[4]{0:T(128)S(1)}, s32[4]{0:T(128)}, u32[]{:S(2)}) copy-start(s32[4]{0:T(128)} %param.14) | copy-start | bytes 52
  0.0 16.0 %copy-start.4 = (f32[2,16,3072]{2,1,0:T(8,128)S(1)}, f32[2,16,3072]{2,1,0:T(8,128)}, u32[]{:S(2)}) copy-start(f32[2,16,3072]{2,1,0:T(8,128)} %param.22) | copy-start | bytes 1179652
  0.0 32.3 %copy-start = (f32[2,4,3072]{2,1,0:T(4,128)S(1)}, f32[2,4,3072]{2,1,0:T(4,128)}, u32[]{:S(2)}) copy-start(f32[2,4,3072]{2,1,0:T(4,128)} %conv_weight.3) | copy-start | bytes 294916
  0.0 32.3 %copy-start.2 = (f32[2,3072]{1,0:T(2,128)S(1)}, f32[2,3072]{1,0:T(2,128)}, u32[]{:S(2)}) copy-start(f32[2,3072]{1,0:T(2,128)} %conv_bias.1) | copy-start | bytes 73732
  2.3 25.5 %all-to-all-start = ((bf16[128,8,256]{2,1,0:T(8,128)(2,1)}), bf16[128,8,256]{2,1,0:T(8,128)(2,1)S(1)}, u32[]{:S(2)}, u32[]{:S(2)}) async-start(bf16[128,8,256]{2,1,0:T(8,128)(2,1)} %bitcast.4), calls=%async_computation | async-start | bytes 1048576 | tf_op jit(solution)/shard_map/all_to_all | solution.py:599
  28.3 9.9 %collective-permute-start = (bf16[8,1536]{1,0:T(8,128)(2,1)S(1)}, bf16[8,1536]{1,0:T(8,128)(2,1)S(1)}, u32[]{:S(2)}, u32[]{:S(2)}) collective-permute-start(bf16[8,1536]{1,0:T(8,128)(2,1)S(1)} %get-tuple-element.26), channel_id=1, source_target_pairs={{0,1},{2,3},{4,5},{6,7},{8,9},{10,11},{12,13},{14,15},{16,17},{18,... | collective-permute-start | bytes 73736 | tf_op jit(solution)/shard_map/ppermute | solution.py:616
  28.7 9.5 %collective-permute-start.1 = (bf16[8,1536]{1,0:T(8,128)(2,1)S(1)}, bf16[8,1536]{1,0:T(8,128)(2,1)S(1)}, u32[]{:S(2)}, u32[]{:S(2)}) collective-permute-start(bf16[8,1536]{1,0:T(8,128)(2,1)S(1)} %get-tuple-element.27), channel_id=1, source_target_pairs={{1,2},{3,4},{5,6},{7,8},{9,10},{11,12},{13,14},{15,16},{17,18},{19... | collective-permute-start | bytes 73736 | tf_op jit(solution)/shard_map/ppermute | solution.py:618
  32.3 6.0 %copy-start.1 = (f32[2,3072]{1,0:T(2,128)S(1)}, f32[2,3072]{1,0:T(2,128)}, u32[]{:S(2)}) copy-start(f32[2,3072]{1,0:T(2,128)} %dt_bias.1) | copy-start | bytes 73732
  54.0 18.9 %all-to-all-start.1 = ((bf16[128,4,384]{2,1,0:T(4,128)(2,1)}), bf16[128,4,384]{2,1,0:T(4,128)(2,1)S(1)}, u32[]{:S(2)}, u32[]{:S(2)}) async-start(bf16[128,4,384]{2,1,0:T(4,128)(2,1)} %bitcast.18), calls=%async_computation.1 | async-start | bytes 786432 | tf_op jit(solution)/shard_map/all_to_all | solution.py:683
  60.5 28.1 %copy-start.3 = (f32[2,3072]{1,0:T(2,128)S(1)}, f32[2,3072]{1,0:T(2,128)}, u32[]{:S(2)}) copy-start(f32[2,3072]{1,0:T(2,128)} %skip_gain.1) | copy-start | bytes 73732
  104.3 4.0 %copy-start.5 = (bf16[128,1536]{1,0:T(8,128)(2,1)S(1)}, bf16[128,1536]{1,0:T(8,128)(2,1)}, u32[]{:S(2)}) copy-start(bf16[128,1536]{1,0:T(8,128)(2,1)} %embed.1) | copy-start | bytes 1179652
  104.3 20.9 %all-to-all-start.3 = ((bf16[128,8,384]{2,1,0:T(8,128)(2,1)}), bf16[128,8,384]{2,1,0:T(8,128)(2,1)S(1)}, u32[]{:S(2)}, u32[]{:S(2)}) async-start(bf16[128,8,384]{2,1,0:T(8,128)(2,1)} %bitcast.17), calls=%async_computation.3 | async-start | bytes 1572864 | tf_op jit(solution)/shard_map/all_to_all | solution.py:741
